TPU v7x, 32 devices: a whole 2x2x4 slice. The times are simulated.
32 devices in a mesh: ctx: 8 (over z, y), wa: 4 (over x, core).
Axes of the slice: x: 2, y: 2, z: 4, core: 2. Of those that a mesh axis runs over, the one named last changes fastest.
Arguments:
- tokens: bfloat16 [4, 1024, 896], P('wa', 'ctx'), may hold values from -6 to 6
- neighbours: bfloat16 [4, 16, 256, 896], P('wa', 'ctx'), may hold values from -6 to 6
- teacher: bfloat16 [4, 1024, 896], P('wa', 'ctx'), may hold values from -6 to 6
- valid_mask: int32 [4, 1024], P('wa', 'ctx'), may hold values from 0 to 1, as said below
- block_order: int32 [16], replicated, may hold values from 0 to 15, as said below
- query_weight: bfloat16 [896, 1024], P('wa'), may hold values from -0.1875 to 0.1875
- key_weight: bfloat16 [896, 1024], P('wa'), may hold values from -0.1875 to 0.1875
- value_weight: bfloat16 [896, 1024], P('wa'), may hold values from -0.1875 to 0.1875
- output_weight: bfloat16 [1024, 896], P('wa'), may hold values from -3 to 3
- relative_weight: bfloat16 [896, 1024], P('wa'), may hold values from -0.1875 to 0.1875
- content_bias: bfloat16 [1024], P('wa'), may hold values from -3 to 3
- position_bias: bfloat16 [1024], P('wa'), may hold values from -3 to 3
- cross_query_weight: bfloat16 [896, 1024], P('wa'), may hold values from -0.1875 to 0.1875
- cross_key_weight: bfloat16 [896, 1024], P('wa'), may hold values from -0.1875 to 0.1875
- cross_value_weight: bfloat16 [896, 1024], P('wa'), may hold values from -0.1875 to 0.1875
- cross_output_weight: bfloat16 [1024, 896], P('wa'), may hold values from -1.5 to 1.5
- up_weight: bfloat16 [896, 3584], P('wa'), may hold values from -0.1875 to 0.1875
- down_weight: bfloat16 [3584, 896], P('wa'), may hold values from -0.09375 to 0.09375
- attention_gain: bfloat16 [896], P('wa'), may hold values from 0.5 to 1.5
- cross_gain: bfloat16 [896], P('wa'), may hold values from 0.5 to 1.5
- feedforward_gain: bfloat16 [896], P('wa'), may hold values from 0.5 to 1.5
Outputs:
- layer_out: float32 [4, 1024, 896], P('wa', 'ctx')
- loss: float32 [], replicated
- tokens_grad: float32 [4, 1024, 896], P('wa', 'ctx')
- neighbours_grad: float32 [4, 16, 256, 896], P('wa', 'ctx')
- query_weight_grad: float32 [896, 1024], P('wa')
- key_weight_grad: float32 [896, 1024], P('wa')
- value_weight_grad: float32 [896, 1024], P('wa')
- output_weight_grad: float32 [1024, 896], P('wa')
- relative_weight_grad: float32 [896, 1024], P('wa')
- content_bias_grad: float32 [1024], P('wa')
- position_bias_grad: float32 [1024], P('wa')
- cross_query_weight_grad: float32 [896, 1024], P('wa')
- cross_key_weight_grad: float32 [896, 1024], P('wa')
- cross_value_weight_grad: float32 [896, 1024], P('wa')
- cross_output_weight_grad: float32 [1024, 896], P('wa')
- up_weight_grad: float32 [896, 3584], P('wa')
- down_weight_grad: float32 [3584, 896], P('wa')
- attention_gain_grad: float32 [896], P('wa')
- cross_gain_grad: float32 [896], P('wa')
- feedforward_gain_grad: float32 [896], P('wa')
Inputs may be any that keep to these rules, and one draw needn't show every extreme that they name: `block_order`: a permutation of 0 to 15 in which entries 2 k and 2 k + 1 are p and 15 - p for some p. `valid_mask`: each entry 0 or 1; the entry of every stored position t with t % 16 == 15 is 1.
All inputs are finite; a program needn't handle non-finite values.
Results may differ from a plain program's by a relative error of at most 0.029.
Values may be sent and summed in bfloat16 or wider, within the bound.
A program may use at most 512 MiB of HBM per device.

v0:
```python
import jax
import jax.numpy as jnp
from jax import lax
from jax.sharding import PartitionSpec as P

HEADS = 16
HEAD_DIM = 64
GROUP = 64
NK = 256


eps_norm = 1e-06
neg_big = -1e30
highest = lax.Precision.HIGHEST


def rms_scale(hidden, gain):
    return hidden * lax.rsqrt(jnp.mean(hidden * hidden, axis=-1, keepdims=True) + eps_norm) * gain


def gelu_tanh(value):
    return jax.nn.gelu(value, approximate=True)


def norm_back(hidden, gain, grad):
    _, pull = jax.vjp(rms_scale, hidden, gain)
    return pull(grad)


def sinusoid(distance, width):
    half = width // 2
    freq = jnp.exp(-jnp.log(10000.0) * jnp.arange(half, dtype=jnp.float32) * 2.0 / width)
    angle = distance[:, None] * freq[None, :]
    return jnp.concatenate([jnp.sin(angle), jnp.cos(angle)], axis=1)


def project(left, right):
    return jnp.einsum("...i,ij->...j", left, right, preferred_element_type=jnp.float32)


def project_back(grad, right):
    return jnp.einsum("...j,ij->...i", grad, right, preferred_element_type=jnp.float32)


def outer_sum(left, grad):
    flat_left = left.reshape(-1, left.shape[-1])
    flat_grad = grad.reshape(-1, grad.shape[-1])
    return jnp.einsum("ni,nj->ij", flat_left, flat_grad, preferred_element_type=jnp.float32)


def outer_exact(left, grad):
    return jnp.einsum("ni,nj->ij", left.astype(jnp.float32), grad, precision=highest)


def skew(wide, count):
    lead = wide.shape[:-2]
    rows, span = wide.shape[-2:]
    edge = [(0, 0)] * len(lead)
    padded = jnp.pad(wide, edge + [(0, 0), (0, 1)])
    flat = padded.reshape(lead + (rows * (span + 1),))
    flat = lax.slice_in_dim(flat, rows - 1, rows - 1 + rows * span, axis=len(lead))
    return flat.reshape(lead + (rows, span))[..., :count]


def unskew(grad, span):
    lead = grad.shape[:-2]
    rows, count = grad.shape[-2:]
    edge = [(0, 0)] * len(lead)
    wide = jnp.pad(grad, edge + [(0, 0), (0, span - count)])
    flat = jnp.pad(wide.reshape(lead + (rows * span,)), edge + [(rows - 1, 1)])
    return flat.reshape(lead + (rows, span + 1))[..., :span]


def tile_scores(content_rows, position_rows, key_rows, table, row_start, key_start, seq_len):
    rows = content_rows.shape[0]
    count = key_rows.shape[0]
    scale = content_rows.shape[-1] ** (-0.5)
    offset = seq_len - rows - row_start + key_start
    relative = lax.dynamic_slice_in_dim(table, offset, rows + count, 0)
    content = jnp.einsum("qhe,khe->hqk", content_rows, key_rows, preferred_element_type=jnp.float32)
    wide = jnp.einsum("qhe,whe->hqw", position_rows, relative, preferred_element_type=jnp.float32)
    scores = (content + skew(wide, count)) * scale
    causal = (row_start + jnp.arange(rows))[:, None] >= (key_start + jnp.arange(count))[None, :]
    return (scores, causal[None], relative)


def tile_forward(
    content_rows, position_rows, row_start, key_rows, value_rows, table, key_start, seq_len, state
):
    top, total, accum = state
    scores, causal, _ = tile_scores(
        content_rows, position_rows, key_rows, table, row_start, key_start, seq_len
    )
    scores = jnp.where(causal, scores, neg_big)
    new_top = jnp.maximum(top, jnp.max(scores, axis=-1))
    raised = jnp.where(causal, jnp.exp(scores - new_top[..., None]), 0.0)
    fade = jnp.exp(top - new_top)
    total = total * fade + jnp.sum(raised, axis=-1)
    accum = accum * fade[..., None] + jnp.einsum(
        "hqk,khe->hqe", raised.astype(jnp.bfloat16), value_rows, preferred_element_type=jnp.float32
    )
    return (new_top, total, accum)


def tile_backward(
    content_rows,
    position_rows,
    row_start,
    key_rows,
    value_rows,
    grad_rows,
    log_rows,
    delta_rows,
    table,
    key_start,
    seq_len,
):
    scores, causal, relative = tile_scores(
        content_rows, position_rows, key_rows, table, row_start, key_start, seq_len
    )
    scale = content_rows.shape[-1] ** (-0.5)
    shares = jnp.where(causal, jnp.exp(scores - log_rows[..., None]), 0.0)
    share_grad = jnp.einsum(
        "qhe,khe->hqk", grad_rows, value_rows, preferred_element_type=jnp.float32
    )
    score_grad = (shares * (share_grad - delta_rows[..., None])).astype(jnp.bfloat16)
    content_grad = (
        jnp.einsum("hqk,khe->qhe", score_grad, key_rows, preferred_element_type=jnp.float32) * scale
    )
    wide_grad = unskew(score_grad, relative.shape[0])
    position_grad = (
        jnp.einsum("hqw,whe->qhe", wide_grad, relative, preferred_element_type=jnp.float32) * scale
    )
    table_part = (
        jnp.einsum("hqw,qhe->whe", wide_grad, position_rows, preferred_element_type=jnp.float32)
        * scale
    )
    key_grad = (
        jnp.einsum("hqk,qhe->khe", score_grad, content_rows, preferred_element_type=jnp.float32)
        * scale
    )
    value_grad = jnp.einsum(
        "hqk,qhe->khe", shares.astype(jnp.bfloat16), grad_rows, preferred_element_type=jnp.float32
    )
    return (content_grad, position_grad, table_part, key_grad, value_grad)


def nest_tiles(tile_fn):
    inner = jax.vmap(tile_fn, in_axes=(0, 0, 0, None, None, 0))
    return jax.vmap(inner, in_axes=(0, 0, None, 0, 0, 0))


def to_global(stored, inverse, block):
    seqs_dev, seq_len = stored.shape[:2]
    blocks = stored.reshape((seqs_dev, seq_len // block, block) + stored.shape[2:])
    return jnp.take(blocks, inverse, axis=1).reshape(stored.shape)


def local(
    tokens,
    neighbours,
    teacher,
    valid_mask,
    block_order,
    query_weight,
    key_weight,
    value_weight,
    output_weight,
    relative_weight,
    content_bias,
    position_bias,
    cross_query_weight,
    cross_key_weight,
    cross_value_weight,
    cross_output_weight,
    up_weight,
    down_weight,
    attention_gain,
    cross_gain,
    feedforward_gain,
):
    (
        query_full,
        key_full,
        value_full,
        output_full,
        relative_full,
        content_full,
        position_full,
        cross_query_full,
        cross_key_full,
        cross_value_full,
        cross_output_full,
        up_full,
        down_full,
        gain_one,
        gain_two,
        gain_three,
    ) = (
        lax.all_gather(query_weight, "wa", axis=0, tiled=True),
        lax.all_gather(key_weight, "wa", axis=0, tiled=True),
        lax.all_gather(value_weight, "wa", axis=0, tiled=True),
        lax.all_gather(output_weight, "wa", axis=0, tiled=True),
        lax.all_gather(relative_weight, "wa", axis=0, tiled=True),
        lax.all_gather(content_bias, "wa", axis=0, tiled=True),
        lax.all_gather(position_bias, "wa", axis=0, tiled=True),
        lax.all_gather(cross_query_weight, "wa", axis=0, tiled=True),
        lax.all_gather(cross_key_weight, "wa", axis=0, tiled=True),
        lax.all_gather(cross_value_weight, "wa", axis=0, tiled=True),
        lax.all_gather(cross_output_weight, "wa", axis=0, tiled=True),
        lax.all_gather(up_weight, "wa", axis=0, tiled=True),
        lax.all_gather(down_weight, "wa", axis=0, tiled=True),
        lax.all_gather(attention_gain, "wa", axis=0, tiled=True),
        lax.all_gather(cross_gain, "wa", axis=0, tiled=True),
        lax.all_gather(feedforward_gain, "wa", axis=0, tiled=True),
    )
    gain_one = gain_one.astype(jnp.float32)
    gain_two = gain_two.astype(jnp.float32)
    gain_three = gain_three.astype(jnp.float32)
    seqs_dev, tok_dev, width = tokens.shape
    attn_width = HEADS * HEAD_DIM
    ctx_count = lax.axis_size("ctx")
    seq_len = tok_dev * ctx_count
    block = tok_dev // 2
    key_len = min(512, seq_len)
    key_steps = seq_len // key_len
    table_rows = seq_len + key_len + block
    slots = jnp.arange(2 * ctx_count)
    inverse = jnp.sum(jnp.where(block_order[None, :] == slots[:, None], slots[None, :], 0), axis=1)
    row_starts = lax.dynamic_slice_in_dim(block_order, 2 * lax.axis_index("ctx"), 2, 0) * block
    tile_lead = (seqs_dev, 2, block, HEADS, HEAD_DIM)
    share = seq_len // lax.axis_size(("ctx", "wa"))
    first = lax.axis_index(("ctx", "wa")) * share
    own_sinusoid = sinusoid(
        (seq_len - 1 - first - jnp.arange(share)).astype(jnp.float32), width
    ).astype(jnp.bfloat16)
    all_distance = (seq_len - 1 - jnp.arange(seq_len)).astype(jnp.float32)
    relative = project(sinusoid(all_distance, width).astype(jnp.bfloat16), relative_full).astype(
        jnp.bfloat16
    )
    table = jnp.concatenate(
        [relative, jnp.zeros((key_len + block, attn_width), jnp.bfloat16)], axis=0
    )
    table = table.reshape(table_rows, HEADS, HEAD_DIM)
    hidden_in = tokens.astype(jnp.float32)
    normed_a = rms_scale(hidden_in, gain_one).astype(jnp.bfloat16)
    query = project(normed_a, query_full)
    content_flat = (query + content_full.astype(jnp.float32)).astype(jnp.bfloat16)
    position_flat = (query + position_full.astype(jnp.float32)).astype(jnp.bfloat16)
    key_local = project(normed_a, key_full).astype(jnp.bfloat16)
    value_local = project(normed_a, value_full).astype(jnp.bfloat16)
    key_all, value_all = (
        lax.all_gather(key_local, "ctx", axis=1, tiled=True),
        lax.all_gather(value_local, "ctx", axis=1, tiled=True),
    )
    key_glob = to_global(key_all, inverse, block).reshape(seqs_dev, seq_len, HEADS, HEAD_DIM)
    value_glob = to_global(value_all, inverse, block).reshape(seqs_dev, seq_len, HEADS, HEAD_DIM)
    content_tiles = content_flat.reshape(tile_lead)
    position_tiles = position_flat.reshape(tile_lead)

    def forward_step(state, index):
        key_start = index * key_len
        key_rows = lax.dynamic_slice_in_dim(key_glob, key_start, key_len, 1)
        value_rows = lax.dynamic_slice_in_dim(value_glob, key_start, key_len, 1)

        def forward_tile(content_rows, position_rows, row_start, keys_seq, values_seq, tile_state):
            return tile_forward(
                content_rows,
                position_rows,
                row_start,
                keys_seq,
                values_seq,
                table,
                key_start,
                seq_len,
                tile_state,
            )

        return (
            nest_tiles(forward_tile)(
                content_tiles, position_tiles, row_starts, key_rows, value_rows, state
            ),
            None,
        )

    state_shape = (seqs_dev, 2, HEADS, block)
    start_state = (
        jnp.full(state_shape, neg_big, jnp.float32),
        jnp.zeros(state_shape, jnp.float32),
        jnp.zeros(state_shape + (HEAD_DIM,), jnp.float32),
    )
    (top, total, accum), _ = lax.scan(forward_step, start_state, jnp.arange(key_steps))
    log_total = top + jnp.log(total)
    attended_tiles = accum / total[..., None]
    attended_low = (
        jnp.transpose(attended_tiles, (0, 1, 3, 2, 4))
        .reshape(seqs_dev, tok_dev, attn_width)
        .astype(jnp.bfloat16)
    )
    hidden_one = hidden_in + project(attended_low, output_full)
    groups = tok_dev // GROUP
    scale = HEAD_DIM ** (-0.5)
    normed_b = rms_scale(hidden_one, gain_two).astype(jnp.bfloat16)
    cross_q = (
        project(normed_b, cross_query_full)
        .astype(jnp.bfloat16)
        .reshape(seqs_dev, groups, GROUP, HEADS, HEAD_DIM)
    )
    cross_k = (
        project(neighbours, cross_key_full)
        .astype(jnp.bfloat16)
        .reshape(seqs_dev, groups, NK, HEADS, HEAD_DIM)
    )
    cross_v = (
        project(neighbours, cross_value_full)
        .astype(jnp.bfloat16)
        .reshape(seqs_dev, groups, NK, HEADS, HEAD_DIM)
    )
    cross_scores = (
        jnp.einsum("sczhe,sckhe->schzk", cross_q, cross_k, preferred_element_type=jnp.float32)
        * scale
    )
    cross_raised = jnp.exp(cross_scores - jnp.max(cross_scores, axis=-1, keepdims=True))
    cross_shares = cross_raised / jnp.sum(cross_raised, axis=-1, keepdims=True)
    cross_low = cross_shares.astype(jnp.bfloat16)
    crossed = jnp.einsum(
        "schzk,sckhe->sczhe", cross_low, cross_v, preferred_element_type=jnp.float32
    )
    crossed_low = crossed.reshape(seqs_dev, tok_dev, attn_width).astype(jnp.bfloat16)
    hidden_two = hidden_one + project(crossed_low, cross_output_full)
    normed_c = rms_scale(hidden_two, gain_three).astype(jnp.bfloat16)
    pre_act = project(normed_c, up_full)
    activated = gelu_tanh(pre_act).astype(jnp.bfloat16)
    layer_out = hidden_two + project(activated, down_full)
    valid = valid_mask.astype(jnp.float32)
    error = layer_out - teacher.astype(jnp.float32)
    error_sum, valid_count = lax.psum(
        (jnp.sum(valid[..., None] * error * error), jnp.sum(valid)), ("ctx", "wa")
    )
    loss = error_sum / (2.0 * valid_count * width)
    token_total = seqs_dev * lax.axis_size("wa") * seq_len
    out_grad = token_total / valid_count * valid[..., None] * error
    out_low = out_grad.astype(jnp.bfloat16)
    down_grad = outer_sum(activated, out_low)
    act_grad = project_back(out_low, down_full)
    _, gelu_pull = jax.vjp(gelu_tanh, pre_act)
    pre_grad = gelu_pull(act_grad)[0].astype(jnp.bfloat16)
    up_grad = outer_sum(normed_c, pre_grad)
    back_two, third_gain_grad = norm_back(hidden_two, gain_three, project_back(pre_grad, up_full))
    two_grad = out_grad + back_two
    two_low = two_grad.astype(jnp.bfloat16)
    cross_output_grad = outer_sum(crossed_low, two_low)
    crossed_grad = project_back(two_low, cross_output_full).astype(jnp.bfloat16)
    crossed_grad = crossed_grad.reshape(seqs_dev, groups, GROUP, HEADS, HEAD_DIM)
    cross_share_grad = jnp.einsum(
        "sczhe,sckhe->schzk", crossed_grad, cross_v, preferred_element_type=jnp.float32
    )
    cross_score_grad = (
        cross_shares
        * (cross_share_grad - jnp.sum(cross_shares * cross_share_grad, axis=-1, keepdims=True))
    ).astype(jnp.bfloat16)
    cross_q_grad = (
        (
            jnp.einsum(
                "schzk,sckhe->sczhe", cross_score_grad, cross_k, preferred_element_type=jnp.float32
            )
            * scale
        )
        .astype(jnp.bfloat16)
        .reshape(seqs_dev, tok_dev, attn_width)
    )
    cross_k_grad = (
        (
            jnp.einsum(
                "schzk,sczhe->sckhe", cross_score_grad, cross_q, preferred_element_type=jnp.float32
            )
            * scale
        )
        .astype(jnp.bfloat16)
        .reshape(seqs_dev, groups, NK, attn_width)
    )
    cross_v_grad = (
        jnp.einsum(
            "schzk,sczhe->sckhe", cross_low, crossed_grad, preferred_element_type=jnp.float32
        )
        .astype(jnp.bfloat16)
        .reshape(seqs_dev, groups, NK, attn_width)
    )
    cross_query_grad = outer_sum(normed_b, cross_q_grad)
    cross_key_grad = outer_sum(neighbours, cross_k_grad)
    cross_value_grad = outer_sum(neighbours, cross_v_grad)
    neighbours_grad = project_back(cross_k_grad, cross_key_full) + project_back(
        cross_v_grad, cross_value_full
    )
    back_one, second_gain_grad = norm_back(
        hidden_one, gain_two, project_back(cross_q_grad, cross_query_full)
    )
    one_grad = two_grad + back_one
    one_low = one_grad.astype(jnp.bfloat16)
    output_grad = outer_sum(attended_low, one_low)
    attended_grad = project_back(one_low, output_full).astype(jnp.bfloat16)
    grad_tiles = attended_grad.reshape(tile_lead)
    delta = jnp.einsum("sbqhe,sbhqe->sbhq", grad_tiles.astype(jnp.float32), attended_tiles)
    blocks_per_step = key_len // block

    def backward_step(carry, index):
        key_start = index * key_len
        key_rows = lax.dynamic_slice_in_dim(key_glob, key_start, key_len, 1)
        value_rows = lax.dynamic_slice_in_dim(value_glob, key_start, key_len, 1)

        def backward_tile(content_rows, position_rows, row_start, keys_seq, values_seq, extra):
            return tile_backward(
                content_rows,
                position_rows,
                row_start,
                keys_seq,
                values_seq,
                extra[0],
                extra[1],
                extra[2],
                table,
                key_start,
                seq_len,
            )

        parts = nest_tiles(backward_tile)(
            content_tiles,
            position_tiles,
            row_starts,
            key_rows,
            value_rows,
            (grad_tiles, log_total, delta),
        )
        content_acc = carry[0] + parts[0]
        position_acc = carry[1] + parts[1]
        table_acc = carry[2]
        table_sum = jnp.sum(parts[2], axis=0)
        for slot in range(2):
            offset = seq_len - block - row_starts[slot] + key_start
            current = lax.dynamic_slice_in_dim(table_acc, offset, block + key_len, 0)
            table_acc = lax.dynamic_update_slice_in_dim(
                table_acc, current + table_sum[slot], offset, 0
            )
        stored_slots = lax.dynamic_slice_in_dim(inverse, key_start // block, blocks_per_step, 0)
        piece_shape = (seqs_dev, blocks_per_step, block, HEADS, HEAD_DIM)
        key_piece = jnp.sum(parts[3], axis=1).reshape(piece_shape)
        value_piece = jnp.sum(parts[4], axis=1).reshape(piece_shape)
        key_acc = carry[3].at[:, stored_slots].add(key_piece)
        value_acc = carry[4].at[:, stored_slots].add(value_piece)
        return ((content_acc, position_acc, table_acc, key_acc, value_acc), None)

    zero_tiles = jnp.zeros(tile_lead, jnp.float32)
    start_carry = (zero_tiles, zero_tiles, jnp.zeros((table_rows, HEADS, HEAD_DIM), jnp.float32))
    zero_keys = jnp.zeros((seqs_dev, 2 * ctx_count, block, HEADS, HEAD_DIM), jnp.float32)
    start_carry = start_carry + (zero_keys, zero_keys)
    carried, _ = lax.scan(backward_step, start_carry, jnp.arange(key_steps))
    content_acc, position_acc, table_acc = (carried[0], carried[1], carried[2])
    key_mine, value_mine = (
        lax.psum_scatter(
            carried[3].reshape(seqs_dev, seq_len, attn_width),
            "ctx",
            scatter_dimension=1,
            tiled=True,
        ),
        lax.psum_scatter(
            carried[4].reshape(seqs_dev, seq_len, attn_width),
            "ctx",
            scatter_dimension=1,
            tiled=True,
        ),
    )
    content_bias_grad = jnp.sum(content_acc, axis=(0, 1, 2)).reshape(attn_width)
    position_bias_grad = jnp.sum(position_acc, axis=(0, 1, 2)).reshape(attn_width)
    query_grad = (
        (content_acc + position_acc).reshape(seqs_dev, tok_dev, attn_width).astype(jnp.bfloat16)
    )
    key_low = key_mine.astype(jnp.bfloat16)
    value_low = value_mine.astype(jnp.bfloat16)
    query_weight_grad = outer_sum(normed_a, query_grad)
    key_weight_grad = outer_sum(normed_a, key_low)
    value_weight_grad = outer_sum(normed_a, value_low)
    normed_a_grad = (
        project_back(query_grad, query_full)
        + project_back(key_low, key_full)
        + project_back(value_low, value_full)
    )
    back_zero, first_gain_grad = norm_back(hidden_in, gain_one, normed_a_grad)
    tokens_grad = one_grad + back_zero
    table_flat = table_acc.reshape(table_rows, attn_width)[:seq_len]
    relative_rows = lax.psum_scatter(table_flat, ("ctx", "wa"), scatter_dimension=0, tiled=True)
    relative_grad = outer_exact(own_sinusoid, relative_rows)
    owned = (
        lax.psum_scatter(
            query_weight_grad.astype(jnp.bfloat16), "wa", scatter_dimension=0, tiled=True
        ).astype(jnp.float32),
        lax.psum_scatter(
            key_weight_grad.astype(jnp.bfloat16), "wa", scatter_dimension=0, tiled=True
        ).astype(jnp.float32),
        lax.psum_scatter(
            value_weight_grad.astype(jnp.bfloat16), "wa", scatter_dimension=0, tiled=True
        ).astype(jnp.float32),
        lax.psum_scatter(
            output_grad.astype(jnp.bfloat16), "wa", scatter_dimension=0, tiled=True
        ).astype(jnp.float32),
        lax.psum_scatter(
            relative_grad.astype(jnp.bfloat16), "wa", scatter_dimension=0, tiled=True
        ).astype(jnp.float32),
        lax.psum_scatter(
            content_bias_grad.astype(jnp.bfloat16), "wa", scatter_dimension=0, tiled=True
        ).astype(jnp.float32),
        lax.psum_scatter(
            position_bias_grad.astype(jnp.bfloat16), "wa", scatter_dimension=0, tiled=True
        ).astype(jnp.float32),
        lax.psum_scatter(
            cross_query_grad.astype(jnp.bfloat16), "wa", scatter_dimension=0, tiled=True
        ).astype(jnp.float32),
        lax.psum_scatter(
            cross_key_grad.astype(jnp.bfloat16), "wa", scatter_dimension=0, tiled=True
        ).astype(jnp.float32),
        lax.psum_scatter(
            cross_value_grad.astype(jnp.bfloat16), "wa", scatter_dimension=0, tiled=True
        ).astype(jnp.float32),
        lax.psum_scatter(
            cross_output_grad.astype(jnp.bfloat16), "wa", scatter_dimension=0, tiled=True
        ).astype(jnp.float32),
        lax.psum_scatter(
            up_grad.astype(jnp.bfloat16), "wa", scatter_dimension=0, tiled=True
        ).astype(jnp.float32),
        lax.psum_scatter(
            down_grad.astype(jnp.bfloat16), "wa", scatter_dimension=0, tiled=True
        ).astype(jnp.float32),
        lax.psum_scatter(
            first_gain_grad.astype(jnp.bfloat16), "wa", scatter_dimension=0, tiled=True
        ).astype(jnp.float32),
        lax.psum_scatter(
            second_gain_grad.astype(jnp.bfloat16), "wa", scatter_dimension=0, tiled=True
        ).astype(jnp.float32),
        lax.psum_scatter(
            third_gain_grad.astype(jnp.bfloat16), "wa", scatter_dimension=0, tiled=True
        ).astype(jnp.float32),
    )
    summed = lax.psum(
        (
            owned[0],
            owned[1],
            owned[2],
            owned[3],
            owned[4],
            owned[5],
            owned[6],
            owned[7],
            owned[8],
            owned[9],
            owned[10],
            owned[11],
            owned[12],
            owned[13],
            owned[14],
            owned[15],
        ),
        "ctx",
    )
    return (
        layer_out,
        loss,
        tokens_grad,
        neighbours_grad,
        summed[0],
        summed[1],
        summed[2],
        summed[3],
        summed[4],
        summed[5],
        summed[6],
        summed[7],
        summed[8],
        summed[9],
        summed[10],
        summed[11],
        summed[12],
        summed[13],
        summed[14],
        summed[15],
    )


def solution(mesh):
    in_specs = (
        P("wa", "ctx", None),
        P("wa", "ctx", None, None),
        P("wa", "ctx", None),
        P("wa", "ctx"),
        P(),
        P("wa", None),
        P("wa", None),
        P("wa", None),
        P("wa", None),
        P("wa", None),
        P("wa"),
        P("wa"),
        P("wa", None),
        P("wa", None),
        P("wa", None),
        P("wa", None),
        P("wa", None),
        P("wa", None),
        P("wa"),
        P("wa"),
        P("wa"),
    )
    out_specs = (
        P("wa", "ctx", None),
        P(),
        P("wa", "ctx", None),
        P("wa", "ctx", None, None),
        P("wa", None),
        P("wa", None),
        P("wa", None),
        P("wa", None),
        P("wa", None),
        P("wa"),
        P("wa"),
        P("wa", None),
        P("wa", None),
        P("wa", None),
        P("wa", None),
        P("wa", None),
        P("wa", None),
        P("wa"),
        P("wa"),
        P("wa"),
    )
    return jax.shard_map(local, mesh=mesh, in_specs=in_specs, out_specs=out_specs, check_vma=False)
```

profile of v0, /device:TPU:0, one launch (start us, length us, event | category | flops | bytes accessed | tf_op | source)
XLA Modules:
  0.0 2145.5 jit_solution(16097502657547615393)
XLA Ops:
  21.9 11.6 all-gather.24.cloned.1.call-done
  36.3 19.9 all-gather.18.cloned.1.call-done
  107.6 16.6 all-gather.32.cloned.1.call-done
  130.1 16.6 all-gather.22.cloned.1.call-done
  166.4 32.4 %all-gather.42.cloned.1.call-done = bf16[1024,1024]{1,0:T(8,128)(2,1)} async-done(((bf16[128,1024]{1,0:T(8,128)(2,1)}), bf16[1024,1024]{1,0:T(8,128)(2,1)}) %all-gather.42.cloned.1.call-update) | async-done | bytes 2097168 | tf_op jit(solution)/shard_map/all_gather | solution.py:254
  202.5 46.8 %all-gather.40.cloned.1.call-done = bf16[1024,1024]{1,0:T(8,128)(2,1)} async-done(((bf16[128,1024]{1,0:T(8,128)(2,1)}), bf16[1024,1024]{1,0:T(8,128)(2,1)}) %all-gather.40.cloned.1.call-update) | async-done | bytes 2097168 | tf_op jit(solution)/shard_map/all_gather | solution.py:253
  278.6 103.0 %while.45 = (s32[]{:T(128)}, f32[1,2,16,64]{3,1,2,0:T(2,128)S(1)}, f32[1,2,16,64]{3,1,2,0:T(2,128)S(1)}, f32[1,2,16,64,64]{4,3,1,2,0:T(8,128)}, s32[2]{0:T(128)S...) while((s32[]{:T(128)}, f32[1,2,16,64]{3,1,2,0:T(2,128)S(1)}, ...), condition=%wide.region_5.7_spmd.clone, body=%wide.region_2.6_spmd.clone.sunk | while | flops 436679296 | bytes 128112296 | solution.py:292
  280.3 16.3 while.48
  331.5 16.4 while.48
  418.4 39.8 %all-reduce.15 = (f32[]{:T(128)}, f32[]{:T(128)}) all-reduce(f32[]{:T(128)} %convert_reduce_fusion, f32[]{:T(128)} %get-tuple-element.871), channel_id=1, replica_groups=mesh['ctx'=8,'wa'=4] {'ctx','wa'}, use_global_device_ids=true, to_apply=%region_13.15 | all-reduce | flops 2 | bytes 16 | tf_op jit(solution)/shard_map/psum | solution.py:337
  503.8 309.9 %while.47 = (s32[]{:T(128)}, f32[1,2,64,16,64]{2,4,1,3,0:T(8,128)}, f32[1,2,64,16,64]{2,4,3,1,0:T(8,128)}, f32[1600,16,64]{0,2,1:T(8,128)}, f32[1,16,64,16,64]{4...) while((s32[]{:T(128)}, f32[1,2,64,16,64]{2,4,1,3,0:T(8,128)}, ...), condition=%wide.region_21.23_spmd.clone, body=%wide.region_17.22_spmd.clone.sunk | while | flops 1142489728 | bytes 261704432 | solution.py:456
  509.7 16.3 while.49
  612.9 10.5 dynamic_update_slice.16
  626.8 12.6 dynamic_update_slice.17
  664.0 16.3 while.49
  768.5 9.9 dynamic_update_slice.16
  781.9 12.4 dynamic_update_slice.17
  868.0 42.1 %reduce-scatter.23.cloned.1.call-done = f32[1,128,1024]{2,1,0:T(8,128)} async-done(((f32[1,1024,1024]{2,1,0:T(8,128)}), f32[1,128,1024]{2,1,0:T(8,128)}) %reduce-scatter.23.cloned.1.call-update) | async-done | bytes 524304 | tf_op jit(solution)/shard_map/reduce_scatter | solution.py:465
  913.6 139.4 %reduce-scatter.43.cloned.1.call-done = f32[32,1024]{1,0:T(8,128)} async-done(((f32[1024,1024]{1,0:T(8,128)}), f32[32,1024]{1,0:T(8,128)}) %reduce-scatter.43.cloned.1.call-update) | async-done | bytes 131088
  1057.0 83.9 %reduce-scatter.21.cloned.1.call-done = f32[1,128,1024]{2,1,0:T(8,128)} async-done(((f32[1,1024,1024]{2,1,0:T(8,128)}), f32[1,128,1024]{2,1,0:T(8,128)}) %reduce-scatter.21.cloned.1.call-update) | async-done | bytes 524304 | tf_op jit(solution)/shard_map/reduce_scatter | solution.py:459
  1174.9 30.4 %reduce-scatter.47.cloned.1.call-done = bf16[224,1024]{1,0:T(8,128)(2,1)} async-done(((bf16[896,1024]{1,0:T(8,128)(2,1)}), bf16[224,1024]{1,0:T(8,128)(2,1)}) %reduce-scatter.47.cloned.1.call-update) | async-done | bytes 458768
  1207.3 30.4 %reduce-scatter.35.cloned.1.call-done = bf16[224,1024]{1,0:T(8,128)(2,1)} async-done(((bf16[896,1024]{1,0:T(8,128)(2,1)}), bf16[224,1024]{1,0:T(8,128)(2,1)}) %reduce-scatter.35.cloned.1.call-update) | async-done | bytes 458768 | tf_op jit(solution)/shard_map/reduce_scatter | solution.py:514
  1237.7 32.4 %reduce-scatter.37.cloned.1.call-done = bf16[256,896]{1,0:T(8,128)(2,1)} async-done(((bf16[1024,896]{1,0:T(8,128)(2,1)}), bf16[256,896]{1,0:T(8,128)(2,1)}) %reduce-scatter.37.cloned.1.call-update) | async-done | bytes 458768 | tf_op jit(solution)/shard_map/reduce_scatter | solution.py:523
  1270.1 32.4 %reduce-scatter.31.cloned.1.call-done = bf16[256,896]{1,0:T(8,128)(2,1)} async-done(((bf16[1024,896]{1,0:T(8,128)(2,1)}), bf16[256,896]{1,0:T(8,128)(2,1)}) %reduce-scatter.31.cloned.1.call-update) | async-done | bytes 458768 | tf_op jit(solution)/shard_map/reduce_scatter | solution.py:502
  1302.5 33.2 %reduce-scatter.25.cloned.1.call-done = bf16[224,1024]{1,0:T(8,128)(2,1)} async-done(((bf16[896,1024]{1,0:T(8,128)(2,1)}), bf16[224,1024]{1,0:T(8,128)(2,1)}) %reduce-scatter.25.cloned.1.call-update) | async-done | bytes 458768 | tf_op jit(solution)/shard_map/reduce_scatter | solution.py:493
  1338.6 10.4 all-reduce.17
  1350.2 17.8 reduce-scatter.29.cloned.1.call-done
  1368.0 32.4 %reduce-scatter.33.cloned.1.call-done = bf16[224,1024]{1,0:T(8,128)(2,1)} async-done(((bf16[896,1024]{1,0:T(8,128)(2,1)}), bf16[224,1024]{1,0:T(8,128)(2,1)}) %reduce-scatter.33.cloned.1.call-update) | async-done | bytes 458768 | tf_op jit(solution)/shard_map/reduce_scatter | solution.py:505
  1400.4 32.9 %reduce-scatter.27.cloned.1.call-done = bf16[224,1024]{1,0:T(8,128)(2,1)} async-done(((bf16[896,1024]{1,0:T(8,128)(2,1)}), bf16[224,1024]{1,0:T(8,128)(2,1)}) %reduce-scatter.27.cloned.1.call-update) | async-done | bytes 458768 | tf_op jit(solution)/shard_map/reduce_scatter | solution.py:496
  1433.4 61.9 %reduce-scatter.41.cloned.1.call-done = bf16[896,896]{1,0:T(8,128)(2,1)} async-done(((bf16[3584,896]{1,0:T(8,128)(2,1)}), bf16[896,896]{1,0:T(8,128)(2,1)}) %reduce-scatter.41.cloned.1.call-update) | async-done | bytes 1605648 | tf_op jit(solution)/shard_map/reduce_scatter | solution.py:529
  1495.3 61.7 %reduce-scatter.39.cloned.1.call-done = bf16[224,3584]{1,0:T(8,128)(2,1)} async-done(((bf16[896,3584]{1,0:T(8,128)(2,1)}), bf16[224,3584]{1,0:T(8,128)(2,1)}) %reduce-scatter.39.cloned.1.call-update) | async-done | bytes 1605648 | tf_op jit(solution)/shard_map/reduce_scatter | solution.py:526
  1557.0 576.6 %all-reduce.20 = (f32[224,1024]{1,0:T(8,128)}, f32[224,1024]{1,0:T(8,128)}, f32[224,1024]{1,0:T(8,128)}, f32[256,896]{1,0:T(8,128)}, f32[224,1024]{1,0:T(8,128)}...) all-reduce(bf16[224,1024]{1,0:T(8,128)(2,1)} %reduce-scatter.25.clo, ...), channel_id=1, replica_groups=mesh['ctx'=8,'wa'=4] {'ctx'}, use_global_device_ids=true, to_apply=%region_26.28 | all-reduce | flops 3671200 | bytes 22029568 | tf_op jit(solution)/shard_map/psum | solution.py:542
  (622 shorter events, 671.6 us)
Async XLA Ops:
  7.3 26.2 %all-gather.24.cloned.1.call-start = ((), (), s32[]{:S(2)}) async-start(), calls=%async_computation.17 | async-start | bytes 2293760 | tf_op jit(solution)/shard_map/all_gather | solution.py:202
  8.0 48.2 %all-gather.18.cloned.1.call-start = ((), (), s32[]{:S(2)}) async-start(), calls=%async_computation.14 | async-start | bytes 2293760 | tf_op jit(solution)/shard_map/all_gather | solution.py:201
  8.7 80.2 %all-gather.20.cloned.1.call-start = ((), (), s32[]{:S(2)}) async-start(), calls=%async_computation.15 | async-start | bytes 2293760 | tf_op jit(solution)/shard_map/all_gather | solution.py:200
  9.5 92.1 %all-gather.28.cloned.1.call-start = ((), (), s32[]{:S(2)}) async-start(), calls=%async_computation.19 | async-start | bytes 2293760 | tf_op jit(solution)/shard_map/all_gather | solution.py:209
  10.1 114.1 %all-gather.32.cloned.1.call-start = ((), (), s32[]{:S(2)}) async-start(), calls=%async_computation.21 | async-start | bytes 2293760 | tf_op jit(solution)/shard_map/all_gather | solution.py:208
  10.6 136.1 %all-gather.22.cloned.1.call-start = ((), (), s32[]{:S(2)}) async-start(), calls=%async_computation.16 | async-start | bytes 2293760 | tf_op jit(solution)/shard_map/all_gather | solution.py:204
  11.2 187.5 %all-gather.42.cloned.1.call-start = ((), (), s32[]{:S(2)}) async-start(), calls=%async_computation.37 | async-start | bytes 2359296 | tf_op jit(solution)/shard_map/all_gather | solution.py:254
  36.2 213.0 %all-gather.40.cloned.1.call-start = ((), (), s32[]{:S(2)}) async-start(), calls=%async_computation.36 | async-start | bytes 2359296 | tf_op jit(solution)/shard_map/all_gather | solution.py:253
  58.9 325.2 %all-gather.26.cloned.1.call-start = ((), (), s32[]{:S(2)}) async-start(), calls=%async_computation.18 | async-start | bytes 2293760 | tf_op jit(solution)/shard_map/all_gather | solution.py:203
  59.7 326.6 %all-gather.30.cloned.1.call-start = ((), (), s32[]{:S(2)}) async-start(), calls=%async_computation.20 | async-start | bytes 2293760 | tf_op jit(solution)/shard_map/all_gather | solution.py:207
  60.3 339.8 %all-gather.34.cloned.1.call-start = ((), (), s32[]{:S(2)}) async-start(), calls=%async_computation.22 | async-start | bytes 2293760 | tf_op jit(solution)/shard_map/all_gather | solution.py:210
  61.1 341.3 %all-gather.36.cloned.1.call-start = ((), (), s32[]{:S(2)}) async-start(), calls=%async_computation.23 | async-start | bytes 8028160 | tf_op jit(solution)/shard_map/all_gather | solution.py:211
  61.6 351.5 %all-gather.38.cloned.1.call-start = ((), (), s32[]{:S(2)}) async-start(), calls=%async_computation.24 | async-start | bytes 8028160 | tf_op jit(solution)/shard_map/all_gather | solution.py:212
  62.4 847.8 %reduce-scatter.23.cloned.1.call-start = ((), (), s32[]{:S(2)}) async-start(), calls=%async_computation.26 | async-start | bytes 4718592 | tf_op jit(solution)/shard_map/reduce_scatter | solution.py:465
  386.2 99.5 %copy-start.23 = (f32[1,128,896]{2,1,0:T(8,128)}, f32[1,128,896]{2,1,0:T(8,128)S(1)}, u32[]{:S(2)}) copy-start(f32[1,128,896]{2,1,0:T(8,128)S(1)} %get-tuple-element.866) | copy-start | bytes 1376260
  386.3 99.5 %copy-start.90 = (f32[128]{0:T(128)}, f32[128]{0:T(128)S(1)}, u32[]{:S(2)}) copy-start(f32[128]{0:T(128)S(1)} %fusion.151) | copy-start | bytes 1540
  821.3 231.7 %reduce-scatter.43.cloned.1.call-start = ((), (), s32[]{:S(2)}) async-start(), calls=%async_computation.38 | async-start | bytes 4325376
  831.5 309.4 %reduce-scatter.21.cloned.1.call-start = ((), (), s32[]{:S(2)}) async-start(), calls=%async_computation.25 | async-start | bytes 4718592 | tf_op jit(solution)/shard_map/reduce_scatter | solution.py:459
  839.2 333.7 %reduce-scatter.45.cloned.1.call-start = ((), (), s32[]{:S(2)}) async-start(), calls=%async_computation.39 | async-start | bytes 2293760
  848.8 356.5 %reduce-scatter.47.cloned.1.call-start = ((), (), s32[]{:S(2)}) async-start(), calls=%async_computation.40 | async-start | bytes 2293760
  857.2 380.4 %reduce-scatter.35.cloned.1.call-start = ((), (), s32[]{:S(2)}) async-start(), calls=%async_computation.32 | async-start | bytes 2293760 | tf_op jit(solution)/shard_map/reduce_scatter | solution.py:514
  859.3 410.8 %reduce-scatter.37.cloned.1.call-start = ((), (), s32[]{:S(2)}) async-start(), calls=%async_computation.33 | async-start | bytes 2293760 | tf_op jit(solution)/shard_map/reduce_scatter | solution.py:523
  861.3 441.2 %reduce-scatter.31.cloned.1.call-start = ((), (), s32[]{:S(2)}) async-start(), calls=%async_computation.30 | async-start | bytes 2293760 | tf_op jit(solution)/shard_map/reduce_scatter | solution.py:502
  863.3 472.3 %reduce-scatter.25.cloned.1.call-start = ((), (), s32[]{:S(2)}) async-start(), calls=%async_computation.27 | async-start | bytes 2293760 | tf_op jit(solution)/shard_map/reduce_scatter | solution.py:493
  867.8 500.2 %reduce-scatter.29.cloned.1.call-start = ((), (), s32[]{:S(2)}) async-start(), calls=%async_computation.29 | async-start | bytes 2293760 | tf_op jit(solution)/shard_map/reduce_scatter | solution.py:499
  913.2 487.2 %reduce-scatter.33.cloned.1.call-start = ((), (), s32[]{:S(2)}) async-start(), calls=%async_computation.31 | async-start | bytes 2293760 | tf_op jit(solution)/shard_map/reduce_scatter | solution.py:505
  1056.9 376.5 %reduce-scatter.27.cloned.1.call-start = ((), (), s32[]{:S(2)}) async-start(), calls=%async_computation.28 | async-start | bytes 2293760 | tf_op jit(solution)/shard_map/reduce_scatter | solution.py:496
  1143.9 351.3 %reduce-scatter.41.cloned.1.call-start = ((), (), s32[]{:S(2)}) async-start(), calls=%async_computation.35 | async-start | bytes 8028160 | tf_op jit(solution)/shard_map/reduce_scatter | solution.py:529
  1149.6 407.3 %reduce-scatter.39.cloned.1.call-start = ((), (), s32[]{:S(2)}) async-start(), calls=%async_computation.34 | async-start | bytes 8028160 | tf_op jit(solution)/shard_map/reduce_scatter | solution.py:526
  1168.3 167.4 %copy-start.31 = (bf16[896,1024]{1,0:T(8,128)(2,1)S(1)}, bf16[896,1024]{1,0:T(8,128)(2,1)}, u32[]{:S(2)}) copy-start(bf16[896,1024]{1,0:T(8,128)(2,1)} %all-gather.18.cloned.1.call-done) | copy-start | bytes 5505028
  1337.7 219.2 %copy-start.56 = (bf16[224,1024]{0,1:T(8,128)(2,1)S(1)}, bf16[224,1024]{0,1:T(8,128)(2,1)}, u32[]{:S(2)}) copy-start(bf16[224,1024]{0,1:T(8,128)(2,1)} %copy.219) | copy-start | bytes 1376260
  1337.7 219.2 %copy-start.57 = (bf16[224,1024]{0,1:T(8,128)(2,1)S(1)}, bf16[224,1024]{0,1:T(8,128)(2,1)}, u32[]{:S(2)}) copy-start(bf16[224,1024]{0,1:T(8,128)(2,1)} %copy.221) | copy-start | bytes 1376260
  (130 other events, 1402.6 us)
Sparse Core Ops, SparseCore 0:
  9.7 23.8 all-gather.23
  35.1 21.1 all-gather.17
  57.8 21.1 all-gather.19
  80.4 21.1 all-gather.27
  103.0 21.1 all-gather.31
  125.6 21.1 all-gather.21
  149.4 49.2 all-gather.41
  201.4 47.7 all-gather.39
  250.8 19.5 all-gather.25
  271.9 21.1 all-gather.29
  294.6 21.1 all-gather.33
  317.2 47.1 all-gather.35
  365.9 47.1 all-gather.37
  821.4 88.7 reduce-scatter.22
  912.4 140.5 reduce-scatter.42
  1056.9 83.9 reduce-scatter.20
  1143.3 29.5 reduce-scatter.44
  1175.4 29.8 reduce-scatter.46
  1207.8 29.7 reduce-scatter.34
  1240.2 29.8 reduce-scatter.36
  1272.6 29.7 reduce-scatter.30
  1305.7 29.8 reduce-scatter.24
  1338.2 29.7 reduce-scatter.28
  1370.6 29.8 reduce-scatter.32
  1403.5 29.7 reduce-scatter.26
  1436.0 59.2 reduce-scatter.40
  1497.7 59.2 reduce-scatter.38
where the time goes:
time: 2150 us
  waiting for transfers between devices  798 us (37%)
  blocking collectives  646 us (30%)
  local copies, waits for them, and re-layouts  411 us (19%)
  matrix products  165 us (8%)
  other arithmetic  98.2 us (5%)
  between operations  22.7 us (1%)
    psum x1, blocking collectives, local(): lax.psum((owned[0], owned[1], owned[2], owned[3], owned[4], owned[5], own...  577 us
    unnamed x30, waiting for transfers between devices  181 us
    reduce_scatter x1, waiting for transfers between devices, local(): lax.psum_scatter(carried[3].reshape(seqs_dev, seq_len, attn_width), 'ctx'...  83.9 us
    gather x32, local copies, waits for them, and re-layouts  65.3 us
    reduce_scatter x1, waiting for transfers between devices, local(): lax.psum_scatter(down_grad.astype(jnp.bfloat16), 'wa', scatter_dimension=...  61.9 us
    reduce_scatter x1, waiting for transfers between devices, local(): lax.psum_scatter(up_grad.astype(jnp.bfloat16), 'wa', scatter_dimension=0,...  61.7 us
    unnamed x205, local copies, waits for them, and re-layouts  56.4 us
    all_gather x1, waiting for transfers between devices, local(): lax.all_gather(key_local, 'ctx', axis=1, tiled=True)  46.8 us
  transfers between devices with their start and end apart: 27, of which 22 were waited for; matrix products, arithmetic and copies ran while one was open for 14% of the time, Pallas kernels for 0%

commit v1 on v0

v1 whole, which is shorter than its diff:
```python
import functools

import jax
import jax.numpy as jnp
from jax import lax
from jax.experimental import pallas as pl
from jax.experimental.pallas import tpu as pltpu
from jax.sharding import PartitionSpec as P

HEADS = 16
HEAD_DIM = 64
GROUP = 64
NK = 256
TILE = 128

eps_norm = 1e-06
neg_big = -1e30
highest = lax.Precision.HIGHEST
f32 = jnp.float32
bf16 = jnp.bfloat16


def inverse_rms(hidden):
    return lax.rsqrt(jnp.mean(hidden * hidden, axis=-1, keepdims=True) + eps_norm)


def norm_pull(hidden, scale, gain, grad):
    scaled = grad * gain
    mean = jnp.mean(hidden * scaled, axis=-1, keepdims=True)
    return scale * scaled - hidden * (scale * scale * scale) * mean


def gelu_tanh(value):
    return jax.nn.gelu(value, approximate=True)


def sinusoid(distance, width):
    half = width // 2
    freq = jnp.exp(-jnp.log(10000.0) * jnp.arange(half, dtype=f32) * 2.0 / width)
    angle = distance[:, None] * freq[None, :]
    return jnp.concatenate([jnp.sin(angle), jnp.cos(angle)], axis=1)


def dot_nn(a, b):
    return lax.dot_general(a, b, (((1,), (0,)), ((), ())), preferred_element_type=f32)


def dot_nt(a, b):
    return lax.dot_general(a, b, (((1,), (1,)), ((), ())), preferred_element_type=f32)


def dot_tn(a, b):
    return lax.dot_general(a, b, (((0,), (0,)), ((), ())), preferred_element_type=f32)


def swap(value, axis, bit):
    pairs = [(i, i ^ bit) for i in range(lax.axis_size(axis))]
    return lax.ppermute(value, axis, pairs)


def bits_of(axis):
    bits, bit = [], 1
    while bit < lax.axis_size(axis):
        bits.append(bit)
        bit *= 2
    return bits


def my_bit(axis, bit):
    return (lax.axis_index(axis) // bit) % 2


def ordered(bit, own, other, dim):
    return jnp.where(
        bit == 0,
        jnp.concatenate([own, other], axis=dim),
        jnp.concatenate([other, own], axis=dim),
    )


def split(value, bit, dim):
    half = value.shape[dim] // 2
    keep = lax.dynamic_slice_in_dim(value, bit * half, half, dim)
    send = lax.dynamic_slice_in_dim(value, (1 - bit) * half, half, dim)
    return keep, send


def gather_parts(value):
    parts = {0: value}
    for bit in reversed(bits_of("wa")):
        parts.update({r | bit: swap(part, "wa", bit) for r, part in list(parts.items())})
    return [parts[r] for r in sorted(parts)]


def scatter_parts(parts):
    parts = dict(enumerate(parts))
    for bit in bits_of("wa"):
        kept = {}
        for r, part in parts.items():
            if not r & bit:
                got = swap(parts[r | bit].astype(bf16), "wa", bit)
                kept[r] = part + got.astype(f32)
        parts = kept
    return parts[0]


def take_columns(weight):
    value = weight[None]
    for bit in reversed(bits_of("wa")):
        mine = my_bit("wa", bit)
        keep, send = split(value, mine, 2)
        value = ordered(mine, keep[:, None], swap(send, "wa", bit)[:, None], 1)
        value = value.reshape((-1,) + value.shape[2:])
    return value.reshape(-1, value.shape[-1])


def spread_columns(value):
    for bit in bits_of("wa"):
        mine = my_bit("wa", bit)
        paired = value.reshape((value.shape[0], value.shape[1] // 2, 2) + value.shape[2:])
        keep, send = split(paired, mine, 2)
        value = ordered(mine, keep[:, :, 0], swap(send[:, :, 0], "wa", bit), 3)
    return value[:, 0]


def halving_dim(shape):
    if shape[-2] % 16 == 0:
        return len(shape) - 2
    if shape[0] % 2 == 0:
        return 0
    if shape[-2] % 2 == 0:
        return len(shape) - 2
    return len(shape) - 1


def sum_over_ctx(value, bits, finish):
    dims = []
    for bit in bits:
        dim = halving_dim(value.shape)
        keep, send = split(value, my_bit("ctx", bit), dim)
        value = (keep.astype(f32) + swap(send, "ctx", bit).astype(f32)).astype(bf16)
        dims.append(dim - value.ndim if dim else 0)
    value = finish(value)
    for bit, dim in reversed(list(zip(bits, dims))):
        dim = dim % value.ndim
        value = ordered(my_bit("ctx", bit), value, swap(value, "ctx", bit), dim)
    return value


def all_summed(value, axis):
    for bit in bits_of(axis):
        value = value + swap(value, axis, bit)
    return value


def sum_column_grads(grads):
    places = lax.axis_size("wa")
    grads = grads.reshape(grads.shape[0], places, grads.shape[1] // places, grads.shape[2])
    bits = bits_of("ctx")
    if grads.shape[2] % lax.axis_size("ctx") == 0:
        return sum_over_ctx(grads, bits, spread_columns).astype(f32)
    return sum_over_ctx(spread_columns(grads), bits, lambda value: value).astype(f32)


def sum_row_grads(grads):
    return sum_over_ctx(grads[None], bits_of("ctx"), lambda value: value)[0].astype(f32)


def first_half(shape):
    return lax.broadcasted_iota(jnp.int32, shape, 1) < HEAD_DIM


def stack_heads(rows):
    mask = first_half(rows.shape)
    zero = jnp.zeros_like(rows)
    return jnp.concatenate([jnp.where(mask, rows, zero), jnp.where(mask, zero, rows)], axis=0)


def join_heads(stacked):
    rows = stacked.shape[0] // 2
    return jnp.where(first_half((rows, stacked.shape[1])), stacked[:rows], stacked[rows:])


def copy_blocks(order_ref, source, target, block, inward):
    for place in range(source.shape[0] // block):
        start = pl.multiple_of(order_ref[place] * block, block)
        if inward:
            target[place * block : (place + 1) * block, :] = source[pl.ds(start, block), :]
        else:
            target[pl.ds(start, block), :] = source[place * block : (place + 1) * block, :]


def attention_shares(content, position, key_ref, rel_ref, row_start, seq_len):
    length = row_start + TILE
    wide_len = length + TILE
    offset = seq_len - TILE - row_start
    scale = HEAD_DIM ** (-0.5)
    scores = dot_nt(content, key_ref[0:length, :])
    wide = dot_nt(position, rel_ref[offset : offset + wide_len, :])
    halves = []
    for head in range(2):
        part = wide[head * TILE : (head + 1) * TILE]
        turned = pltpu.roll(part, wide_len - (TILE - 1), 1, stride=1, stride_axis=0)
        halves.append(turned[:, :length])
    scores = (scores + jnp.concatenate(halves, axis=0)) * scale
    row = lax.broadcasted_iota(jnp.int32, scores.shape, 0) % TILE + row_start
    col = lax.broadcasted_iota(jnp.int32, scores.shape, 1)
    scores = jnp.where(col <= row, scores, neg_big)
    top = jnp.max(scores, axis=1, keepdims=True)
    raised = jnp.exp(scores - top)
    total = jnp.sum(raised, axis=1, keepdims=True)
    return raised * (1.0 / total)


def attend_forward_kernel(seq_len, block, order_ref, qkv_ref, rel_ref, bias_ref, out_ref, qkv, out):
    copy_blocks(order_ref, qkv_ref, qkv, block, True)
    keys = qkv.at[:, 128:256]
    values = qkv.at[:, 256:384]
    content_bias = bias_ref[0:1, :]
    position_bias = bias_ref[1:2, :]
    for tile in range(seq_len // TILE):
        start = tile * TILE
        query = qkv[start : start + TILE, 0:128].astype(f32)
        content = stack_heads((query + content_bias).astype(bf16))
        position = stack_heads((query + position_bias).astype(bf16))
        shares = attention_shares(content, position, keys, rel_ref, start, seq_len)
        got = dot_nn(shares.astype(bf16), values[0 : start + TILE, :])
        out[start : start + TILE, :] = join_heads(got).astype(bf16)
    copy_blocks(order_ref, out, out_ref, block, False)


def attend_backward_kernel(
    seq_len,
    block,
    order_ref,
    qkv_ref,
    rel_ref,
    bias_ref,
    grad_ref,
    dqkv_ref,
    drel_ref,
    dbias_ref,
    qkv,
    grad,
    dqkv,
    dkey,
    dvalue,
    drel,
):
    scale = HEAD_DIM ** (-0.5)
    copy_blocks(order_ref, qkv_ref, qkv, block, True)
    copy_blocks(order_ref, grad_ref, grad, block, True)
    keys = qkv.at[:, 128:256]
    values = qkv.at[:, 256:384]
    content_bias = bias_ref[0:1, :]
    position_bias = bias_ref[1:2, :]
    dkey[...] = jnp.zeros_like(dkey)
    dvalue[...] = jnp.zeros_like(dvalue)
    drel[...] = jnp.zeros_like(drel)
    row = lax.broadcasted_iota(jnp.int32, (TILE, TILE), 0)
    col = lax.broadcasted_iota(jnp.int32, (TILE, TILE), 1)
    flip = jnp.where(row + col == TILE - 1, 1.0, 0.0).astype(bf16)
    content_sum = jnp.zeros((1, 128), f32)
    position_sum = jnp.zeros((1, 128), f32)
    for tile in range(seq_len // TILE):
        start = tile * TILE
        length = start + TILE
        wide_len = length + TILE
        offset = seq_len - TILE - start
        query = qkv[start : start + TILE, 0:128].astype(f32)
        content = stack_heads((query + content_bias).astype(bf16))
        plain = (query + position_bias).astype(bf16)
        position = stack_heads(plain)
        shares = attention_shares(content, position, keys, rel_ref, start, seq_len)
        out_grad = stack_heads(grad[start : start + TILE, :])
        share_grad = dot_nt(out_grad, values[0:length, :])
        delta = jnp.sum(shares * share_grad, axis=1, keepdims=True)
        score_grad = (shares * (share_grad - delta)).astype(bf16)
        content_grad = join_heads(dot_nn(score_grad, keys[0:length, :])) * scale
        parts = []
        for head in range(2):
            turned = dot_nn(flip, score_grad[head * TILE : (head + 1) * TILE])
            turned = jnp.concatenate([turned, jnp.zeros((TILE, TILE), f32)], axis=1)
            parts.append(pltpu.roll(turned, 0, 1, stride=1, stride_axis=0))
        wide_grad = jnp.concatenate(parts, axis=0).astype(bf16)
        relative = rel_ref[offset : offset + wide_len, :]
        turned_grad = join_heads(dot_nn(wide_grad, relative)) * scale
        turned_rows = stack_heads(dot_nn(flip, plain).astype(bf16))
        drel[offset : offset + wide_len, :] += dot_tn(wide_grad, turned_rows)
        high = turned_grad.astype(bf16)
        low = (turned_grad - high.astype(f32)).astype(bf16)
        position_grad = dot_nn(flip, high) + dot_nn(flip, low)
        content_sum += jnp.sum(content_grad, axis=0, keepdims=True)
        position_sum += jnp.sum(turned_grad, axis=0, keepdims=True)
        dqkv[start : start + TILE, 0:128] = (content_grad + position_grad).astype(bf16)
        dkey[0:length, :] += dot_tn(score_grad, content)
        dvalue[0:length, :] += dot_tn(shares.astype(bf16), out_grad)
    dqkv[:, 128:256] = (dkey[...] * scale).astype(bf16)
    dqkv[:, 256:384] = dvalue[...].astype(bf16)
    copy_blocks(order_ref, dqkv, dqkv_ref, block, False)
    drel_ref[...] = drel[0:seq_len, :] * scale
    dbias_ref[...] = jnp.concatenate(
        [content_sum, position_sum, jnp.zeros((6, 128), f32)], axis=0
    )


in_vmem = pl.BlockSpec(memory_space=pltpu.VMEM)
in_smem = pl.BlockSpec(memory_space=pltpu.SMEM)


def attend_forward(order, qkv, rel, bias, block):
    rows = qkv.shape[0]
    return pl.pallas_call(
        functools.partial(attend_forward_kernel, rows, block),
        out_shape=jax.ShapeDtypeStruct((rows, 128), bf16),
        in_specs=[in_smem, in_vmem, in_vmem, in_vmem],
        out_specs=in_vmem,
        scratch_shapes=[pltpu.VMEM((rows, 384), bf16), pltpu.VMEM((rows, 128), bf16)],
        compiler_params=pltpu.CompilerParams(vmem_limit_bytes=40 * 2**20),
        cost_estimate=pl.CostEstimate(
            flops=4 * 256 * rows * rows * 2, bytes_accessed=rows * 1300, transcendentals=rows * rows
        ),
        name="attend_forward",
    )(order, qkv, rel, bias)


def attend_backward(order, qkv, rel, bias, grad, block):
    rows = qkv.shape[0]
    return pl.pallas_call(
        functools.partial(attend_backward_kernel, rows, block),
        out_shape=[
            jax.ShapeDtypeStruct((rows, 384), bf16),
            jax.ShapeDtypeStruct((rows, 128), f32),
            jax.ShapeDtypeStruct((8, 128), f32),
        ],
        in_specs=[in_smem, in_vmem, in_vmem, in_vmem, in_vmem],
        out_specs=[in_vmem, in_vmem, in_vmem],
        scratch_shapes=[
            pltpu.VMEM((rows, 384), bf16),
            pltpu.VMEM((rows, 128), bf16),
            pltpu.VMEM((rows, 384), bf16),
            pltpu.VMEM((rows, 128), f32),
            pltpu.VMEM((rows, 128), f32),
            pltpu.VMEM((rows + TILE, 128), f32),
        ],
        compiler_params=pltpu.CompilerParams(vmem_limit_bytes=40 * 2**20),
        cost_estimate=pl.CostEstimate(
            flops=10 * 256 * rows * rows * 2, bytes_accessed=rows * 3000, transcendentals=rows * rows
        ),
        name="attend_backward",
    )(order, qkv, rel, bias, grad)


def head_mask(shape, head):
    lane = lax.broadcasted_iota(jnp.int32, shape, 1)
    return (lane >= head * HEAD_DIM) & (lane < (head + 1) * HEAD_DIM)


def stack_all(rows):
    zero = jnp.zeros_like(rows)
    heads = rows.shape[1] // HEAD_DIM
    return jnp.concatenate(
        [jnp.where(head_mask(rows.shape, head), rows, zero) for head in range(heads)], axis=0
    )


def join_all(stacked):
    heads = stacked.shape[1] // HEAD_DIM
    rows = stacked.shape[0] // heads
    out = jnp.zeros((rows, stacked.shape[1]), stacked.dtype)
    for head in range(heads):
        part = stacked[head * rows : (head + 1) * rows]
        out = jnp.where(head_mask(part.shape, head), part, out)
    return out


def cross_shares(query, keys):
    scores = dot_nt(query, keys) * (HEAD_DIM ** (-0.5))
    raised = jnp.exp(scores - jnp.max(scores, axis=1, keepdims=True))
    return raised / jnp.sum(raised, axis=1, keepdims=True)


def cross_forward_kernel(q_ref, kv_ref, out_ref):
    width = q_ref.shape[1]
    shares = cross_shares(stack_all(q_ref[...]), kv_ref[:, 0:width])
    out_ref[...] = join_all(dot_nn(shares.astype(bf16), kv_ref[:, width:])).astype(bf16)


def cross_backward_kernel(q_ref, kv_ref, grad_ref, dq_ref, dkv_ref):
    width = q_ref.shape[1]
    scale = HEAD_DIM ** (-0.5)
    keys = kv_ref[:, 0:width]
    query = stack_all(q_ref[...])
    grad = stack_all(grad_ref[...])
    shares = cross_shares(query, keys)
    share_grad = dot_nt(grad, kv_ref[:, width:])
    delta = jnp.sum(shares * share_grad, axis=1, keepdims=True)
    score_grad = (shares * (share_grad - delta)).astype(bf16)
    dq_ref[...] = (join_all(dot_nn(score_grad, keys)) * scale).astype(bf16)
    dkv_ref[:, 0:width] = (dot_tn(score_grad, query) * scale).astype(bf16)
    dkv_ref[:, width:] = dot_tn(shares.astype(bf16), grad).astype(bf16)


def cross_forward(query, pair):
    width = query.shape[1]
    groups = query.shape[0] // GROUP
    return pl.pallas_call(
        cross_forward_kernel,
        out_shape=jax.ShapeDtypeStruct(query.shape, bf16),
        grid=(groups,),
        in_specs=[
            pl.BlockSpec((GROUP, width), lambda g: (g, 0)),
            pl.BlockSpec((NK, 2 * width), lambda g: (g, 0)),
        ],
        out_specs=pl.BlockSpec((GROUP, width), lambda g: (g, 0)),
        cost_estimate=pl.CostEstimate(
            flops=groups * 4 * 256 * 256 * 256, bytes_accessed=groups * 330000, transcendentals=groups * 65536
        ),
        name="cross_forward",
    )(query, pair)


def cross_backward(query, pair, grad):
    width = query.shape[1]
    groups = query.shape[0] // GROUP
    return pl.pallas_call(
        cross_backward_kernel,
        out_shape=[
            jax.ShapeDtypeStruct(query.shape, bf16),
            jax.ShapeDtypeStruct(pair.shape, bf16),
        ],
        grid=(groups,),
        in_specs=[
            pl.BlockSpec((GROUP, width), lambda g: (g, 0)),
            pl.BlockSpec((NK, 2 * width), lambda g: (g, 0)),
            pl.BlockSpec((GROUP, width), lambda g: (g, 0)),
        ],
        out_specs=[
            pl.BlockSpec((GROUP, width), lambda g: (g, 0)),
            pl.BlockSpec((NK, 2 * width), lambda g: (g, 0)),
        ],
        cost_estimate=pl.CostEstimate(
            flops=groups * 10 * 256 * 256 * 256, bytes_accessed=groups * 660000, transcendentals=groups * 65536
        ),
        name="cross_backward",
    )(query, pair, grad)


def skew(wide, count):
    lead = wide.shape[:-2]
    rows, span = wide.shape[-2:]
    edge = [(0, 0)] * len(lead)
    padded = jnp.pad(wide, edge + [(0, 0), (0, 1)])
    flat = padded.reshape(lead + (rows * (span + 1),))
    flat = lax.slice_in_dim(flat, rows - 1, rows - 1 + rows * span, axis=len(lead))
    return flat.reshape(lead + (rows, span))[..., :count]


def unskew(grad, span):
    lead = grad.shape[:-2]
    rows, count = grad.shape[-2:]
    edge = [(0, 0)] * len(lead)
    wide = jnp.pad(grad, edge + [(0, 0), (0, span - count)])
    flat = jnp.pad(wide.reshape(lead + (rows * span,)), edge + [(rows - 1, 1)])
    return flat.reshape(lead + (rows, span + 1))[..., :span]


def tile_scores(content_rows, position_rows, key_rows, relative, row_start, key_start):
    rows = content_rows.shape[0]
    count = key_rows.shape[0]
    scale = content_rows.shape[-1] ** (-0.5)
    content = jnp.einsum("qhe,khe->hqk", content_rows, key_rows, preferred_element_type=f32)
    wide = jnp.einsum("qhe,whe->hqw", position_rows, relative, preferred_element_type=f32)
    scores = (content + skew(wide, count)) * scale
    causal = (row_start + jnp.arange(rows))[:, None] >= (key_start + jnp.arange(count))[None, :]
    return (scores, causal[None])


def tile_forward(
    content_rows, position_rows, row_start, relative, key_rows, value_rows, key_start, state
):
    top, total, accum = state
    scores, causal = tile_scores(
        content_rows, position_rows, key_rows, relative, row_start, key_start
    )
    scores = jnp.where(causal, scores, neg_big)
    new_top = jnp.maximum(top, jnp.max(scores, axis=-1))
    raised = jnp.where(causal, jnp.exp(scores - new_top[..., None]), 0.0)
    fade = jnp.exp(top - new_top)
    total = total * fade + jnp.sum(raised, axis=-1)
    accum = accum * fade[..., None] + jnp.einsum(
        "hqk,khe->hqe", raised.astype(bf16), value_rows, preferred_element_type=f32
    )
    return (new_top, total, accum)


def tile_backward(
    content_rows,
    position_rows,
    row_start,
    relative,
    key_rows,
    value_rows,
    grad_rows,
    log_rows,
    delta_rows,
    key_start,
):
    scores, causal = tile_scores(
        content_rows, position_rows, key_rows, relative, row_start, key_start
    )
    scale = content_rows.shape[-1] ** (-0.5)
    shares = jnp.where(causal, jnp.exp(scores - log_rows[..., None]), 0.0)
    share_grad = jnp.einsum("qhe,khe->hqk", grad_rows, value_rows, preferred_element_type=f32)
    score_grad = (shares * (share_grad - delta_rows[..., None])).astype(bf16)
    content_grad = jnp.einsum("hqk,khe->qhe", score_grad, key_rows, preferred_element_type=f32)
    wide_grad = unskew(score_grad, relative.shape[0])
    position_grad = jnp.einsum("hqw,whe->qhe", wide_grad, relative, preferred_element_type=f32)
    table_part = jnp.einsum("hqw,qhe->whe", wide_grad, position_rows, preferred_element_type=f32)
    key_grad = jnp.einsum("hqk,qhe->khe", score_grad, content_rows, preferred_element_type=f32)
    value_grad = jnp.einsum(
        "hqk,qhe->khe", shares.astype(bf16), grad_rows, preferred_element_type=f32
    )
    return (
        content_grad * scale,
        position_grad * scale,
        table_part * scale,
        key_grad * scale,
        value_grad,
    )


def nest_tiles(tile_fn):
    inner = jax.vmap(tile_fn, in_axes=(0, 0, 0, 0, None, None, 0))
    return jax.vmap(inner, in_axes=(0, 0, None, None, 0, 0, 0))


def to_global(stored, inverse, block):
    seqs, seq_len, width = stored.shape
    blocks = stored.reshape(seqs, seq_len // block, block * width)
    chosen = (inverse[:, None] == jnp.arange(seq_len // block)[None, :]).astype(bf16)
    moved = jnp.einsum("gs,nsx->ngx", chosen, blocks, preferred_element_type=f32)
    return moved.astype(bf16).reshape(stored.shape)


class SplitQueries:

    def __init__(self, query, keys, values, biases, relative, block_order, inverse, block):
        self.seqs, self.tok_dev, self.width = keys.shape
        self.heads = self.width // HEAD_DIM
        self.block = block
        self.block_order = block_order
        ctx_count = lax.axis_size("ctx")
        self.seq_len = self.tok_dev * ctx_count
        self.key_len = min(512, self.seq_len)
        pad = jnp.zeros((self.key_len + block, self.width), bf16)
        table = jnp.concatenate([relative, pad], axis=0)
        self.table = table.reshape(-1, self.heads, HEAD_DIM)
        lead = (self.seqs, 2, block, self.heads, HEAD_DIM)
        self.content = (query + biases[0]).astype(bf16).reshape(lead)
        self.position = (query + biases[1]).astype(bf16).reshape(lead)
        gathered = [lax.all_gather(part, "ctx", axis=1, tiled=True) for part in (keys, values)]
        shape = (self.seqs, self.seq_len, self.heads, HEAD_DIM)
        self.keys, self.values = [to_global(part, inverse, block).reshape(shape) for part in gathered]
        self.starts = lax.dynamic_slice_in_dim(block_order, 2 * lax.axis_index("ctx"), 2, 0) * block

    def rows(self, index):
        start = index * self.key_len
        keys = lax.dynamic_slice_in_dim(self.keys, start, self.key_len, 1)
        values = lax.dynamic_slice_in_dim(self.values, start, self.key_len, 1)
        span = self.block + self.key_len
        offsets = [self.seq_len - self.block - self.starts[slot] + start for slot in range(2)]
        relative = [lax.dynamic_slice_in_dim(self.table, offset, span, 0) for offset in offsets]
        return start, keys, values, jnp.stack(relative), offsets

    def to_stored(self, part):
        count = self.seq_len // self.block
        blocks = part.reshape(self.seqs, count, self.block * self.width)
        chosen = (self.block_order[:, None] == jnp.arange(count)[None, :]).astype(f32)
        moved = jnp.einsum("sg,ngx->nsx", chosen, blocks, precision=highest)
        return moved.reshape(self.seqs, self.seq_len, self.width)

    def forward(self):
        def step(state, index):
            start, keys, values, relative, _ = self.rows(index)

            def tile(content, position, row_start, table, keys_seq, values_seq, tile_state):
                return tile_forward(
                    content, position, row_start, table, keys_seq, values_seq, start, tile_state
                )

            return nest_tiles(tile)(
                self.content, self.position, self.starts, relative, keys, values, state
            ), None

        shape = (self.seqs, 2, self.heads, self.block)
        state = (
            jnp.full(shape, neg_big, f32),
            jnp.zeros(shape, f32),
            jnp.zeros(shape + (HEAD_DIM,), f32),
        )
        (top, total, accum), _ = lax.scan(step, state, jnp.arange(self.seq_len // self.key_len))
        self.log_total = top + jnp.log(total)
        self.out = accum / total[..., None]
        moved = jnp.transpose(self.out, (0, 1, 3, 2, 4))
        return moved.reshape(self.seqs * self.tok_dev, self.width).astype(bf16)

    def backward(self, grad):
        block, seq_len, key_len = self.block, self.seq_len, self.key_len
        lead = (self.seqs, 2, block, self.heads, HEAD_DIM)
        grad = grad.reshape(lead)
        delta = jnp.einsum("sbqhe,sbhqe->sbhq", grad.astype(f32), self.out)
        def step(carry, index):
            start, keys, values, relative, offsets = self.rows(index)

            def tile(content, position, row_start, table, keys_seq, values_seq, extra):
                return tile_backward(
                    content, position, row_start, table, keys_seq, values_seq, *extra, start
                )

            extra = (grad, self.log_total, delta)
            parts = nest_tiles(tile)(
                self.content, self.position, self.starts, relative, keys, values, extra
            )
            table = carry[2]
            table_sum = jnp.sum(parts[2], axis=0)
            for slot in range(2):
                offset = offsets[slot]
                current = lax.dynamic_slice_in_dim(table, offset, block + key_len, 0)
                table = lax.dynamic_update_slice_in_dim(table, current + table_sum[slot], offset, 0)
            sums = []
            for total, part in zip(carry[3:], parts[3:]):
                current = lax.dynamic_slice_in_dim(total, start, key_len, 1)
                part = current + jnp.sum(part, axis=1)
                sums.append(lax.dynamic_update_slice_in_dim(total, part, start, 1))
            key_acc, value_acc = sums
            return (carry[0] + parts[0], carry[1] + parts[1], table, key_acc, value_acc), None

        zero_tiles = jnp.zeros(lead, f32)
        zero_keys = jnp.zeros((self.seqs, seq_len, self.heads, HEAD_DIM), f32)
        carry = (zero_tiles, zero_tiles, jnp.zeros(self.table.shape, f32), zero_keys, zero_keys)
        carry, _ = lax.scan(step, carry, jnp.arange(seq_len // key_len))
        owned = [
            lax.psum_scatter(
                self.to_stored(part), "ctx", scatter_dimension=1, tiled=True
            )
            for part in carry[3:]
        ]
        flat = (self.seqs * self.tok_dev, self.width)
        query_grad = (carry[0] + carry[1]).reshape(flat).astype(bf16)
        key_grad, value_grad = [part.reshape(flat).astype(bf16) for part in owned]
        bias_grads = jnp.stack(
            [jnp.sum(part, axis=(0, 1, 2)).reshape(self.width) for part in carry[:2]]
        )
        table_grad = carry[2].reshape(-1, self.width)[:seq_len]
        return query_grad, key_grad, value_grad, bias_grads, table_grad


def local(
    tokens,
    neighbours,
    teacher,
    valid_mask,
    block_order,
    query_weight,
    key_weight,
    value_weight,
    output_weight,
    relative_weight,
    content_bias,
    position_bias,
    cross_query_weight,
    cross_key_weight,
    cross_value_weight,
    cross_output_weight,
    up_weight,
    down_weight,
    attention_gain,
    cross_gain,
    feedforward_gain,
):
    places = lax.axis_size("wa")
    ctx_count = lax.axis_size("ctx")
    place = lax.axis_index("wa")
    here = lax.axis_index("ctx")
    _, tok_dev, width = tokens.shape
    seq_len = tok_dev * ctx_count
    block = tok_dev // 2
    cols = HEADS * HEAD_DIM // places
    rows = places * tok_dev
    pairs = cols // 128
    by_heads = places * pairs == ctx_count and seq_len % TILE == 0

    token_parts = gather_parts(tokens[0])
    query_cols, key_cols, value_cols = [
        take_columns(weight) for weight in (query_weight, key_weight, value_weight)
    ]
    relative_cols = take_columns(relative_weight)
    gains = lax.all_gather(
        jnp.stack([attention_gain, cross_gain, feedforward_gain]), "wa", axis=1, tiled=True
    ).astype(f32)
    gain_one, gain_two, gain_three = gains[0:1], gains[1:2], gains[2:3]
    cross_query_cols, cross_key_cols, cross_value_cols = [
        take_columns(weight) for weight in (cross_query_weight, cross_key_weight, cross_value_weight)
    ]
    cross_pair_cols = jnp.concatenate([cross_key_cols, cross_value_cols], axis=1)
    near_rows = jnp.concatenate(gather_parts(neighbours.reshape(-1, width)), axis=0)
    up_cols = take_columns(up_weight)
    valid = valid_mask.astype(f32).reshape(tok_dev, 1)
    count = jnp.sum(valid).reshape(1, 1)
    count = all_summed(all_summed(count, "wa"), "ctx")

    slots = jnp.arange(2 * ctx_count)
    inverse = jnp.sum(jnp.where(block_order[None, :] == slots[:, None], slots[None, :], 0), axis=1)
    inverse = inverse.astype(jnp.int32)
    distance = (seq_len - 1 - jnp.arange(seq_len)).astype(f32)
    waves = sinusoid(distance, width).astype(bf16)

    hidden_all = jnp.concatenate(token_parts, axis=0).astype(f32)
    scale_all = inverse_rms(hidden_all)
    normed_a = (hidden_all * scale_all * gain_one).astype(bf16)
    biases = jnp.stack([content_bias, position_bias]).astype(f32)
    if by_heads:
        which = here % pairs
        mixed_cols = jnp.concatenate(
            [
                part[:, 128 * pair : 128 * (pair + 1)]
                for pair in range(pairs)
                for part in (query_cols, key_cols, value_cols)
            ],
            axis=1,
        )
        qkv = dot_nn(normed_a, mixed_cols).astype(bf16)
        qkv = qkv.reshape(places, tok_dev, pairs, 384).transpose(0, 2, 1, 3)
        qkv = qkv.reshape(ctx_count, tok_dev, 384)
        qkv = lax.all_to_all(qkv, "ctx", split_axis=0, concat_axis=0, tiled=True)
        qkv = qkv.reshape(seq_len, 384)
        my_relative = lax.dynamic_slice_in_dim(relative_cols, which * 128, 128, 1)
        table = dot_nn(waves, my_relative).astype(bf16)
        table = jnp.concatenate([table, jnp.zeros((TILE, 128), bf16)], axis=0)
        my_biases = lax.dynamic_slice_in_dim(biases, which * 128, 128, 1)
        my_biases = jnp.concatenate([my_biases, jnp.zeros((6, 128), f32)], axis=0)
        out = attend_forward(inverse, qkv, table, my_biases, block)
        out = lax.all_to_all(
            out.reshape(ctx_count, tok_dev, 128), "ctx", split_axis=0, concat_axis=0, tiled=True
        )
        out = out.reshape(places, pairs, tok_dev, 128).transpose(0, 2, 1, 3)
        attended = out.reshape(rows, cols)
    else:
        mixed_cols = jnp.concatenate([query_cols, key_cols, value_cols], axis=1)
        qkv = dot_nn(normed_a, mixed_cols).reshape(places, tok_dev, 3 * cols)
        relative = dot_nn(waves, relative_cols).astype(bf16)
        general = SplitQueries(
            qkv[..., :cols],
            qkv[..., cols : 2 * cols].astype(bf16),
            qkv[..., 2 * cols :].astype(bf16),
            biases,
            relative,
            block_order,
            inverse,
            block,
        )
        attended = general.forward()

    def to_owner(product):
        return scatter_parts([product[r * tok_dev : (r + 1) * tok_dev] for r in range(places)])

    def from_all(value):
        return jnp.concatenate(gather_parts(value), axis=0)

    hidden_in = tokens[0].astype(f32)
    hidden_one = hidden_in + to_owner(dot_nn(attended, output_weight))

    scale_two = inverse_rms(hidden_one)
    normed_b = from_all((hidden_one * scale_two * gain_two).astype(bf16))
    cross_q = dot_nn(normed_b, cross_query_cols).astype(bf16)
    cross_pair = dot_nn(near_rows, cross_pair_cols).astype(bf16)
    crossed = cross_forward(cross_q, cross_pair)
    hidden_two = hidden_one + to_owner(dot_nn(crossed, cross_output_weight))

    scale_three = inverse_rms(hidden_two)
    normed_c = from_all((hidden_two * scale_three * gain_three).astype(bf16))
    pre_act = dot_nn(normed_c, up_cols)
    activated = gelu_tanh(pre_act).astype(bf16)
    layer_out = hidden_two + to_owner(dot_nn(activated, down_weight))

    error = layer_out - teacher[0].astype(f32)
    error_sum = jnp.sum(valid * error * error).reshape(1, 1)
    error_sum = all_summed(all_summed(error_sum, "wa"), "ctx")
    loss = (error_sum / (2.0 * count * width)).reshape(())
    out_grad = (places * seq_len) / count * valid * error

    out_low = from_all(out_grad.astype(bf16))
    act_grad = dot_nt(out_low, down_weight)
    _, gelu_pull = jax.vjp(gelu_tanh, pre_act)
    pre_grad = gelu_pull(act_grad)[0].astype(bf16)
    down_grad = dot_tn(activated, out_low).astype(bf16)
    up_grad = dot_tn(normed_c, pre_grad).astype(bf16)
    normed_c_grad = to_owner(dot_nt(pre_grad, up_cols))
    two_grad = out_grad + norm_pull(hidden_two, scale_three, gain_three, normed_c_grad)
    gain_three_grad = jnp.sum(normed_c_grad * hidden_two * scale_three, axis=0, keepdims=True)
    down_out = sum_row_grads(down_grad)
    up_out = sum_column_grads(up_grad[None])[0]

    two_low = from_all(two_grad.astype(bf16))
    crossed_grad = dot_nt(two_low, cross_output_weight).astype(bf16)
    cross_q_grad, cross_pair_grad = cross_backward(cross_q, cross_pair, crossed_grad)
    normed_b_grad = to_owner(dot_nt(cross_q_grad, cross_query_cols))
    one_grad = two_grad + norm_pull(hidden_one, scale_two, gain_two, normed_b_grad)
    gain_two_grad = jnp.sum(normed_b_grad * hidden_one * scale_two, axis=0, keepdims=True)
    cross_output_grad = dot_tn(crossed, two_low).astype(bf16)
    cross_query_grad = dot_tn(normed_b, cross_q_grad).astype(bf16)
    cross_key_grad = dot_tn(near_rows, cross_pair_grad[:, :cols]).astype(bf16)
    cross_value_grad = dot_tn(near_rows, cross_pair_grad[:, cols:]).astype(bf16)
    cross_output_out = sum_row_grads(cross_output_grad)
    cross_out = sum_column_grads(jnp.stack([cross_key_grad, cross_value_grad]))
    cross_query_out = sum_column_grads(cross_query_grad[None])[0]
    near_grad = dot_nt(cross_pair_grad, cross_pair_cols)
    near_count = near_rows.shape[0] // places
    near_grad = scatter_parts(
        [near_grad[r * near_count : (r + 1) * near_count] for r in range(places)]
    )
    neighbours_grad = near_grad.reshape(neighbours.shape)

    one_low = from_all(one_grad.astype(bf16))
    attended_grad = dot_nt(one_low, output_weight).astype(bf16)
    output_grad = dot_tn(attended, one_low).astype(bf16)
    output_out = sum_row_grads(output_grad)
    if by_heads:
        grad = attended_grad.reshape(places, tok_dev, pairs, 128).transpose(0, 2, 1, 3)
        grad = grad.reshape(ctx_count, tok_dev, 128)
        grad = lax.all_to_all(grad, "ctx", split_axis=0, concat_axis=0, tiled=True)
        grad = grad.reshape(seq_len, 128)
        qkv_grad, table_grad, bias_part = attend_backward(
            inverse, qkv, table, my_biases, grad, block
        )
        qkv_grad = lax.all_to_all(
            qkv_grad.reshape(ctx_count, tok_dev, 384), "ctx", split_axis=0, concat_axis=0, tiled=True
        )
        qkv_grad = qkv_grad.reshape(places, pairs, tok_dev, 384).transpose(0, 2, 1, 3)
        qkv_grad = qkv_grad.reshape(rows, 3 * cols)
        bias_grads = jnp.concatenate(
            [jnp.where(which == pair, bias_part[0:2], 0.0) for pair in range(pairs)], axis=1
        )
    else:
        query_grad, key_grad, value_grad, bias_grads, table_grad = general.backward(attended_grad)
        qkv_grad = jnp.concatenate([query_grad, key_grad, value_grad], axis=1)
    table_high = table_grad.astype(bf16)
    table_low = (table_grad - table_high.astype(f32)).astype(bf16)
    relative_grad = (dot_tn(waves, table_high) + dot_tn(waves, table_low)).astype(bf16)
    mixed_grad = dot_tn(normed_a, qkv_grad).astype(bf16)
    if by_heads:
        relative_grad = jnp.concatenate(
            [jnp.where(which == pair, relative_grad, 0.0) for pair in range(pairs)], axis=1
        )
        whole = [
            jnp.concatenate(
                [
                    mixed_grad[:, 384 * pair + 128 * m : 384 * pair + 128 * (m + 1)]
                    for pair in range(pairs)
                ],
                axis=1,
            )
            for m in range(3)
        ]
    else:
        whole = [mixed_grad[:, m * cols : (m + 1) * cols] for m in range(3)]
    attention_out = sum_column_grads(jnp.stack(whole + [relative_grad]))
    normed_a_part = dot_nt(qkv_grad, mixed_cols)
    gain_one_part = jnp.sum(normed_a_part * hidden_all * scale_all, axis=0, keepdims=True)
    normed_a_grad = to_owner(normed_a_part)
    tokens_grad = one_grad + norm_pull(hidden_in, scale_all[:tok_dev], gain_one, normed_a_grad)

    gain_grads = jnp.concatenate([gain_one_part, gain_two_grad, gain_three_grad], axis=0)
    gain_grads = all_summed(gain_grads, "wa")
    share = width // places
    gain_grads = lax.dynamic_slice_in_dim(gain_grads, place * share, share, 1)
    small = jnp.concatenate([gain_grads.reshape(1, -1), bias_grads.reshape(1, -1)], axis=1)
    small = all_summed(small, "ctx")[0]
    gain_out = small[: 3 * share].reshape(3, share)
    bias_out = small[3 * share :].reshape(2, cols)

    return (
        layer_out[None],
        loss,
        tokens_grad[None],
        neighbours_grad,
        attention_out[0],
        attention_out[1],
        attention_out[2],
        output_out,
        attention_out[3],
        bias_out[0],
        bias_out[1],
        cross_query_out,
        cross_out[0],
        cross_out[1],
        cross_output_out,
        up_out,
        down_out,
        gain_out[0],
        gain_out[1],
        gain_out[2],
    )


def solution(mesh):
    row = P("wa", None)
    flat = P("wa")
    in_specs = (
        P("wa", "ctx", None),
        P("wa", "ctx", None, None),
        P("wa", "ctx", None),
        P("wa", "ctx"),
        P(),
        row,
        row,
        row,
        row,
        row,
        flat,
        flat,
        row,
        row,
        row,
        row,
        row,
        row,
        flat,
        flat,
        flat,
    )
    out_specs = (
        P("wa", "ctx", None),
        P(),
        P("wa", "ctx", None),
        P("wa", "ctx", None, None),
        row,
        row,
        row,
        row,
        row,
        flat,
        flat,
        row,
        row,
        row,
        row,
        row,
        row,
        flat,
        flat,
        flat,
    )
    return jax.shard_map(local, mesh=mesh, in_specs=in_specs, out_specs=out_specs, check_vma=False)
```

time: 2150 us -> 617 us (0.29)
  blocking collectives: 646 us -> 14.9 us
  waiting for transfers between devices: 798 us -> 244 us
  local copies, waits for them, and re-layouts: 411 us -> 39.9 us
  starting transfers between devices: 1.29 us -> 145 us
  matrix products: 165 us -> 55.5 us
  Pallas kernels: 0 us -> 37.5 us
  other arithmetic: 98.2 us -> 65.3 us
    psum x2 -> x0, blocking collectives: 616 us -> none  [the longest x1 577 us: local(): lax.psum((owned[0], owned[1], owned[2], owned[3], owned[4], owned[5], own...]
    reduce_scatter x11 -> x0, waiting for transfers between devices: 461 us -> none  [the longest x1 83.9 us: local(): lax.psum_scatter(carried[3].reshape(seqs_dev, seq_len, attn_width), 'ctx'...]
    ppermute x0 -> x123, waiting for transfers between devices: none -> 237 us  [swap(): return lax.ppermute(value, axis, pairs)]
    unnamed x30 -> x0, waiting for transfers between devices: 181 us -> none
    all_gather x13 -> x0, waiting for transfers between devices: 156 us -> none  [the longest x1 46.8 us: local(): lax.all_gather(key_local, 'ctx', axis=1, tiled=True)]
    ppermute x0 -> x123, starting transfers between devices: none -> 125 us  [swap(): return lax.ppermute(value, axis, pairs)]
    dot_general x53 -> x25, matrix products: 145 us -> 55.5 us  [the longest x7 19.5 us: dot_nt(): lax.dot_general(a, b, (((1,), (1,)), ((), ())), preferred_element_type=f32)]
    reshape x17 -> x3, local copies, waits for them, and re-layouts: 91.7 us -> 3.15 us  [the longest x1 2.05 us: local(): qkv = qkv.reshape(places, tok_dev, pairs, 384).transpose(0, 2, 1, 3)]
  transfers between devices with their start and end apart: 27 -> 127, of which waited for: 22 -> 58; matrix products, arithmetic and copies ran while one was open for 14% -> 24% of each run, Pallas kernels for 0% -> 6%
where the time goes in v1:
time: 617 us; the launch traced here: 615 us
  waiting for transfers between devices  244 us (40%)
  starting transfers between devices  145 us (24%)
  other arithmetic  65.3 us (11%)
  matrix products  55.5 us (9%)
  local copies, waits for them, and re-layouts  39.9 us (6%)
  Pallas kernels  37.5 us (6%)
  blocking collectives  14.9 us (2%)
  between operations  12.5 us (2%)
    ppermute x123, waiting for transfers between devices, swap(): return lax.ppermute(value, axis, pairs)  237 us
    ppermute x123, starting transfers between devices, swap(): return lax.ppermute(value, axis, pairs)  125 us
    dot_general x7, matrix products, dot_nt(): lax.dot_general(a, b, (((1,), (1,)), ((), ())), preferred_element_type=f32)  19.5 us
    select_n x47, other arithmetic, ordered(): jnp.where(bit == 0, jnp.concatenate([own, other], axis=dim), jnp.concaten...  19 us
    dot_general x10, matrix products, dot_tn(): lax.dot_general(a, b, (((0,), (0,)), ((), ())), preferred_element_type=f32)  18.5 us
    dot_general x8, matrix products, dot_nn(): lax.dot_general(a, b, (((1,), (0,)), ((), ())), preferred_element_type=f32)  17.5 us
    all_gather x1, blocking collectives, local(): lax.all_gather(jnp.stack([attention_gain, cross_gain, feedforward_gain]),...  14.9 us
    pallas_call x1, Pallas kernels, attend_backward(): pl.pallas_call(functools.partial(attend_backward_kernel, rows, block), ou...  14.1 us
  transfers between devices with their start and end apart: 127, of which 58 were waited for; matrix products, arithmetic and copies ran while one was open for 24% of the time, Pallas kernels for 6%

profile of v1, /device:TPU:0, one launch (start us, length us, event | category | flops | bytes accessed | tf_op | source)
XLA Modules:
  0.0 615.1 jit_solution(17517240807161708531)
XLA Ops:
  10.4 14.9 %all-gather = bf16[4,224,3]{1,2,0:T(4,128)(2,1)S(1)} all-gather(bf16[1,224,3]{1,2,0:T(4,128)(2,1)S(1)} %maximum_bitcast_fusion), channel_id=1, replica_groups=mesh['ctx'=8,'wa'=4] {'wa'}, dimensions={0}, use_global_device_ids=true | all-gather | bytes 6720 | tf_op jit(solution)/shard_map/all_gather | solution.py:699
  29.3 4.7 collective-permute-done.9
  47.7 6.4 %all-to-all-start = ((bf16[8,128,384]{2,1,0:T(8,128)(2,1)}), bf16[8,128,384]{2,1,0:T(8,128)(2,1)S(1)}, u32[]{:S(2)}, u32[]{:S(2)}) async-start(bf16[8,128,384]{2,1,0:T(8,128)(2,1)} %bitcast.308), calls=%async_computation | async-start | bytes 1572864 | tf_op jit(solution)/shard_map/all_to_all | solution.py:736
  62.1 8.2 %fusion = (bf16[1024,448]{1,0:T(8,128)(2,1)S(1)}, bf16[1024,448]{1,0:T(8,128)(2,1)S(1)}) fusion(f32[448]{0:T(512)S(1)} %multiply_exponential_fusion, f32[1024]{0:T(1024)S(1)} %subtract_convert_fusion.2), kind=kLoop, calls=%fused_computation.9 | loop fusion | flops 1376256 | bytes 1840896 | tf_op jit(solution)/shard_map/convert.18
  74.8 6.8 %attend_forward.1 = bf16[1024,128]{1,0:T(8,128)(2,1)} custom-call(s32[16]{0:T(128)S(1)} %select_reduce_fusion.order_ref, bf16[1024,384]{1,0:T(8,128)(2,1)S(1)} %bitcast.295, bf16[1152,128]{1,0:T(8,128)(2,1)S(1)} %concatenate.1117.rel_ref, f32[8,128]{1,0:T(8,128)S(1)} %concatenate.1118.bias_ref), custom_call_target="tpu_custom_call" | custom-call | flops 2147483648 | bytes 1331200 | tf_op jit(solution)/shard_map/attend_forward/pallas_call | solution.py:313
  103.8 4.6 collective-permute-done.13
  110.3 19.3 %collective-permute-done.15 = bf16[128,896]{1,0:T(8,128)(2,1)S(1)} collective-permute-done((bf16[128,896]{1,0:T(8,128)(2,1)S(1)}, bf16[128,896]{1,0:T(8,128)(2,1)S(1)}, u32[]{:S(2)}, u32[]{:S(2)}) %collective-permute-start.15) | collective-permute-done | bytes 229408 | tf_op jit(solution)/shard_map/ppermute | solution.py:58
  129.6 5.8 convolution_convert_fusion.kv_ref
  137.4 7.8 %cross_forward.1 = bf16[512,256]{1,0:T(8,128)(2,1)} custom-call(bf16[512,256]{1,0:T(8,128)(2,1)} %convolution_convert_fusion.13.q_ref, bf16[2048,512]{1,0:T(8,128)(2,1)} %convolution_convert_fusion.kv_ref), custom_call_target="tpu_custom_call" | custom-call | flops 536870912 | bytes 2640000 | tf_op jit(solution)/shard_map/cross_forward/pallas_call | solution.py:407
  162.2 6.0 collective-permute-done.30
  198.3 5.3 collective-permute-done.48
  232.4 17.3 %collective-permute-start.39 = (f32[1,1]{1,0:T(1,128)}, f32[1,1]{1,0:T(1,128)}, u32[]{:S(2)}, u32[]{:S(2)}) collective-permute-start(f32[1,1]{1,0:T(1,128)} %add.523), channel_id=1, source_target_pairs={{0,4},{4,0},{8,12},{12,8},{16,20},{20,16},{24,28},{28,24},{1,5},{5... | collective-permute-start | bytes 20 | tf_op jit(solution)/shard_map/ppermute | solution.py:58
  255.7 12.3 %collective-permute-start.41 = (f32[1,1]{1,0:T(1,128)}, f32[1,1]{1,0:T(1,128)}, u32[]{:S(2)}, u32[]{:S(2)}) collective-permute-start(f32[1,1]{1,0:T(1,128)} %add.525), channel_id=1, source_target_pairs={{0,16},{4,20},{8,24},{12,28},{16,0},{20,4},{24,8},{28,12},{1,17},{... | collective-permute-start | bytes 20 | tf_op jit(solution)/shard_map/ppermute | solution.py:58
  280.9 8.8 %cross_backward.1 = (bf16[512,256]{1,0:T(8,128)(2,1)}, bf16[2048,512]{1,0:T(8,128)(2,1)}) custom-call(bf16[512,256]{1,0:T(8,128)(2,1)} %convolution_convert_fusion.13.q_ref, bf16[2048,512]{1,0:T(8,128)(2,1)} %convolution_convert_fusion.kv_ref, bf16[512,256]{1,0:T(8,128)(2,1)} %convolution_convert_fusion.12.grad_ref), custom_call_target="tpu_custom_call" | custom-call | flops 1342177280 | bytes 5280000 | tf_op jit(solution)/shard_map/cross_backward/pallas_call | solution.py:426
  296.4 5.4 fusion.108
  324.9 5.2 collective-permute-done.89
  331.5 5.5 collective-permute-done.105
  348.3 15.9 %collective-permute-done.106 = bf16[1,32,896]{2,1,0:T(8,128)(2,1)S(1)} collective-permute-done((bf16[1,32,896]{2,1,0:T(8,128)(2,1)S(1)}, bf16[1,32,896]{2,1,0:T(8,128)(2,1)S(1)}, u32[]{:S(2)}, u32[]{:S(2)}) %collective-permute-start.106) | collective-permute-done | bytes 57376 | tf_op jit(solution)/shard_map/ppermute | solution.py:58
  370.9 5.2 collective-permute-done.107
  377.9 4.8 collective-permute-done.93
  389.5 8.0 %collective-permute-done.120 = bf16[1,112,896]{2,1,0:T(8,128)(2,1)S(1)} collective-permute-done((bf16[1,112,896]{2,1,0:T(8,128)(2,1)S(1)}, bf16[1,112,896]{2,1,0:T(8,128)(2,1)S(1)}, u32[]{:S(2)}, u32[]{:S(2)}) %collective-permute-start.120) | collective-permute-done | bytes 200736 | tf_op jit(solution)/shard_map/ppermute | solution.py:58
  398.4 6.1 collective-permute-done.97
  406.4 5.6 collective-permute-done.94
  413.0 6.0 collective-permute-done.114
  429.3 4.7 all-to-all-start.2
  467.2 14.1 %attend_backward.1 = (bf16[1024,384]{1,0:T(8,128)(2,1)}, f32[1024,128]{1,0:T(8,128)S(1)}, f32[8,128]{1,0:T(8,128)S(1)}) custom-call(s32[16]{0:T(128)S(1)} %select_reduce_fusion.order_ref, bf16[1024,384]{1,0:T(8,128)(2,1)S(1)} %bitcast.296, bf16[1152,128]{1,0:T(8,128)(2,1)S(1)} %concatenate.1117.rel_ref, f32[8,128]{1,0:T(8,128)S(1)} %concatenate.1118.bias_ref, ...), custom_call_target="tpu_custom_call" | custom-call | flops 5368709120 | bytes 3072000 | tf_op jit(solution)/shard_map/attend_backward/pallas_call | solution.py:329
  517.3 12.7 %collective-permute-done.68 = bf16[4,4,112,256]{3,2,1,0:T(8,128)(2,1)S(1)} collective-permute-done((bf16[4,4,112,256]{3,2,1,0:T(8,128)(2,1)S(1)}, bf16[4,4,112,256]{3,2,1,0:T(8,128)(2,1)S(1)}, u32[]{:S(2)}, u32[]{:S(2)}) %collective-permute-start.68) | collective-permute-done | bytes 917536 | tf_op jit(solution)/shard_map/ppermute | solution.py:58
  535.9 7.4 %collective-permute-done.69 = bf16[4,4,56,256]{3,2,1,0:T(8,128)(2,1)S(1)} collective-permute-done((bf16[4,4,56,256]{3,2,1,0:T(8,128)(2,1)S(1)}, bf16[4,4,56,256]{3,2,1,0:T(8,128)(2,1)S(1)}, u32[]{:S(2)}, u32[]{:S(2)}) %collective-permute-start.69) | collective-permute-done | bytes 458784 | tf_op jit(solution)/shard_map/ppermute | solution.py:58
  549.7 6.9 %collective-permute-done.70 = bf16[2,4,56,256]{3,2,1,0:T(8,128)(2,1)S(1)} collective-permute-done((bf16[2,4,56,256]{3,2,1,0:T(8,128)(2,1)S(1)}, bf16[2,4,56,256]{3,2,1,0:T(8,128)(2,1)S(1)}, u32[]{:S(2)}, u32[]{:S(2)}) %collective-permute-start.70) | collective-permute-done | bytes 229408 | tf_op jit(solution)/shard_map/ppermute | solution.py:58
  567.9 8.5 %collective-permute-done.73 = bf16[2,56,1024]{2,1,0:T(8,128)(2,1)S(1)} collective-permute-done((bf16[2,56,1024]{2,1,0:T(8,128)(2,1)S(1)}, bf16[2,56,1024]{2,1,0:T(8,128)(2,1)S(1)}, u32[]{:S(2)}, u32[]{:S(2)}) %collective-permute-start.73) | collective-permute-done | bytes 229408 | tf_op jit(solution)/shard_map/ppermute | solution.py:58
  581.4 7.6 %collective-permute-done.74 = bf16[4,56,1024]{2,1,0:T(8,128)(2,1)S(1)} collective-permute-done((bf16[4,56,1024]{2,1,0:T(8,128)(2,1)S(1)}, bf16[4,56,1024]{2,1,0:T(8,128)(2,1)S(1)}, u32[]{:S(2)}, u32[]{:S(2)}) %collective-permute-start.74) | collective-permute-done | bytes 458784 | tf_op jit(solution)/shard_map/ppermute | solution.py:58
  592.9 17.9 %collective-permute-done.75 = bf16[4,112,1024]{2,1,0:T(8,128)(2,1)S(1)} collective-permute-done((bf16[4,112,1024]{2,1,0:T(8,128)(2,1)S(1)}, bf16[4,112,1024]{2,1,0:T(8,128)(2,1)S(1)}, u32[]{:S(2)}, u32[]{:S(2)}) %collective-permute-start.75) | collective-permute-done | bytes 917536 | tf_op jit(solution)/shard_map/ppermute | solution.py:58
  (638 shorter events, 327.2 us)
Async XLA Ops:
  0.7 35.2 %collective-permute-start.1 = (bf16[128,896]{1,0:T(8,128)(2,1)}, bf16[128,896]{1,0:T(8,128)(2,1)}, u32[]{:S(2)}, u32[]{:S(2)}) collective-permute-start(bf16[128,896]{1,0:T(8,128)(2,1)} %bitcast.300), channel_id=1, source_target_pairs={{0,2},{1,3},{2,0},{3,1},{4,6},{5,7},{6,4},{7,5},{8,10},{9,11},{10,... | collective-permute-start | bytes 688136 | tf_op jit(solution)/shard_map/ppermute | solution.py:58
  3.7 32.8 %collective-permute-start = (bf16[128,896]{1,0:T(8,128)(2,1)}, bf16[128,896]{1,0:T(8,128)(2,1)}, u32[]{:S(2)}, u32[]{:S(2)}) collective-permute-start(bf16[128,896]{1,0:T(8,128)(2,1)} %bitcast.301), channel_id=1, source_target_pairs={{0,1},{1,0},{2,3},{3,2},{4,5},{5,4},{6,7},{7,6},{8,9},{9,8},{10,11... | collective-permute-start | bytes 688136 | tf_op jit(solution)/shard_map/ppermute | solution.py:58
  27.3 75.9 %collective-permute-start.20 = (bf16[512,896]{1,0:T(8,128)(2,1)}, bf16[512,896]{1,0:T(8,128)(2,1)}, u32[]{:S(2)}, u32[]{:S(2)}) collective-permute-start(bf16[512,896]{1,0:T(8,128)(2,1)} %bitcast.45), channel_id=1, source_target_pairs={{0,2},{1,3},{2,0},{3,1},{4,6},{5,7},{6,4},{7,5},{8,10},{9,11},{10,... | collective-permute-start | bytes 2752520 | tf_op jit(solution)/shard_map/ppermute | solution.py:58
  35.3 94.3 %collective-permute-start.19 = (bf16[512,896]{1,0:T(8,128)(2,1)}, bf16[512,896]{1,0:T(8,128)(2,1)}, u32[]{:S(2)}, u32[]{:S(2)}) collective-permute-start(bf16[512,896]{1,0:T(8,128)(2,1)} %bitcast.45), channel_id=1, source_target_pairs={{0,1},{1,0},{2,3},{3,2},{4,5},{5,4},{6,7},{7,6},{8,9},{9,8},{10,11... | collective-permute-start | bytes 2752520 | tf_op jit(solution)/shard_map/ppermute | solution.py:58
  47.7 27.1 %all-to-all-start = ((bf16[8,128,384]{2,1,0:T(8,128)(2,1)}), bf16[8,128,384]{2,1,0:T(8,128)(2,1)S(1)}, u32[]{:S(2)}, u32[]{:S(2)}) async-start(bf16[8,128,384]{2,1,0:T(8,128)(2,1)} %bitcast.308), calls=%async_computation | async-start | bytes 1572864 | tf_op jit(solution)/shard_map/all_to_all | solution.py:736
  56.0 32.5 %collective-permute-start.17 = (bf16[1,224,512]{2,1,0:T(8,128)(2,1)}, bf16[1,224,512]{2,1,0:T(8,128)(2,1)}, u32[]{:S(2)}, u32[]{:S(2)}) collective-permute-start(bf16[1,224,512]{2,1,0:T(8,128)(2,1)} %get-tuple-element.91), channel_id=1, source_target_pairs={{0,2},{1,3},{2,0},{3,1},{4,6},{5,7},{6,4},{7,5},{8,10},{9,11},{10,... | collective-permute-start | bytes 688136 | tf_op jit(solution)/shard_map/ppermute | solution.py:58
  59.3 29.2 %collective-permute-start.22 = (bf16[1,224,512]{2,1,0:T(8,128)(2,1)}, bf16[1,224,512]{2,1,0:T(8,128)(2,1)}, u32[]{:S(2)}, u32[]{:S(2)}) collective-permute-start(bf16[1,224,512]{2,1,0:T(8,128)(2,1)} %get-tuple-element.83), channel_id=1, source_target_pairs={{0,2},{1,3},{2,0},{3,1},{4,6},{5,7},{6,4},{7,5},{8,10},{9,11},{10,... | collective-permute-start | bytes 688136 | tf_op jit(solution)/shard_map/ppermute | solution.py:58
  70.3 27.7 %collective-permute-start.24 = (bf16[1,224,512]{2,1,0:T(8,128)(2,1)}, bf16[1,224,512]{2,1,0:T(8,128)(2,1)}, u32[]{:S(2)}, u32[]{:S(2)}) collective-permute-start(bf16[1,224,512]{2,1,0:T(8,128)(2,1)} %get-tuple-element.87), channel_id=1, source_target_pairs={{0,2},{1,3},{2,0},{3,1},{4,6},{5,7},{6,4},{7,5},{8,10},{9,11},{10,... | collective-permute-start | bytes 688136 | tf_op jit(solution)/shard_map/ppermute | solution.py:58
  101.0 51.9 %collective-permute-start.32 = (bf16[1,224,1792]{2,1,0:T(8,128)(2,1)}, bf16[1,224,1792]{2,1,0:T(8,128)(2,1)}, u32[]{:S(2)}, u32[]{:S(2)}) collective-permute-start(bf16[1,224,1792]{2,1,0:T(8,128)(2,1)} %get-tuple-element.60), channel_id=1, source_target_pairs={{0,2},{1,3},{2,0},{3,1},{4,6},{5,7},{6,4},{7,5},{8,10},{9,11},{10,... | collective-permute-start | bytes 2408456 | tf_op jit(solution)/shard_map/ppermute | solution.py:58
  110.0 25.4 %collective-permute-start.14 = (bf16[128,896]{1,0:T(8,128)(2,1)S(1)}, bf16[128,896]{1,0:T(8,128)(2,1)S(1)}, u32[]{:S(2)}, u32[]{:S(2)}) collective-permute-start(bf16[128,896]{1,0:T(8,128)(2,1)S(1)} %multiply_convert_fusion.2), channel_id=1, source_target_pairs={{0,1},{1,0},{2,3},{3,2},{4,5},{5,4},{6,7},{7,6},{8,9},{9,8},{10,11... | collective-permute-start | bytes 688136 | tf_op jit(solution)/shard_map/ppermute | solution.py:58
  172.6 23.6 %collective-permute-start.34 = (bf16[128,896]{1,0:T(8,128)(2,1)S(1)}, bf16[128,896]{1,0:T(8,128)(2,1)S(1)}, u32[]{:S(2)}, u32[]{:S(2)}) collective-permute-start(bf16[128,896]{1,0:T(8,128)(2,1)S(1)} %get-tuple-element.73), channel_id=1, source_target_pairs={{0,1},{1,0},{2,3},{3,2},{4,5},{5,4},{6,7},{7,6},{8,9},{9,8},{10,11... | collective-permute-start | bytes 688136 | tf_op jit(solution)/shard_map/ppermute | solution.py:58
  213.3 57.5 %collective-permute-start.109 = (bf16[1,4,112,896]{3,2,1,0:T(8,128)(2,1)}, bf16[1,4,112,896]{3,2,1,0:T(8,128)(2,1)}, u32[]{:S(2)}, u32[]{:S(2)}) collective-permute-start(bf16[1,4,112,896]{3,2,1,0:T(8,128)(2,1)} %constant_dynamic-slice_fusion.7), channel_id=1, source_target_pairs={{0,4},{4,0},{8,12},{12,8},{16,20},{20,16},{24,28},{28,24},{1,5},{5... | collective-permute-start | bytes 2408456 | tf_op jit(solution)/shard_map/ppermute | solution.py:58
  219.4 54.8 %collective-permute-start.117 = (bf16[1,448,896]{2,1,0:T(8,128)(2,1)}, bf16[1,448,896]{2,1,0:T(8,128)(2,1)}, u32[]{:S(2)}, u32[]{:S(2)}) collective-permute-start(bf16[1,448,896]{2,1,0:T(8,128)(2,1)} %dynamic-slice_bitcast_fusion), channel_id=1, source_target_pairs={{0,4},{4,0},{8,12},{12,8},{16,20},{20,16},{24,28},{28,24},{1,5},{5... | collective-permute-start | bytes 2408456 | tf_op jit(solution)/shard_map/ppermute | solution.py:58
  224.2 46.5 %collective-permute-start.54 = (bf16[128,896]{1,0:T(8,128)(2,1)}, bf16[128,896]{1,0:T(8,128)(2,1)}, u32[]{:S(2)}, u32[]{:S(2)}) collective-permute-start(bf16[128,896]{1,0:T(8,128)(2,1)} %get-tuple-element.39), channel_id=1, source_target_pairs={{0,2},{1,3},{2,0},{3,1},{4,6},{5,7},{6,4},{7,5},{8,10},{9,11},{10,... | collective-permute-start | bytes 688136 | tf_op jit(solution)/shard_map/ppermute | solution.py:58
  225.3 52.1 %collective-permute-start.53 = (bf16[128,896]{1,0:T(8,128)(2,1)}, bf16[128,896]{1,0:T(8,128)(2,1)S(1)}, u32[]{:S(2)}, u32[]{:S(2)}) collective-permute-start(bf16[128,896]{1,0:T(8,128)(2,1)} %get-tuple-element.39), channel_id=1, source_target_pairs={{0,1},{1,0},{2,3},{3,2},{4,5},{5,4},{6,7},{7,6},{8,9},{9,8},{10,11... | collective-permute-start | bytes 688136 | tf_op jit(solution)/shard_map/ppermute | solution.py:58
  273.2 39.7 %collective-permute-start.110 = (bf16[1,4,56,896]{3,2,1,0:T(8,128)(2,1)}, bf16[1,4,56,896]{3,2,1,0:T(8,128)(2,1)}, u32[]{:S(2)}, u32[]{:S(2)}) collective-permute-start(bf16[1,4,56,896]{3,2,1,0:T(8,128)(2,1)} %constant_dynamic-slice_fusion.6), channel_id=1, source_target_pairs={{0,8},{4,12},{8,0},{12,4},{16,24},{20,28},{24,16},{28,20},{1,9},{5... | collective-permute-start | bytes 1204232 | tf_op jit(solution)/shard_map/ppermute | solution.py:58
  276.4 37.9 %collective-permute-start.118 = (bf16[1,224,896]{2,1,0:T(8,128)(2,1)}, bf16[1,224,896]{2,1,0:T(8,128)(2,1)}, u32[]{:S(2)}, u32[]{:S(2)}) collective-permute-start(bf16[1,224,896]{2,1,0:T(8,128)(2,1)} %constant_dynamic-slice_fusion.3), channel_id=1, source_target_pairs={{0,8},{4,12},{8,0},{12,4},{16,24},{20,28},{24,16},{28,20},{1,9},{5... | collective-permute-start | bytes 1204232 | tf_op jit(solution)/shard_map/ppermute | solution.py:58
  307.7 34.3 %collective-permute-start.95 = (bf16[2,4,112,256]{3,2,1,0:T(8,128)(2,1)S(1)}, bf16[2,4,112,256]{3,2,1,0:T(8,128)(2,1)S(1)}, u32[]{:S(2)}, u32[]{:S(2)}) collective-permute-start(bf16[2,4,112,256]{3,2,1,0:T(8,128)(2,1)S(1)} %fusion.31), channel_id=1, source_target_pairs={{0,4},{4,0},{8,12},{12,8},{16,20},{20,16},{24,28},{28,24},{1,5},{5... | collective-permute-start | bytes 1376264 | tf_op jit(solution)/shard_map/ppermute | solution.py:58
  310.6 31.7 %collective-permute-start.56 = (bf16[128,896]{1,0:T(8,128)(2,1)S(1)}, bf16[128,896]{1,0:T(8,128)(2,1)S(1)}, u32[]{:S(2)}, u32[]{:S(2)}) collective-permute-start(bf16[128,896]{1,0:T(8,128)(2,1)S(1)} %get-tuple-element.69), channel_id=1, source_target_pairs={{0,1},{1,0},{2,3},{3,2},{4,5},{5,4},{6,7},{7,6},{8,9},{9,8},{10,11... | collective-permute-start | bytes 688136 | tf_op jit(solution)/shard_map/ppermute | solution.py:58
  312.5 217.8 %collective-permute-start.65 = (bf16[512,896]{1,0:T(8,128)(2,1)}, bf16[512,896]{1,0:T(8,128)(2,1)}, u32[]{:S(2)}, u32[]{:S(2)}) collective-permute-start(bf16[512,896]{1,0:T(8,128)(2,1)} %get-tuple-element.51), channel_id=1, source_target_pairs={{0,1},{1,0},{2,3},{3,2},{4,5},{5,4},{6,7},{7,6},{8,9},{9,8},{10,11... | collective-permute-start | bytes 2752520 | tf_op jit(solution)/shard_map/ppermute | solution.py:58
  312.9 123.0 %collective-permute-start.66 = (bf16[512,896]{1,0:T(8,128)(2,1)}, bf16[512,896]{1,0:T(8,128)(2,1)}, u32[]{:S(2)}, u32[]{:S(2)}) collective-permute-start(bf16[512,896]{1,0:T(8,128)(2,1)} %get-tuple-element.52), channel_id=1, source_target_pairs={{0,1},{1,0},{2,3},{3,2},{4,5},{5,4},{6,7},{7,6},{8,9},{9,8},{10,11... | collective-permute-start | bytes 2752520 | tf_op jit(solution)/shard_map/ppermute | solution.py:58
  342.0 22.3 %collective-permute-start.111 = (bf16[1,4,28,896]{3,2,1,0:T(8,128)(2,1)S(1)}, bf16[1,4,28,896]{3,2,1,0:T(8,128)(2,1)S(1)}, u32[]{:S(2)}, u32[]{:S(2)}) collective-permute-start(bf16[1,4,28,896]{3,2,1,0:T(8,128)(2,1)S(1)} %constant_dynamic-slice_fusion.5), channel_id=1, source_target_pairs={{0,16},{4,20},{8,24},{12,28},{16,0},{20,4},{24,8},{28,12},{1,17},{... | collective-permute-start | bytes 602120 | tf_op jit(solution)/shard_map/ppermute | solution.py:58
  342.3 24.6 %collective-permute-start.119 = (bf16[1,112,896]{2,1,0:T(8,128)(2,1)S(1)}, bf16[1,112,896]{2,1,0:T(8,128)(2,1)S(1)}, u32[]{:S(2)}, u32[]{:S(2)}) collective-permute-start(bf16[1,112,896]{2,1,0:T(8,128)(2,1)S(1)} %constant_dynamic-slice_fusion.2), channel_id=1, source_target_pairs={{0,16},{4,20},{8,24},{12,28},{16,0},{20,4},{24,8},{28,12},{1,17},{... | collective-permute-start | bytes 602120 | tf_op jit(solution)/shard_map/ppermute | solution.py:58
  364.3 24.1 %collective-permute-start.96 = (bf16[2,4,56,256]{3,2,1,0:T(8,128)(2,1)S(1)}, bf16[2,4,56,256]{3,2,1,0:T(8,128)(2,1)S(1)}, u32[]{:S(2)}, u32[]{:S(2)}) collective-permute-start(bf16[2,4,56,256]{3,2,1,0:T(8,128)(2,1)S(1)} %constant_dynamic-slice_fusion.12), channel_id=1, source_target_pairs={{0,8},{4,12},{8,0},{12,4},{16,24},{20,28},{24,16},{28,20},{1,9},{5... | collective-permute-start | bytes 688136 | tf_op jit(solution)/shard_map/ppermute | solution.py:58
  369.8 36.2 %collective-permute-start.60 = (bf16[128,896]{1,0:T(8,128)(2,1)S(1)}, bf16[128,896]{1,0:T(8,128)(2,1)S(1)}, u32[]{:S(2)}, u32[]{:S(2)}) collective-permute-start(bf16[128,896]{1,0:T(8,128)(2,1)S(1)} %get-tuple-element.37), channel_id=1, source_target_pairs={{0,2},{1,3},{2,0},{3,1},{4,6},{5,7},{6,4},{7,5},{8,10},{9,11},{10,... | collective-permute-start | bytes 688136 | tf_op jit(solution)/shard_map/ppermute | solution.py:58
  423.2 37.0 %collective-permute-start.115 = (bf16[1,56,3584]{2,1,0:T(8,128)(2,1)}, bf16[1,56,3584]{2,1,0:T(8,128)(2,1)S(1)}, u32[]{:S(2)}, u32[]{:S(2)}) collective-permute-start(bf16[1,56,3584]{2,1,0:T(8,128)(2,1)} %maximum_select_fusion.31), channel_id=1, source_target_pairs={{0,8},{4,12},{8,0},{12,4},{16,24},{20,28},{24,16},{28,20},{1,9},{5... | collective-permute-start | bytes 1204232 | tf_op jit(solution)/shard_map/ppermute | solution.py:58
  429.3 37.9 %all-to-all-start.2 = ((bf16[8,128,128]{2,1,0:T(8,128)(2,1)}), bf16[8,128,128]{2,1,0:T(8,128)(2,1)S(1)}, u32[]{:S(2)}, u32[]{:S(2)}) async-start(bf16[8,128,128]{2,1,0:T(8,128)(2,1)} %bitcast.340), calls=%async_computation.2 | async-start | bytes 524288 | tf_op jit(solution)/shard_map/all_to_all | solution.py:832
  444.2 87.1 %collective-permute-start.67 = (bf16[512,896]{1,0:T(8,128)(2,1)}, bf16[512,896]{1,0:T(8,128)(2,1)}, u32[]{:S(2)}, u32[]{:S(2)}) collective-permute-start(bf16[512,896]{1,0:T(8,128)(2,1)} %fusion.14), channel_id=1, source_target_pairs={{0,2},{1,3},{2,0},{3,1},{4,6},{5,7},{6,4},{7,5},{8,10},{9,11},{10,... | collective-permute-start | bytes 2752520 | tf_op jit(solution)/shard_map/ppermute | solution.py:58
  450.4 95.9 %collective-permute-start.122 = (bf16[1,448,896]{2,1,0:T(8,128)(2,1)}, bf16[1,448,896]{2,1,0:T(8,128)(2,1)}, u32[]{:S(2)}, u32[]{:S(2)}) collective-permute-start(bf16[1,448,896]{2,1,0:T(8,128)(2,1)} %maximum_select_fusion.10), channel_id=1, source_target_pairs={{0,4},{4,0},{8,12},{12,8},{16,20},{20,16},{24,28},{28,24},{1,5},{5... | collective-permute-start | bytes 2408456 | tf_op jit(solution)/shard_map/ppermute | solution.py:58
  458.5 48.2 %collective-permute-start.102 = (bf16[2,112,1024]{2,1,0:T(8,128)(2,1)S(1)}, bf16[2,112,1024]{2,1,0:T(8,128)(2,1)}, u32[]{:S(2)}, u32[]{:S(2)}) collective-permute-start(bf16[2,112,1024]{2,1,0:T(8,128)(2,1)S(1)} %maximum_select_fusion.28), channel_id=1, source_target_pairs={{0,4},{4,0},{8,12},{12,8},{16,20},{20,16},{24,28},{28,24},{1,5},{5... | collective-permute-start | bytes 1376264 | tf_op jit(solution)/shard_map/ppermute | solution.py:58
  506.6 23.4 %collective-permute-start.68 = (bf16[4,4,112,256]{3,2,1,0:T(8,128)(2,1)S(1)}, bf16[4,4,112,256]{3,2,1,0:T(8,128)(2,1)S(1)}, u32[]{:S(2)}, u32[]{:S(2)}) collective-permute-start(bf16[4,4,112,256]{3,2,1,0:T(8,128)(2,1)S(1)} %constant_dynamic-slice_fusion.25), channel_id=1, source_target_pairs={{0,4},{4,0},{8,12},{12,8},{16,20},{20,16},{24,28},{28,24},{1,5},{5... | collective-permute-start | bytes 2752520 | tf_op jit(solution)/shard_map/ppermute | solution.py:58
  510.9 65.7 %collective-permute-start.116 = (bf16[1,112,3584]{2,1,0:T(8,128)(2,1)}, bf16[1,112,3584]{2,1,0:T(8,128)(2,1)}, u32[]{:S(2)}, u32[]{:S(2)}) collective-permute-start(bf16[1,112,3584]{2,1,0:T(8,128)(2,1)} %maximum_select_fusion.8), channel_id=1, source_target_pairs={{0,4},{4,0},{8,12},{12,8},{16,20},{20,16},{24,28},{28,24},{1,5},{5... | collective-permute-start | bytes 2408456 | tf_op jit(solution)/shard_map/ppermute | solution.py:58
  (180 other events, 2169.6 us)

commit v2 on v1

--- a/solution.py
+++ b/solution.py
@@ -446,6 +446,394 @@
     )(query, pair, grad)
 
 
+mesh_id = pl.DeviceIdType.MESH
+
+
+def signal_to(barrier, ctx, wa):
+    pl.semaphore_signal(barrier, inc=1, device_id=(ctx, wa), device_id_type=mesh_id)
+
+
+def tree_sum(values):
+    while len(values) > 1:
+        values = [a + b for a, b in zip(values[::2], values[1::2])]
+    return values[0]
+
+
+def gather_kernel(
+    parts,
+    block_ref,
+    small_ref,
+    *refs,
+):
+    part_refs = refs[:parts]
+    out_ref, total_ref = refs[parts : parts + 2]
+    part_outs = refs[parts + 2 : 2 * parts + 2]
+    near, far, y_send, y_recv, r_send, r_recv, l_send, l_recv, s_send, s_recv, p_send, p_recv, o_sem = refs[
+        2 * parts + 2 :
+    ]
+    c = lax.axis_index("ctx")
+    w = lax.axis_index("wa")
+    z = c // 2
+    right = z < 3
+    left = z > 0
+    barrier = pltpu.get_barrier_semaphore()
+    for j in range(1, 8):
+        signal_to(barrier, c ^ j, w)
+    for j in range(1, 4):
+        signal_to(barrier, c, w ^ j)
+    pl.semaphore_wait(barrier, 10)
+
+    def small_copy(source, j):
+        wide = j < 4
+        return pltpu.make_async_remote_copy(
+            src_ref=source,
+            dst_ref=near.at[j] if wide else far.at[j - 3],
+            send_sem=s_send.at[j],
+            recv_sem=s_recv.at[j],
+            device_id=(c, w ^ j) if wide else (c ^ (j - 3), w),
+            device_id_type=mesh_id,
+        )
+
+    for j in range(1, 4):
+        small_copy(small_ref, j).start()
+
+    def part_copy(m, j):
+        return pltpu.make_async_remote_copy(
+            src_ref=part_refs[m],
+            dst_ref=part_outs[m].at[w],
+            send_sem=p_send.at[m, j],
+            recv_sem=p_recv.at[m, j],
+            device_id=(c, w ^ j),
+            device_id_type=mesh_id,
+        )
+
+    for m in reversed(range(parts)):
+        for j in (1, 2, 3):
+            part_copy(m, j).start()
+
+    def y_copy(source, block, slot):
+        return pltpu.make_async_remote_copy(
+            src_ref=source,
+            dst_ref=out_ref.at[block],
+            send_sem=y_send.at[slot],
+            recv_sem=y_recv.at[slot],
+            device_id=(c ^ 1, w),
+            device_id_type=mesh_id,
+        )
+
+    def z_copy(source, block, slot, step, send, recv):
+        return pltpu.make_async_remote_copy(
+            src_ref=source,
+            dst_ref=out_ref.at[block],
+            send_sem=send.at[slot],
+            recv_sem=recv.at[slot],
+            device_id=(c + step, w),
+            device_id_type=mesh_id,
+        )
+
+    @pl.when(right)
+    def _():
+        z_copy(block_ref, c, 0, 2, r_send, r_recv).start()
+
+    @pl.when(left)
+    def _():
+        z_copy(block_ref, c, 0, -2, l_send, l_recv).start()
+
+    y_copy(block_ref, c, 0).start()
+    own = [pltpu.make_async_copy(block_ref, out_ref.at[c], o_sem.at[0])]
+    for m in range(parts):
+        own.append(pltpu.make_async_copy(part_refs[m], part_outs[m].at[w], o_sem.at[1 + m]))
+    for copy in own:
+        copy.start()
+    for j in range(1, 4):
+        small_copy(small_ref, j).wait()
+    total_ref[...] = tree_sum([small_ref[...]] + [near[j] for j in range(1, 4)])
+    for j in range(4, 11):
+        small_copy(total_ref, j).start()
+    for t in range(3):
+
+        @pl.when(z > t)
+        def _(t=t):
+            block = c - 2 * (t + 1)
+            z_copy(out_ref.at[block], block, t, 2, r_send, r_recv).wait_recv()
+            if t < 2:
+
+                @pl.when(right)
+                def _():
+                    z_copy(out_ref.at[block], block, t + 1, 2, r_send, r_recv).start()
+
+            y_copy(out_ref.at[block], block, t + 1).start()
+
+        @pl.when(z < 3 - t)
+        def _(t=t):
+            block = c + 2 * (t + 1)
+            z_copy(out_ref.at[block], block, t, -2, l_send, l_recv).wait_recv()
+            if t < 2:
+
+                @pl.when(left)
+                def _():
+                    z_copy(out_ref.at[block], block, t + 1, -2, l_send, l_recv).start()
+
+            y_copy(out_ref.at[block], block, t + 4).start()
+
+    for j in range(4, 11):
+        small_copy(total_ref, j).wait()
+    total_ref[...] = tree_sum([total_ref[...]] + [far[j] for j in range(1, 8)])
+    y_copy(block_ref, c ^ 1, 0).wait()
+    for t in range(3):
+
+        @pl.when(z > t)
+        def _(t=t):
+            block = (c ^ 1) - 2 * (t + 1)
+            y_copy(out_ref.at[block], block, t + 1).wait()
+
+        @pl.when(z < 3 - t)
+        def _(t=t):
+            block = (c ^ 1) + 2 * (t + 1)
+            y_copy(out_ref.at[block], block, t + 4).wait()
+
+    @pl.when(right)
+    def _():
+        z_copy(block_ref, c, 0, 2, r_send, r_recv).wait_send()
+
+    @pl.when(left)
+    def _():
+        z_copy(block_ref, c, 0, -2, l_send, l_recv).wait_send()
+
+    for t in range(2):
+
+        @pl.when(jnp.logical_and(z > t, right))
+        def _(t=t):
+            z_copy(block_ref, c, t + 1, 2, r_send, r_recv).wait_send()
+
+        @pl.when(jnp.logical_and(z < 3 - t, left))
+        def _(t=t):
+            z_copy(block_ref, c, t + 1, -2, l_send, l_recv).wait_send()
+
+    for m in range(parts):
+        for j in range(1, 4):
+            part_copy(m, j).wait_send()
+            pltpu.make_async_remote_copy(
+                src_ref=part_refs[m],
+                dst_ref=part_outs[m].at[w ^ j],
+                send_sem=p_send.at[m, j],
+                recv_sem=p_recv.at[m, j],
+                device_id=(c, w ^ j),
+                device_id_type=mesh_id,
+            ).wait_recv()
+    for copy in own:
+        copy.wait()
+
+
+def gather_all(block, small, parts, collective_id):
+    dma = pltpu.SemaphoreType.DMA
+    count = len(parts)
+    got = pl.pallas_call(
+        functools.partial(gather_kernel, count),
+        out_shape=[
+            jax.ShapeDtypeStruct((8,) + block.shape, block.dtype),
+            jax.ShapeDtypeStruct(small.shape, small.dtype),
+        ]
+        + [jax.ShapeDtypeStruct((4,) + part.shape, part.dtype) for part in parts],
+        in_specs=[in_vmem] * (2 + count),
+        out_specs=[in_vmem] * (2 + count),
+        scratch_shapes=[
+            pltpu.VMEM((4,) + small.shape, small.dtype),
+            pltpu.VMEM((8,) + small.shape, small.dtype),
+            dma((7,)),
+            dma((7,)),
+            dma((3,)),
+            dma((3,)),
+            dma((3,)),
+            dma((3,)),
+            dma((11,)),
+            dma((11,)),
+            dma((max(count, 1), 4)),
+            dma((max(count, 1), 4)),
+            dma((1 + count,)),
+        ],
+        compiler_params=pltpu.CompilerParams(
+            collective_id=collective_id, has_side_effects=True, vmem_limit_bytes=40 * 2**20
+        ),
+        name="gather_all",
+    )(block, small, *parts)
+    return got[0], got[1], got[2:]
+
+
+def swap_heads_kernel(outward, in_ref, out_ref, send_sem, recv_sem):
+    c = lax.axis_index("ctx")
+    w = lax.axis_index("wa")
+    owner = c // 2
+    half = c % 2
+    own = owner == w
+    other = jnp.logical_not(own)
+    barrier = pltpu.get_barrier_semaphore()
+
+    def lanes(start):
+        return pl.ds(pl.multiple_of(start * 128, 128), 128)
+
+    for j in range(1, 8):
+        signal_to(barrier, c ^ j, owner)
+    for r in range(4):
+        for h in range(2):
+            mine = jnp.logical_and(2 * w + h == c, r == 0)
+
+            @pl.when(jnp.logical_not(mine))
+            def _(r=r, h=h):
+                signal_to(barrier, 2 * w + h, w ^ r)
+
+    @pl.when(other)
+    def _():
+        signal_to(barrier, c, owner)
+
+    pl.semaphore_wait(barrier, 16 - 2 * own.astype(jnp.int32))
+    slot = w ^ owner
+    if outward:
+
+        def copy_to(j):
+            return pltpu.make_async_remote_copy(
+                src_ref=in_ref.at[c ^ j],
+                dst_ref=out_ref.at[slot, :, lanes(half)],
+                send_sem=send_sem.at[j],
+                recv_sem=recv_sem.at[slot * 2 + half],
+                device_id=(c ^ j, owner),
+                device_id_type=mesh_id,
+            )
+
+        for j in range(7, 0, -1):
+            copy_to(j).start()
+
+        @pl.when(other)
+        def _():
+            copy_to(0).start()
+
+        @pl.when(own)
+        def _():
+            pltpu.make_async_copy(
+                in_ref.at[c], out_ref.at[slot, :, lanes(half)], recv_sem.at[slot * 2 + half]
+            ).start()
+
+        for r in range(4):
+            for h in range(2):
+                pltpu.make_async_remote_copy(
+                    src_ref=in_ref.at[0],
+                    dst_ref=out_ref.at[r, :, h * 128 : (h + 1) * 128],
+                    send_sem=send_sem.at[0],
+                    recv_sem=recv_sem.at[r * 2 + h],
+                    device_id=(c ^ 1, w),
+                    device_id_type=mesh_id,
+                ).wait_recv()
+        for j in range(1, 8):
+            copy_to(j).wait_send()
+
+        @pl.when(other)
+        def _():
+            copy_to(0).wait_send()
+
+    else:
+
+        def copy_to(r, h):
+            return pltpu.make_async_remote_copy(
+                src_ref=in_ref.at[r, :, h * 128 : (h + 1) * 128],
+                dst_ref=out_ref.at[c],
+                send_sem=send_sem.at[r * 2 + h],
+                recv_sem=recv_sem.at[c],
+                device_id=(2 * w + h, w ^ r),
+                device_id_type=mesh_id,
+            )
+
+        for r in (3, 2, 1, 0):
+            for h in range(2):
+                mine = jnp.logical_and(2 * w + h == c, r == 0)
+
+                @pl.when(jnp.logical_not(mine))
+                def _(r=r, h=h):
+                    copy_to(r, h).start()
+
+                @pl.when(mine)
+                def _(r=r, h=h):
+                    pltpu.make_async_copy(
+                        in_ref.at[r, :, h * 128 : (h + 1) * 128], out_ref.at[c], recv_sem.at[c]
+                    ).start()
+
+        for block in range(8):
+            pltpu.make_async_remote_copy(
+                src_ref=in_ref.at[0, :, 0:128],
+                dst_ref=out_ref.at[block],
+                send_sem=send_sem.at[0],
+                recv_sem=recv_sem.at[block],
+                device_id=(c ^ 1, w),
+                device_id_type=mesh_id,
+            ).wait_recv()
+        for r in range(4):
+            for h in range(2):
+                mine = jnp.logical_and(2 * w + h == c, r == 0)
+
+                @pl.when(jnp.logical_not(mine))
+                def _(r=r, h=h):
+                    copy_to(r, h).wait_send()
+
+
+def swap_heads(value, outward, collective_id):
+    rows = value.shape[1]
+    shape = (4, rows, 256) if outward else (8, rows, 128)
+    return pl.pallas_call(
+        functools.partial(swap_heads_kernel, outward),
+        out_shape=jax.ShapeDtypeStruct(shape, value.dtype),
+        in_specs=[in_vmem],
+        out_specs=in_vmem,
+        scratch_shapes=[pltpu.SemaphoreType.DMA((8,)), pltpu.SemaphoreType.DMA((8,))],
+        compiler_params=pltpu.CompilerParams(collective_id=collective_id, has_side_effects=True),
+        name="swap_heads",
+    )(value)
+
+
+def blocks_to_columns_kernel(in_ref, out_ref, send_sem, recv_sem):
+    c = lax.axis_index("ctx")
+    w = lax.axis_index("wa")
+    width = in_ref.shape[2]
+    barrier = pltpu.get_barrier_semaphore()
+    for j in range(1, 8):
+        signal_to(barrier, c ^ j, w)
+    pl.semaphore_wait(barrier, 7)
+
+    def columns(block):
+        return out_ref.at[:, pl.ds(pl.multiple_of(block * width, 128), width)]
+
+    def copy_to(j, block):
+        return pltpu.make_async_remote_copy(
+            src_ref=in_ref.at[c ^ j],
+            dst_ref=columns(block),
+            send_sem=send_sem.at[j],
+            recv_sem=recv_sem.at[j],
+            device_id=(c ^ j, w),
+            device_id_type=mesh_id,
+        )
+
+    for j in (4, 6, 5, 7, 2, 3, 1):
+        copy_to(j, c).start()
+    own = pltpu.make_async_copy(in_ref.at[c], columns(c), recv_sem.at[0])
+    own.start()
+    for j in range(1, 8):
+        copy_to(j, c ^ j).wait_recv()
+    for j in range(1, 8):
+        copy_to(j, c).wait_send()
+    own.wait()
+
+
+def blocks_to_columns(value, collective_id):
+    blocks, rows, width = value.shape
+    return pl.pallas_call(
+        blocks_to_columns_kernel,
+        out_shape=jax.ShapeDtypeStruct((rows, blocks * width), value.dtype),
+        in_specs=[in_vmem],
+        out_specs=in_vmem,
+        scratch_shapes=[pltpu.SemaphoreType.DMA((8,)), pltpu.SemaphoreType.DMA((8,))],
+        compiler_params=pltpu.CompilerParams(collective_id=collective_id, has_side_effects=True),
+        name="blocks_to_columns",
+    )(value)
+
+
 def skew(wide, count):
     lead = wide.shape[:-2]
     rows, span = wide.shape[-2:]
@@ -656,7 +1044,7 @@
         return query_grad, key_grad, value_grad, bias_grads, table_grad
 
 
-def local(
+def local_general(
     tokens,
     neighbours,
     teacher,
@@ -688,8 +1076,6 @@
     block = tok_dev // 2
     cols = HEADS * HEAD_DIM // places
     rows = places * tok_dev
-    pairs = cols // 128
-    by_heads = places * pairs == ctx_count and seq_len % TILE == 0
 
     token_parts = gather_parts(tokens[0])
     query_cols, key_cols, value_cols = [
@@ -720,47 +1106,20 @@
     scale_all = inverse_rms(hidden_all)
     normed_a = (hidden_all * scale_all * gain_one).astype(bf16)
     biases = jnp.stack([content_bias, position_bias]).astype(f32)
-    if by_heads:
-        which = here % pairs
-        mixed_cols = jnp.concatenate(
-            [
-                part[:, 128 * pair : 128 * (pair + 1)]
-                for pair in range(pairs)
-                for part in (query_cols, key_cols, value_cols)
-            ],
-            axis=1,
-        )
-        qkv = dot_nn(normed_a, mixed_cols).astype(bf16)
-        qkv = qkv.reshape(places, tok_dev, pairs, 384).transpose(0, 2, 1, 3)
-        qkv = qkv.reshape(ctx_count, tok_dev, 384)
-        qkv = lax.all_to_all(qkv, "ctx", split_axis=0, concat_axis=0, tiled=True)
-        qkv = qkv.reshape(seq_len, 384)
-        my_relative = lax.dynamic_slice_in_dim(relative_cols, which * 128, 128, 1)
-        table = dot_nn(waves, my_relative).astype(bf16)
-        table = jnp.concatenate([table, jnp.zeros((TILE, 128), bf16)], axis=0)
-        my_biases = lax.dynamic_slice_in_dim(biases, which * 128, 128, 1)
-        my_biases = jnp.concatenate([my_biases, jnp.zeros((6, 128), f32)], axis=0)
-        out = attend_forward(inverse, qkv, table, my_biases, block)
-        out = lax.all_to_all(
-            out.reshape(ctx_count, tok_dev, 128), "ctx", split_axis=0, concat_axis=0, tiled=True
-        )
-        out = out.reshape(places, pairs, tok_dev, 128).transpose(0, 2, 1, 3)
-        attended = out.reshape(rows, cols)
-    else:
-        mixed_cols = jnp.concatenate([query_cols, key_cols, value_cols], axis=1)
-        qkv = dot_nn(normed_a, mixed_cols).reshape(places, tok_dev, 3 * cols)
-        relative = dot_nn(waves, relative_cols).astype(bf16)
-        general = SplitQueries(
-            qkv[..., :cols],
-            qkv[..., cols : 2 * cols].astype(bf16),
-            qkv[..., 2 * cols :].astype(bf16),
-            biases,
-            relative,
-            block_order,
-            inverse,
-            block,
-        )
-        attended = general.forward()
+    mixed_cols = jnp.concatenate([query_cols, key_cols, value_cols], axis=1)
+    qkv = dot_nn(normed_a, mixed_cols).reshape(places, tok_dev, 3 * cols)
+    relative = dot_nn(waves, relative_cols).astype(bf16)
+    general = SplitQueries(
+        qkv[..., :cols],
+        qkv[..., cols : 2 * cols].astype(bf16),
+        qkv[..., 2 * cols :].astype(bf16),
+        biases,
+        relative,
+        block_order,
+        inverse,
+        block,
+    )
+    attended = general.forward()
 
     def to_owner(product):
         return scatter_parts([product[r * tok_dev : (r + 1) * tok_dev] for r in range(places)])
@@ -826,45 +1185,13 @@
     attended_grad = dot_nt(one_low, output_weight).astype(bf16)
     output_grad = dot_tn(attended, one_low).astype(bf16)
     output_out = sum_row_grads(output_grad)
-    if by_heads:
-        grad = attended_grad.reshape(places, tok_dev, pairs, 128).transpose(0, 2, 1, 3)
-        grad = grad.reshape(ctx_count, tok_dev, 128)
-        grad = lax.all_to_all(grad, "ctx", split_axis=0, concat_axis=0, tiled=True)
-        grad = grad.reshape(seq_len, 128)
-        qkv_grad, table_grad, bias_part = attend_backward(
-            inverse, qkv, table, my_biases, grad, block
-        )
-        qkv_grad = lax.all_to_all(
-            qkv_grad.reshape(ctx_count, tok_dev, 384), "ctx", split_axis=0, concat_axis=0, tiled=True
-        )
-        qkv_grad = qkv_grad.reshape(places, pairs, tok_dev, 384).transpose(0, 2, 1, 3)
-        qkv_grad = qkv_grad.reshape(rows, 3 * cols)
-        bias_grads = jnp.concatenate(
-            [jnp.where(which == pair, bias_part[0:2], 0.0) for pair in range(pairs)], axis=1
-        )
-    else:
-        query_grad, key_grad, value_grad, bias_grads, table_grad = general.backward(attended_grad)
-        qkv_grad = jnp.concatenate([query_grad, key_grad, value_grad], axis=1)
+    query_grad, key_grad, value_grad, bias_grads, table_grad = general.backward(attended_grad)
+    qkv_grad = jnp.concatenate([query_grad, key_grad, value_grad], axis=1)
     table_high = table_grad.astype(bf16)
     table_low = (table_grad - table_high.astype(f32)).astype(bf16)
     relative_grad = (dot_tn(waves, table_high) + dot_tn(waves, table_low)).astype(bf16)
     mixed_grad = dot_tn(normed_a, qkv_grad).astype(bf16)
-    if by_heads:
-        relative_grad = jnp.concatenate(
-            [jnp.where(which == pair, relative_grad, 0.0) for pair in range(pairs)], axis=1
-        )
-        whole = [
-            jnp.concatenate(
-                [
-                    mixed_grad[:, 384 * pair + 128 * m : 384 * pair + 128 * (m + 1)]
-                    for pair in range(pairs)
-                ],
-                axis=1,
-            )
-            for m in range(3)
-        ]
-    else:
-        whole = [mixed_grad[:, m * cols : (m + 1) * cols] for m in range(3)]
+    whole = [mixed_grad[:, m * cols : (m + 1) * cols] for m in range(3)]
     attention_out = sum_column_grads(jnp.stack(whole + [relative_grad]))
     normed_a_part = dot_nt(qkv_grad, mixed_cols)
     gain_one_part = jnp.sum(normed_a_part * hidden_all * scale_all, axis=0, keepdims=True)
@@ -904,6 +1231,222 @@
     )
 
 
+def local_by_heads(
+    tokens,
+    neighbours,
+    teacher,
+    valid_mask,
+    block_order,
+    query_weight,
+    key_weight,
+    value_weight,
+    output_weight,
+    relative_weight,
+    content_bias,
+    position_bias,
+    cross_query_weight,
+    cross_key_weight,
+    cross_value_weight,
+    cross_output_weight,
+    up_weight,
+    down_weight,
+    attention_gain,
+    cross_gain,
+    feedforward_gain,
+):
+    places = 4
+    ctx_count = 8
+    place = lax.axis_index("wa")
+    here = lax.axis_index("ctx")
+    _, tok_dev, width = tokens.shape
+    seq_len = tok_dev * ctx_count
+    block = tok_dev // 2
+    attn = HEADS * HEAD_DIM
+    cols = attn // places
+    rows = places * tok_dev
+    share = width // places
+
+    slots = jnp.arange(2 * ctx_count)
+    inverse = jnp.sum(jnp.where(block_order[None, :] == slots[:, None], slots[None, :], 0), axis=1)
+    inverse = inverse.astype(jnp.int32)
+    valid = valid_mask.astype(f32).reshape(tok_dev, 1)
+
+    pair_rows = jnp.concatenate(
+        [
+            lax.dynamic_slice_in_dim(weight, here * 128, 128, 1)
+            for weight in (query_weight, key_weight, value_weight, relative_weight)
+        ],
+        axis=1,
+    )
+    gain_rows = jnp.stack([attention_gain, cross_gain, feedforward_gain]).astype(f32)
+    bias_rows = jnp.stack([content_bias, position_bias]).astype(f32)
+    gain_rows = jnp.concatenate(
+        [jnp.pad(gain_rows, ((0, 0), (0, cols - share))), bias_rows, jnp.zeros((3, cols), f32)], axis=0
+    )
+    count_row = jnp.broadcast_to(jnp.sum(valid), (8, 128))
+    tokens_all, count_all, (pair_cols, gains) = gather_all(
+        tokens[0], count_row, (pair_rows, gain_rows), 1
+    )
+    count = count_all[0:1, 0:1]
+    pair_cols = pair_cols.reshape(width, 512)
+    bias_all = gains[:, 3:5].transpose(1, 0, 2).reshape(2, attn)
+    gains = gains[:, :3, :share].transpose(1, 0, 2).reshape(3, width)
+    gain_one, gain_two, gain_three = gains[0:1], gains[1:2], gains[2:3]
+
+    cross_query_cols, cross_key_cols, cross_value_cols = [
+        take_columns(weight) for weight in (cross_query_weight, cross_key_weight, cross_value_weight)
+    ]
+    cross_pair_cols = jnp.concatenate([cross_key_cols, cross_value_cols], axis=1)
+    near_rows = jnp.concatenate(gather_parts(neighbours.reshape(-1, width)), axis=0)
+    up_cols = take_columns(up_weight)
+    qkv_rows = jnp.stack(
+        [weight.reshape(share, ctx_count, 128) for weight in (query_weight, key_weight, value_weight)],
+        axis=2,
+    ).reshape(share, 3 * attn)
+    qkv_full = lax.all_gather(qkv_rows, "wa", axis=0, tiled=True)
+
+    distance = (seq_len - 1 - jnp.arange(seq_len)).astype(f32)
+    waves = sinusoid(distance, width).astype(bf16)
+
+    hidden_all = tokens_all.reshape(seq_len, width).astype(f32)
+    normed_a = (hidden_all * inverse_rms(hidden_all) * gain_one).astype(bf16)
+    qkv = dot_nn(normed_a, pair_cols[:, :384]).astype(bf16)
+    table = dot_nn(waves, pair_cols[:, 384:]).astype(bf16)
+    table = jnp.concatenate([table, jnp.zeros((TILE, 128), bf16)], axis=0)
+    my_biases = lax.dynamic_slice_in_dim(bias_all, here * 128, 128, 1)
+    my_biases = jnp.concatenate([my_biases, jnp.zeros((6, 128), f32)], axis=0)
+    out = attend_forward(inverse, qkv, table, my_biases, block)
+    attended = swap_heads(out.reshape(ctx_count, tok_dev, 128), True, 2).reshape(rows, cols)
+
+    def to_owner(product):
+        return scatter_parts([product[r * tok_dev : (r + 1) * tok_dev] for r in range(places)])
+
+    def from_all(value):
+        return jnp.concatenate(gather_parts(value), axis=0)
+
+    hidden_in = tokens[0].astype(f32)
+    hidden_one = hidden_in + to_owner(dot_nn(attended, output_weight))
+
+    scale_two = inverse_rms(hidden_one)
+    normed_b = from_all((hidden_one * scale_two * gain_two).astype(bf16))
+    cross_q = dot_nn(normed_b, cross_query_cols).astype(bf16)
+    cross_pair = dot_nn(near_rows, cross_pair_cols).astype(bf16)
+    crossed = cross_forward(cross_q, cross_pair)
+    hidden_two = hidden_one + to_owner(dot_nn(crossed, cross_output_weight))
+
+    scale_three = inverse_rms(hidden_two)
+    normed_c = from_all((hidden_two * scale_three * gain_three).astype(bf16))
+    pre_act = dot_nn(normed_c, up_cols)
+    activated = gelu_tanh(pre_act).astype(bf16)
+    layer_out = hidden_two + to_owner(dot_nn(activated, down_weight))
+
+    error = layer_out - teacher[0].astype(f32)
+    error_sum = jnp.sum(valid * error * error)
+    out_grad = (places * seq_len) / count * valid * error
+
+    out_low = from_all(out_grad.astype(bf16))
+    act_grad = dot_nt(out_low, down_weight)
+    _, gelu_pull = jax.vjp(gelu_tanh, pre_act)
+    pre_grad = gelu_pull(act_grad)[0].astype(bf16)
+    down_grad = dot_tn(activated, out_low).astype(bf16)
+    up_grad = dot_tn(normed_c, pre_grad).astype(bf16)
+    normed_c_grad = to_owner(dot_nt(pre_grad, up_cols))
+    two_grad = out_grad + norm_pull(hidden_two, scale_three, gain_three, normed_c_grad)
+    gain_three_grad = jnp.sum(normed_c_grad * hidden_two * scale_three, axis=0)
+    down_out = sum_row_grads(down_grad)
+    up_out = sum_column_grads(up_grad[None])[0]
+
+    two_low = from_all(two_grad.astype(bf16))
+    crossed_grad = dot_nt(two_low, cross_output_weight).astype(bf16)
+    cross_q_grad, cross_pair_grad = cross_backward(cross_q, cross_pair, crossed_grad)
+    normed_b_grad = to_owner(dot_nt(cross_q_grad, cross_query_cols))
+    one_grad = two_grad + norm_pull(hidden_one, scale_two, gain_two, normed_b_grad)
+    gain_two_grad = jnp.sum(normed_b_grad * hidden_one * scale_two, axis=0)
+    cross_output_grad = dot_tn(crossed, two_low).astype(bf16)
+    cross_query_grad = dot_tn(normed_b, cross_q_grad).astype(bf16)
+    cross_key_grad = dot_tn(near_rows, cross_pair_grad[:, :cols]).astype(bf16)
+    cross_value_grad = dot_tn(near_rows, cross_pair_grad[:, cols:]).astype(bf16)
+    cross_output_out = sum_row_grads(cross_output_grad)
+    cross_out = sum_column_grads(jnp.stack([cross_key_grad, cross_value_grad]))
+    cross_query_out = sum_column_grads(cross_query_grad[None])[0]
+    near_grad = dot_nt(cross_pair_grad, cross_pair_cols)
+    near_count = near_rows.shape[0] // places
+    near_grad = scatter_parts(
+        [near_grad[r * near_count : (r + 1) * near_count] for r in range(places)]
+    )
+    neighbours_grad = near_grad.reshape(neighbours.shape)
+
+    one_low = from_all(one_grad.astype(bf16))
+    attended_grad = dot_nt(one_low, output_weight).astype(bf16)
+    output_grad = dot_tn(attended, one_low).astype(bf16)
+    output_out = sum_row_grads(output_grad)
+    grad = swap_heads(attended_grad.reshape(places, tok_dev, cols), False, 3)
+    qkv_grad, table_grad, bias_part = attend_backward(
+        inverse, qkv, table, my_biases, grad.reshape(seq_len, 128), block
+    )
+    table_high = table_grad.astype(bf16)
+    table_low = (table_grad - table_high.astype(f32)).astype(bf16)
+    relative_grad = dot_tn(waves, table_high) + dot_tn(waves, table_low)
+    pair_grad = jnp.concatenate([dot_tn(normed_a, qkv_grad), relative_grad], axis=1).astype(bf16)
+    pair_grad = pair_grad.reshape(places, share, 512)
+    for bit in reversed(bits_of("wa")):
+        keep, send = split(pair_grad, my_bit("wa", bit), 0)
+        pair_grad = (keep.astype(f32) + swap(send, "wa", bit).astype(f32)).astype(bf16)
+
+    mine = blocks_to_columns(qkv_grad.reshape(ctx_count, tok_dev, 384), 4)
+    normed_a_grad = dot_nt(mine, qkv_full)
+    scale_one = inverse_rms(hidden_in)
+    tokens_grad = one_grad + norm_pull(hidden_in, scale_one, gain_one, normed_a_grad)
+    gain_one_grad = jnp.sum(normed_a_grad * hidden_in * scale_one, axis=0)
+
+    pair_slots = jnp.arange(ctx_count)[:, None, None]
+    bias_slots = jnp.where(pair_slots == here, bias_part[None, 0:2], 0.0)
+    gain_grads = jnp.concatenate([gain_one_grad, gain_two_grad, gain_three_grad])
+    small = jnp.concatenate(
+        [
+            gain_grads.reshape(-1, 128),
+            bias_slots.reshape(-1, 128),
+            jnp.broadcast_to(error_sum, (3, 128)),
+        ],
+        axis=0,
+    )
+    pair_all, small, _ = gather_all(pair_grad[0], small, (), 5)
+    gain_count = gain_grads.shape[0] // 128
+    gain_out = small[:gain_count].reshape(3, width)
+    gain_out = lax.dynamic_slice_in_dim(gain_out, place * share, share, 1)
+    bias_out = small[gain_count : gain_count + 2 * ctx_count].reshape(ctx_count, 2, 128)
+    bias_out = lax.dynamic_slice_in_dim(bias_out, place * 2, 2, 0)
+    bias_out = bias_out.transpose(1, 0, 2).reshape(2, cols)
+    loss = small[gain_count + 2 * ctx_count, 0] / (2.0 * count[0, 0] * width)
+    whole = [
+        pair_all[:, :, 128 * m : 128 * (m + 1)].transpose(1, 0, 2).reshape(share, attn).astype(f32)
+        for m in range(4)
+    ]
+
+    return (
+        layer_out[None],
+        loss,
+        tokens_grad[None],
+        neighbours_grad,
+        whole[0],
+        whole[1],
+        whole[2],
+        output_out,
+        whole[3],
+        bias_out[0],
+        bias_out[1],
+        cross_query_out,
+        cross_out[0],
+        cross_out[1],
+        cross_output_out,
+        up_out,
+        down_out,
+        gain_out[0],
+        gain_out[1],
+        gain_out[2],
+    )
+
+
 def solution(mesh):
     row = P("wa", None)
     flat = P("wa")
@@ -952,4 +1495,6 @@
         flat,
         flat,
     )
+    by_heads = mesh.shape["ctx"] == 8 and mesh.shape["wa"] == 4
+    local = local_by_heads if by_heads else local_general
     return jax.shard_map(local, mesh=mesh, in_specs=in_specs, out_specs=out_specs, check_vma=False)

time: 617 us -> 603 us (0.977); the launches traced: 615 us -> 594 us
  Pallas kernels: 37.5 us -> 157 us
  starting transfers between devices: 145 us -> 64.9 us
  waiting for transfers between devices: 244 us -> 190 us
  blocking collectives: 14.9 us -> 0 us
  local copies, waits for them, and re-layouts: 39.9 us -> 54 us
  between operations: 12.5 us -> 19.8 us
  other arithmetic: 65.3 us -> 58.5 us
  matrix products: 55.5 us -> 49.3 us
    pallas_call x0 -> x5, Pallas kernels: none -> 122 us  [the longest x2 64.5 us: gather_all(): pl.pallas_call(functools.partial(gather_kernel, count), out_shape=[jax.Sh...]
    ppermute x123 -> x88, starting transfers between devices: 125 us -> 64.9 us  [swap(): return lax.ppermute(value, axis, pairs)]
    ppermute x123 -> x88, waiting for transfers between devices: 237 us -> 190 us  [swap(): return lax.ppermute(value, axis, pairs)]
    all_to_all x4 -> x0, starting transfers between devices: 19.7 us -> none  [the longest x1 6.43 us: local(): qkv = lax.all_to_all(qkv, 'ctx', split_axis=0, concat_axis=0, tiled=True)]
    all_gather x1 -> x0, blocking collectives: 14.9 us -> none  [local(): lax.all_gather(jnp.stack([attention_gain, cross_gain, feedforward_gain]),...]
    another operation x5 -> x8, local copies, waits for them, and re-layouts: 0.02 us -> 9.34 us  [the longest x3 6.05 us: local_by_heads(): jnp.stack([weight.reshape(share, ctx_count, 128) for weight in (query_wei...]
    all_to_all x4 -> x0, waiting for transfers between devices: 7.57 us -> none  [the longest x1 4.21 us: local(): lax.all_to_all(out.reshape(ctx_count, tok_dev, 128), 'ctx', split_axis=0,...]
    unnamed x175 -> x188, local copies, waits for them, and re-layouts: 5.17 us -> 11.8 us
  transfers between devices with their start and end apart: 127 -> 89, of which waited for: 58 -> 47; matrix products, arithmetic and copies ran while one was open for 24% -> 22% of each run, Pallas kernels for 6% -> 22%
where the time goes in v2:
time: 603 us; the launch traced here: 594 us
  waiting for transfers between devices  190 us (32%)
  Pallas kernels  157 us (26%)
  starting transfers between devices  64.9 us (11%)
  other arithmetic  58.5 us (10%)
  local copies, waits for them, and re-layouts  54 us (9%)
  matrix products  49.3 us (8%)
  between operations  19.8 us (3%)
    ppermute x88, waiting for transfers between devices, swap(): return lax.ppermute(value, axis, pairs)  190 us
    ppermute x88, starting transfers between devices, swap(): return lax.ppermute(value, axis, pairs)  64.9 us
    pallas_call x2, Pallas kernels, gather_all(): pl.pallas_call(functools.partial(gather_kernel, count), out_shape=[jax.Sh...  64.5 us
    pallas_call x2, Pallas kernels, swap_heads(): pl.pallas_call(functools.partial(swap_heads_kernel, outward), out_shape=j...  33.8 us
    pallas_call x1, Pallas kernels, blocks_to_columns(): pl.pallas_call(blocks_to_columns_kernel, out_shape=jax.ShapeDtypeStruct((...  23.6 us
    dot_general x7, matrix products, dot_nt(): lax.dot_general(a, b, (((1,), (1,)), ((), ())), preferred_element_type=f32)  17.2 us
    dot_general x8, matrix products, dot_nn(): lax.dot_general(a, b, (((1,), (0,)), ((), ())), preferred_element_type=f32)  16.2 us
    dot_general x10, matrix products, dot_tn(): lax.dot_general(a, b, (((0,), (0,)), ((), ())), preferred_element_type=f32)  16 us
  transfers between devices with their start and end apart: 89, of which 47 were waited for; matrix products, arithmetic and copies ran while one was open for 22% of the time, Pallas kernels for 22%

profile of v2, /device:TPU:0, one launch (start us, length us, event | category | flops | bytes accessed | tf_op | source)
XLA Modules:
  0.0 594.3 jit_solution(14486531754670124365)
XLA Ops:
  18.4 36.0 %gather_all.2 = (bf16[8,128,896]{2,1,0:T(8,128)(2,1)S(1)}, f32[8,128]{1,0:T(8,128)S(1)}, bf16[4,224,512]{2,1,0:T(8,128)(2,1)S(1)}, f32[4,8,256]{2,1,0:T(8,128)S(1)}) custom-call(bf16[128,896]{1,0:T(8,128)(2,1)S(1)} %bitcast.252, f32[8,128]{1,0:T(8,128)S(1)} %broadcast_in_dim.110.small_ref, bf16[224,512]{1,0:T(8,128)(2,1)S(1)} %pad_maximum_fusion.14.refs_0_, ...), custom_call_target="tpu_custom_call" | custom-call | tf_op jit(solution)/shard_map/gather_all/pallas_call | solution.py:631
  59.0 8.2 %fusion.2 = (bf16[1024,448]{1,0:T(8,128)(2,1)S(1)}, bf16[1024,448]{1,0:T(8,128)(2,1)S(1)}) fusion(f32[448]{0:T(512)S(1)} %multiply_exponential_fusion, f32[1024]{0:T(1024)S(1)} %subtract_convert_fusion.2), kind=kLoop, calls=%fused_computation.10 | loop fusion | flops 1376256 | bytes 1840896 | tf_op jit(solution)/shard_map/convert.30
  68.5 6.1 %attend_forward.1 = bf16[1024,128]{1,0:T(8,128)(2,1)S(1)} custom-call(s32[16]{0:T(128)S(1)} %select_reduce_fusion.order_ref, bf16[1024,384]{1,0:T(8,128)(2,1)S(1)} %convolution_convert_fusion.3.qkv_ref, bf16[1152,128]{1,0:T(8,128)(2,1)S(1)} %concatenate.922.rel_ref, f32[8,128]{1,0:T(8,128)S(1)} %concatenate.923.bias_ref), custom_call_target="tpu_custom_call" | custom-call | flops 2147483648 | bytes 1331200 | tf_op jit(solution)/shard_map/attend_forward/pallas_call | solution.py:313
  75.3 8.3 %swap_heads.2 = bf16[4,128,256]{2,1,0:T(8,128)(2,1)} custom-call(bf16[8,128,128]{2,1,0:T(8,128)(2,1)} %bitcast.255), custom_call_target="tpu_custom_call" | custom-call | tf_op jit(solution)/shard_map/swap_heads/pallas_call | solution.py:780
  88.5 4.8 collective-permute-start.6
  102.9 5.4 collective-permute-done.11
  119.8 7.0 %collective-permute-done.4 = bf16[128,896]{1,0:T(8,128)(2,1)S(1)} collective-permute-done((bf16[128,896]{1,0:T(8,128)(2,1)S(1)}, bf16[128,896]{1,0:T(8,128)(2,1)S(1)}, u32[]{:S(2)}, u32[]{:S(2)}) %collective-permute-start.4) | collective-permute-done | bytes 229408 | tf_op jit(solution)/shard_map/ppermute | solution.py:58
  130.3 5.1 convolution_convert_fusion.kv_ref
  135.5 7.5 %cross_forward.1 = bf16[512,256]{1,0:T(8,128)(2,1)} custom-call(bf16[512,256]{1,0:T(8,128)(2,1)} %convolution_convert_fusion.13.q_ref, bf16[2048,512]{1,0:T(8,128)(2,1)} %convolution_convert_fusion.kv_ref), custom_call_target="tpu_custom_call" | custom-call | flops 536870912 | bytes 2640000 | tf_op jit(solution)/shard_map/cross_forward/pallas_call | solution.py:407
  159.5 5.9 collective-permute-done.19
  173.5 5.4 collective-permute-done.25
  209.9 7.3 %collective-permute-done.31 = bf16[128,896]{1,0:T(8,128)(2,1)S(1)} collective-permute-done((bf16[128,896]{1,0:T(8,128)(2,1)S(1)}, bf16[128,896]{1,0:T(8,128)(2,1)S(1)}, u32[]{:S(2)}, u32[]{:S(2)}) %collective-permute-start.31) | collective-permute-done | bytes 229408 | tf_op jit(solution)/shard_map/ppermute | solution.py:58
  225.4 6.2 %collective-permute-done.33 = bf16[128,896]{1,0:T(8,128)(2,1)} collective-permute-done((bf16[128,896]{1,0:T(8,128)(2,1)}, bf16[128,896]{1,0:T(8,128)(2,1)}, u32[]{:S(2)}, u32[]{:S(2)}) %collective-permute-start.33) | collective-permute-done | bytes 229408 | tf_op jit(solution)/shard_map/ppermute | solution.py:58
  233.9 6.4 %collective-permute-done.82 = bf16[1,448,896]{2,1,0:T(8,128)(2,1)} collective-permute-done((bf16[1,448,896]{2,1,0:T(8,128)(2,1)}, bf16[1,448,896]{2,1,0:T(8,128)(2,1)}, u32[]{:S(2)}, u32[]{:S(2)}) %collective-permute-start.82) | collective-permute-done | bytes 802848 | tf_op jit(solution)/shard_map/ppermute | solution.py:58
  246.6 9.0 %cross_backward.1 = (bf16[512,256]{1,0:T(8,128)(2,1)}, bf16[2048,512]{1,0:T(8,128)(2,1)}) custom-call(bf16[512,256]{1,0:T(8,128)(2,1)} %convolution_convert_fusion.13.q_ref, bf16[2048,512]{1,0:T(8,128)(2,1)} %convolution_convert_fusion.kv_ref, bf16[512,256]{1,0:T(8,128)(2,1)} %convolution_convert_fusion.12.grad_ref), custom_call_target="tpu_custom_call" | custom-call | flops 1342177280 | bytes 5280000 | tf_op jit(solution)/shard_map/cross_backward/pallas_call | solution.py:426
  272.5 6.6 %collective-permute-done.68 = bf16[1,128,896]{2,1,0:T(8,128)(2,1)S(1)} collective-permute-done((bf16[1,128,896]{2,1,0:T(8,128)(2,1)S(1)}, bf16[1,128,896]{2,1,0:T(8,128)(2,1)S(1)}, u32[]{:S(2)}, u32[]{:S(2)}) %collective-permute-start.68) | collective-permute-done | bytes 229408 | tf_op jit(solution)/shard_map/ppermute | solution.py:58
  324.1 6.4 %collective-permute-done.76 = bf16[1,4,28,896]{3,2,1,0:T(8,128)(2,1)S(1)} collective-permute-done((bf16[1,4,28,896]{3,2,1,0:T(8,128)(2,1)S(1)}, bf16[1,4,28,896]{3,2,1,0:T(8,128)(2,1)S(1)}, u32[]{:S(2)}, u32[]{:S(2)}) %collective-permute-start.76) | collective-permute-done | bytes 200736 | tf_op jit(solution)/shard_map/ppermute | solution.py:58
  336.6 5.8 collective-permute-done.72
  344.2 4.8 collective-permute-done.58
  355.8 8.3 %collective-permute-done.85 = bf16[1,112,896]{2,1,0:T(8,128)(2,1)S(1)} collective-permute-done((bf16[1,112,896]{2,1,0:T(8,128)(2,1)S(1)}, bf16[1,112,896]{2,1,0:T(8,128)(2,1)S(1)}, u32[]{:S(2)}, u32[]{:S(2)}) %collective-permute-start.85) | collective-permute-done | bytes 200736 | tf_op jit(solution)/shard_map/ppermute | solution.py:58
  366.0 6.7 %collective-permute-done.62 = bf16[1,4,56,256]{3,2,1,0:T(8,128)(2,1)S(1)} collective-permute-done((bf16[1,4,56,256]{3,2,1,0:T(8,128)(2,1)S(1)}, bf16[1,4,56,256]{3,2,1,0:T(8,128)(2,1)S(1)}, u32[]{:S(2)}, u32[]{:S(2)}) %collective-permute-start.62) | collective-permute-done | bytes 114720 | tf_op jit(solution)/shard_map/ppermute | solution.py:58
  375.0 4.6 collective-permute-done.59
  383.5 9.8 %collective-permute-done.79 = bf16[1,28,3584]{2,1,0:T(8,128)(2,1)S(1)} collective-permute-done((bf16[1,28,3584]{2,1,0:T(8,128)(2,1)S(1)}, bf16[1,28,3584]{2,1,0:T(8,128)(2,1)S(1)}, u32[]{:S(2)}, u32[]{:S(2)}) %collective-permute-start.79) | collective-permute-done | bytes 200736 | tf_op jit(solution)/shard_map/ppermute | solution.py:58
  399.8 25.5 %swap_heads.3 = bf16[8,128,128]{2,1,0:T(8,128)(2,1)} custom-call(bf16[4,128,256]{2,1,0:T(8,128)(2,1)} %bitcast.313), custom_call_target="tpu_custom_call" | custom-call | tf_op jit(solution)/shard_map/swap_heads/pallas_call | solution.py:780
  426.3 13.1 %attend_backward.1 = (bf16[1024,384]{1,0:T(8,128)(2,1)S(1)}, f32[1024,128]{1,0:T(8,128)S(1)}, f32[8,128]{1,0:T(8,128)S(1)}) custom-call(s32[16]{0:T(128)S(1)} %select_reduce_fusion.order_ref, bf16[1024,384]{1,0:T(8,128)(2,1)S(1)} %convolution_convert_fusion.3.qkv_ref, bf16[1152,128]{1,0:T(8,128)(2,1)S(1)} %concatenate.922.rel_ref, ...), custom_call_target="tpu_custom_call" | custom-call | flops 5368709120 | bytes 3072000 | tf_op jit(solution)/shard_map/attend_backward/pallas_call | solution.py:329
  447.0 23.6 %blocks_to_columns.1 = bf16[128,3072]{1,0:T(8,128)(2,1)} custom-call(bf16[8,128,384]{2,1,0:T(8,128)(2,1)} %bitcast.253), custom_call_target="tpu_custom_call" | custom-call | tf_op jit(solution)/shard_map/blocks_to_columns/pallas_call | solution.py:826
  473.8 5.1 collective-permute-done.65
  491.1 6.0 %collective-permute-done.66 = bf16[2,56,1024]{2,1,0:T(8,128)(2,1)S(1)} collective-permute-done((bf16[2,56,1024]{2,1,0:T(8,128)(2,1)S(1)}, bf16[2,56,1024]{2,1,0:T(8,128)(2,1)S(1)}, u32[]{:S(2)}, u32[]{:S(2)}) %collective-permute-start.66) | collective-permute-done | bytes 229408 | tf_op jit(solution)/shard_map/ppermute | solution.py:58
  510.7 4.6 collective-permute-done.50
  533.0 8.7 %collective-permute-done.81 = bf16[1,112,3584]{2,1,0:T(8,128)(2,1)S(1)} collective-permute-done((bf16[1,112,3584]{2,1,0:T(8,128)(2,1)S(1)}, bf16[1,112,3584]{2,1,0:T(8,128)(2,1)S(1)}, u32[]{:S(2)}, u32[]{:S(2)}) %collective-permute-start.81) | collective-permute-done | bytes 802848 | tf_op jit(solution)/shard_map/ppermute | solution.py:58
  543.8 4.5 fusion.31
  549.4 28.5 %gather_all.3 = (bf16[8,224,512]{2,1,0:T(8,128)(2,1)S(1)}, f32[40,128]{1,0:T(8,128)S(1)}) custom-call(bf16[224,512]{1,0:T(8,128)(2,1)S(1)} %fusion.54.block_ref, f32[40,128]{1,0:T(8,128)S(1)} %concatenate.960.small_ref), custom_call_target="tpu_custom_call" | custom-call | tf_op jit(solution)/shard_map/gather_all/pallas_call | solution.py:631
  (557 shorter events, 273.2 us)
Async XLA Ops:
  7.2 536.6 %all-gather.2.cloned.1.call-start = ((), (), s32[]{:S(2)}) async-start(), calls=%async_computation | async-start | bytes 6881280 | tf_op jit(solution)/shard_map/all_gather | solution.py:1306
  7.3 111.3 %collective-permute-start.9 = (bf16[512,896]{1,0:T(8,128)(2,1)}, bf16[512,896]{1,0:T(8,128)(2,1)}, u32[]{:S(2)}, u32[]{:S(2)}) collective-permute-start(bf16[512,896]{1,0:T(8,128)(2,1)} %bitcast.339), channel_id=1, source_target_pairs={{0,2},{1,3},{2,0},{3,1},{4,6},{5,7},{6,4},{7,5},{8,10},{9,11},{10,... | collective-permute-start | bytes 2752520 | tf_op jit(solution)/shard_map/ppermute | solution.py:58
  10.3 119.1 %collective-permute-start.8 = (bf16[512,896]{1,0:T(8,128)(2,1)}, bf16[512,896]{1,0:T(8,128)(2,1)}, u32[]{:S(2)}, u32[]{:S(2)}) collective-permute-start(bf16[512,896]{1,0:T(8,128)(2,1)} %bitcast.340), channel_id=1, source_target_pairs={{0,1},{1,0},{2,3},{3,2},{4,5},{5,4},{6,7},{7,6},{8,9},{9,8},{10,11... | collective-permute-start | bytes 2752520 | tf_op jit(solution)/shard_map/ppermute | solution.py:58
  87.2 12.5 %collective-permute-start.1 = (bf16[128,896]{1,0:T(8,128)(2,1)}, bf16[128,896]{1,0:T(8,128)(2,1)}, u32[]{:S(2)}, u32[]{:S(2)}) collective-permute-start(bf16[128,896]{1,0:T(8,128)(2,1)} %get-tuple-element.82), channel_id=1, source_target_pairs={{0,1},{1,0},{2,3},{3,2},{4,5},{5,4},{6,7},{7,6},{8,9},{9,8},{10,11... | collective-permute-start | bytes 688136 | tf_op jit(solution)/shard_map/ppermute | solution.py:58
  87.4 25.9 %collective-permute-start = (bf16[128,896]{1,0:T(8,128)(2,1)}, bf16[128,896]{1,0:T(8,128)(2,1)}, u32[]{:S(2)}, u32[]{:S(2)}) collective-permute-start(bf16[128,896]{1,0:T(8,128)(2,1)} %get-tuple-element.81), channel_id=1, source_target_pairs={{0,1},{1,0},{2,3},{3,2},{4,5},{5,4},{6,7},{7,6},{8,9},{9,8},{10,11... | collective-permute-start | bytes 688136 | tf_op jit(solution)/shard_map/ppermute | solution.py:58
  126.8 23.6 %collective-permute-start.21 = (bf16[1,224,1792]{2,1,0:T(8,128)(2,1)}, bf16[1,224,1792]{2,1,0:T(8,128)(2,1)}, u32[]{:S(2)}, u32[]{:S(2)}) collective-permute-start(bf16[1,224,1792]{2,1,0:T(8,128)(2,1)} %get-tuple-element.72), channel_id=1, source_target_pairs={{0,2},{1,3},{2,0},{3,1},{4,6},{5,7},{6,4},{7,5},{8,10},{9,11},{10,... | collective-permute-start | bytes 2408456 | tf_op jit(solution)/shard_map/ppermute | solution.py:58
  152.7 12.7 %collective-permute-start.22 = (bf16[2,224,896]{2,1,0:T(8,128)(2,1)S(1)}, bf16[2,224,896]{2,1,0:T(8,128)(2,1)S(1)}, u32[]{:S(2)}, u32[]{:S(2)}) collective-permute-start(bf16[2,224,896]{2,1,0:T(8,128)(2,1)S(1)} %get-tuple-element.70), channel_id=1, source_target_pairs={{0,1},{1,0},{2,3},{3,2},{4,5},{5,4},{6,7},{7,6},{8,9},{9,8},{10,11... | collective-permute-start | bytes 2408456 | tf_op jit(solution)/shard_map/ppermute | solution.py:58
  203.1 28.5 %collective-permute-start.74 = (bf16[1,4,112,896]{3,2,1,0:T(8,128)(2,1)S(1)}, bf16[1,4,112,896]{3,2,1,0:T(8,128)(2,1)S(1)}, u32[]{:S(2)}, u32[]{:S(2)}) collective-permute-start(bf16[1,4,112,896]{3,2,1,0:T(8,128)(2,1)S(1)} %constant_dynamic-slice_fusion.5), channel_id=1, source_target_pairs={{0,4},{4,0},{8,12},{12,8},{16,20},{20,16},{24,28},{28,24},{1,5},{5... | collective-permute-start | bytes 2408456 | tf_op jit(solution)/shard_map/ppermute | solution.py:58
  204.2 13.0 %collective-permute-start.31 = (bf16[128,896]{1,0:T(8,128)(2,1)S(1)}, bf16[128,896]{1,0:T(8,128)(2,1)S(1)}, u32[]{:S(2)}, u32[]{:S(2)}) collective-permute-start(bf16[128,896]{1,0:T(8,128)(2,1)S(1)} %fusion.38), channel_id=1, source_target_pairs={{0,2},{1,3},{2,0},{3,1},{4,6},{5,7},{6,4},{7,5},{8,10},{9,11},{10,... | collective-permute-start | bytes 688136 | tf_op jit(solution)/shard_map/ppermute | solution.py:58
  208.8 31.6 %collective-permute-start.82 = (bf16[1,448,896]{2,1,0:T(8,128)(2,1)}, bf16[1,448,896]{2,1,0:T(8,128)(2,1)}, u32[]{:S(2)}, u32[]{:S(2)}) collective-permute-start(bf16[1,448,896]{2,1,0:T(8,128)(2,1)} %dynamic-slice_bitcast_fusion), channel_id=1, source_target_pairs={{0,4},{4,0},{8,12},{12,8},{16,20},{20,16},{24,28},{28,24},{1,5},{5... | collective-permute-start | bytes 2408456 | tf_op jit(solution)/shard_map/ppermute | solution.py:58
  218.6 13.0 %collective-permute-start.33 = (bf16[128,896]{1,0:T(8,128)(2,1)}, bf16[128,896]{1,0:T(8,128)(2,1)}, u32[]{:S(2)}, u32[]{:S(2)}) collective-permute-start(bf16[128,896]{1,0:T(8,128)(2,1)} %get-tuple-element.55), channel_id=1, source_target_pairs={{0,2},{1,3},{2,0},{3,1},{4,6},{5,7},{6,4},{7,5},{8,10},{9,11},{10,... | collective-permute-start | bytes 688136 | tf_op jit(solution)/shard_map/ppermute | solution.py:58
  225.4 17.6 %collective-permute-start.32 = (bf16[128,896]{1,0:T(8,128)(2,1)}, bf16[128,896]{1,0:T(8,128)(2,1)S(1)}, u32[]{:S(2)}, u32[]{:S(2)}) collective-permute-start(bf16[128,896]{1,0:T(8,128)(2,1)} %get-tuple-element.55), channel_id=1, source_target_pairs={{0,1},{1,0},{2,3},{3,2},{4,5},{5,4},{6,7},{7,6},{8,9},{9,8},{10,11... | collective-permute-start | bytes 688136 | tf_op jit(solution)/shard_map/ppermute | solution.py:58
  233.7 46.2 %collective-permute-start.75 = (bf16[1,4,56,896]{3,2,1,0:T(8,128)(2,1)}, bf16[1,4,56,896]{3,2,1,0:T(8,128)(2,1)}, u32[]{:S(2)}, u32[]{:S(2)}) collective-permute-start(bf16[1,4,56,896]{3,2,1,0:T(8,128)(2,1)} %constant_dynamic-slice_fusion.4), channel_id=1, source_target_pairs={{0,8},{4,12},{8,0},{12,4},{16,24},{20,28},{24,16},{28,20},{1,9},{5... | collective-permute-start | bytes 1204232 | tf_op jit(solution)/shard_map/ppermute | solution.py:58
  242.7 39.5 %collective-permute-start.83 = (bf16[1,224,896]{2,1,0:T(8,128)(2,1)}, bf16[1,224,896]{2,1,0:T(8,128)(2,1)}, u32[]{:S(2)}, u32[]{:S(2)}) collective-permute-start(bf16[1,224,896]{2,1,0:T(8,128)(2,1)} %constant_dynamic-slice_fusion.1), channel_id=1, source_target_pairs={{0,8},{4,12},{8,0},{12,4},{16,24},{20,28},{24,16},{28,20},{1,9},{5... | collective-permute-start | bytes 1204232 | tf_op jit(solution)/shard_map/ppermute | solution.py:58
  257.4 21.9 %collective-permute-start.36 = (bf16[128,896]{1,0:T(8,128)(2,1)S(1)}, bf16[128,896]{1,0:T(8,128)(2,1)S(1)}, u32[]{:S(2)}, u32[]{:S(2)}) collective-permute-start(bf16[128,896]{1,0:T(8,128)(2,1)S(1)} %get-tuple-element.74), channel_id=1, source_target_pairs={{0,1},{1,0},{2,3},{3,2},{4,5},{5,4},{6,7},{7,6},{8,9},{9,8},{10,11... | collective-permute-start | bytes 688136 | tf_op jit(solution)/shard_map/ppermute | solution.py:58
  257.4 56.0 %collective-permute-start.35 = (bf16[128,896]{1,0:T(8,128)(2,1)S(1)}, bf16[128,896]{1,0:T(8,128)(2,1)S(1)}, u32[]{:S(2)}, u32[]{:S(2)}) collective-permute-start(bf16[128,896]{1,0:T(8,128)(2,1)S(1)} %get-tuple-element.73), channel_id=1, source_target_pairs={{0,1},{1,0},{2,3},{3,2},{4,5},{5,4},{6,7},{7,6},{8,9},{9,8},{10,11... | collective-permute-start | bytes 688136 | tf_op jit(solution)/shard_map/ppermute | solution.py:58
  279.2 116.0 %collective-permute-start.44 = (bf16[512,896]{1,0:T(8,128)(2,1)S(1)}, bf16[512,896]{1,0:T(8,128)(2,1)S(1)}, u32[]{:S(2)}, u32[]{:S(2)}) collective-permute-start(bf16[512,896]{1,0:T(8,128)(2,1)S(1)} %get-tuple-element.62), channel_id=1, source_target_pairs={{0,1},{1,0},{2,3},{3,2},{4,5},{5,4},{6,7},{7,6},{8,9},{9,8},{10,11... | collective-permute-start | bytes 2752520 | tf_op jit(solution)/shard_map/ppermute | solution.py:58
  279.3 248.2 %collective-permute-start.43 = (bf16[512,896]{1,0:T(8,128)(2,1)}, bf16[512,896]{1,0:T(8,128)(2,1)}, u32[]{:S(2)}, u32[]{:S(2)}) collective-permute-start(bf16[512,896]{1,0:T(8,128)(2,1)} %get-tuple-element.61), channel_id=1, source_target_pairs={{0,1},{1,0},{2,3},{3,2},{4,5},{5,4},{6,7},{7,6},{8,9},{9,8},{10,11... | collective-permute-start | bytes 2752520 | tf_op jit(solution)/shard_map/ppermute | solution.py:58
  279.9 34.9 %collective-permute-start.37 = (bf16[128,896]{1,0:T(8,128)(2,1)S(1)}, bf16[128,896]{1,0:T(8,128)(2,1)S(1)}, u32[]{:S(2)}, u32[]{:S(2)}) collective-permute-start(bf16[128,896]{1,0:T(8,128)(2,1)S(1)} %fusion.36), channel_id=1, source_target_pairs={{0,2},{1,3},{2,0},{3,1},{4,6},{5,7},{6,4},{7,5},{8,10},{9,11},{10,... | collective-permute-start | bytes 688136 | tf_op jit(solution)/shard_map/ppermute | solution.py:58
  313.5 17.1 %collective-permute-start.76 = (bf16[1,4,28,896]{3,2,1,0:T(8,128)(2,1)S(1)}, bf16[1,4,28,896]{3,2,1,0:T(8,128)(2,1)S(1)}, u32[]{:S(2)}, u32[]{:S(2)}) collective-permute-start(bf16[1,4,28,896]{3,2,1,0:T(8,128)(2,1)S(1)} %constant_dynamic-slice_fusion.3), channel_id=1, source_target_pairs={{0,16},{4,20},{8,24},{12,28},{16,0},{20,4},{24,8},{28,12},{1,17},{... | collective-permute-start | bytes 602120 | tf_op jit(solution)/shard_map/ppermute | solution.py:58
  314.8 19.6 %collective-permute-start.84 = (bf16[1,112,896]{2,1,0:T(8,128)(2,1)S(1)}, bf16[1,112,896]{2,1,0:T(8,128)(2,1)S(1)}, u32[]{:S(2)}, u32[]{:S(2)}) collective-permute-start(bf16[1,112,896]{2,1,0:T(8,128)(2,1)S(1)} %constant_dynamic-slice_fusion), channel_id=1, source_target_pairs={{0,16},{4,20},{8,24},{12,28},{16,0},{20,4},{24,8},{28,12},{1,17},{... | collective-permute-start | bytes 602120 | tf_op jit(solution)/shard_map/ppermute | solution.py:58
  321.6 13.4 %collective-permute-start.57 = (bf16[1,28,1024]{2,1,0:T(8,128)(2,1)S(1)}, bf16[1,28,1024]{2,1,0:T(8,128)(2,1)S(1)}, u32[]{:S(2)}, u32[]{:S(2)}) collective-permute-start(bf16[1,28,1024]{2,1,0:T(8,128)(2,1)S(1)} %maximum_select_fusion.43), channel_id=1, source_target_pairs={{0,16},{4,20},{8,24},{12,28},{16,0},{20,4},{24,8},{28,12},{1,17},{... | collective-permute-start | bytes 172040 | tf_op jit(solution)/shard_map/ppermute | solution.py:58
  330.6 51.0 %collective-permute-start.39 = (bf16[128,896]{1,0:T(8,128)(2,1)S(1)}, bf16[128,896]{1,0:T(8,128)(2,1)S(1)}, u32[]{:S(2)}, u32[]{:S(2)}) collective-permute-start(bf16[128,896]{1,0:T(8,128)(2,1)S(1)} %get-tuple-element.53), channel_id=1, source_target_pairs={{0,2},{1,3},{2,0},{3,1},{4,6},{5,7},{6,4},{7,5},{8,10},{9,11},{10,... | collective-permute-start | bytes 688136 | tf_op jit(solution)/shard_map/ppermute | solution.py:58
  334.3 30.7 %collective-permute-start.61 = (bf16[2,4,56,256]{3,2,1,0:T(8,128)(2,1)S(1)}, bf16[2,4,56,256]{3,2,1,0:T(8,128)(2,1)S(1)}, u32[]{:S(2)}, u32[]{:S(2)}) collective-permute-start(bf16[2,4,56,256]{3,2,1,0:T(8,128)(2,1)S(1)} %constant_dynamic-slice_fusion.10), channel_id=1, source_target_pairs={{0,8},{4,12},{8,0},{12,4},{16,24},{20,28},{24,16},{28,20},{1,9},{5... | collective-permute-start | bytes 688136 | tf_op jit(solution)/shard_map/ppermute | solution.py:58
  374.0 23.2 %collective-permute-start.38 = (bf16[128,896]{1,0:T(8,128)(2,1)S(1)}, bf16[128,896]{1,0:T(8,128)(2,1)S(1)}, u32[]{:S(2)}, u32[]{:S(2)}) collective-permute-start(bf16[128,896]{1,0:T(8,128)(2,1)S(1)} %get-tuple-element.53), channel_id=1, source_target_pairs={{0,1},{1,0},{2,3},{3,2},{4,5},{5,4},{6,7},{7,6},{8,9},{9,8},{10,11... | collective-permute-start | bytes 688136 | tf_op jit(solution)/shard_map/ppermute | solution.py:58
  381.6 98.3 %collective-permute-start.86 = (bf16[1,224,896]{2,1,0:T(8,128)(2,1)}, bf16[1,224,896]{2,1,0:T(8,128)(2,1)}, u32[]{:S(2)}, u32[]{:S(2)}) collective-permute-start(bf16[1,224,896]{2,1,0:T(8,128)(2,1)} %maximum_select_fusion.22), channel_id=1, source_target_pairs={{0,8},{4,12},{8,0},{12,4},{16,24},{20,28},{24,16},{28,20},{1,9},{5... | collective-permute-start | bytes 1204232 | tf_op jit(solution)/shard_map/ppermute | solution.py:58
  395.1 50.9 %collective-permute-start.64 = (bf16[1,1,56,512]{3,2,1,0:T(8,128)(2,1)}, bf16[1,1,56,512]{3,2,1,0:T(8,128)(2,1)}, u32[]{:S(2)}, u32[]{:S(2)}) collective-permute-start(bf16[1,1,56,512]{3,2,1,0:T(8,128)(2,1)} %get-tuple-element.102), channel_id=1, source_target_pairs={{0,2},{1,3},{2,0},{3,1},{4,6},{5,7},{6,4},{7,5},{8,10},{9,11},{10,... | collective-permute-start | bytes 172040 | tf_op jit(solution)/shard_map/ppermute | solution.py:58
  397.1 101.1 %collective-permute-start.80 = (bf16[1,56,3584]{2,1,0:T(8,128)(2,1)}, bf16[1,56,3584]{2,1,0:T(8,128)(2,1)}, u32[]{:S(2)}, u32[]{:S(2)}) collective-permute-start(bf16[1,56,3584]{2,1,0:T(8,128)(2,1)} %maximum_select_fusion.20), channel_id=1, source_target_pairs={{0,8},{4,12},{8,0},{12,4},{16,24},{20,28},{24,16},{28,20},{1,9},{5... | collective-permute-start | bytes 1204232 | tf_op jit(solution)/shard_map/ppermute | solution.py:58
  397.1 130.4 %collective-permute-start.45 = (bf16[512,896]{1,0:T(8,128)(2,1)}, bf16[512,896]{1,0:T(8,128)(2,1)}, u32[]{:S(2)}, u32[]{:S(2)}) collective-permute-start(bf16[512,896]{1,0:T(8,128)(2,1)} %fusion.11), channel_id=1, source_target_pairs={{0,2},{1,3},{2,0},{3,1},{4,6},{5,7},{6,4},{7,5},{8,10},{9,11},{10,... | collective-permute-start | bytes 2752520 | tf_op jit(solution)/shard_map/ppermute | solution.py:58
  479.8 30.5 %collective-permute-start.41 = (bf16[2,224,512]{2,1,0:T(8,128)(2,1)S(1)}, bf16[2,224,512]{2,1,0:T(8,128)(2,1)S(1)}, u32[]{:S(2)}, u32[]{:S(2)}) collective-permute-start(bf16[2,224,512]{2,1,0:T(8,128)(2,1)S(1)} %fusion.32), channel_id=1, source_target_pairs={{0,2},{1,3},{2,0},{3,1},{4,6},{5,7},{6,4},{7,5},{8,10},{9,11},{10,... | collective-permute-start | bytes 1376264 | tf_op jit(solution)/shard_map/ppermute | solution.py:58
  497.2 33.8 %collective-permute-start.87 = (bf16[1,448,896]{2,1,0:T(8,128)(2,1)S(1)}, bf16[1,448,896]{2,1,0:T(8,128)(2,1)S(1)}, u32[]{:S(2)}, u32[]{:S(2)}) collective-permute-start(bf16[1,448,896]{2,1,0:T(8,128)(2,1)S(1)} %maximum_select_fusion.8), channel_id=1, source_target_pairs={{0,4},{4,0},{8,12},{12,8},{16,20},{20,16},{24,28},{28,24},{1,5},{5... | collective-permute-start | bytes 2408456 | tf_op jit(solution)/shard_map/ppermute | solution.py:58
  519.7 22.0 %collective-permute-start.81 = (bf16[1,112,3584]{2,1,0:T(8,128)(2,1)S(1)}, bf16[1,112,3584]{2,1,0:T(8,128)(2,1)S(1)}, u32[]{:S(2)}, u32[]{:S(2)}) collective-permute-start(bf16[1,112,3584]{2,1,0:T(8,128)(2,1)S(1)} %maximum_select_fusion.6), channel_id=1, source_target_pairs={{0,4},{4,0},{8,12},{12,8},{16,20},{20,16},{24,28},{28,24},{1,5},{5... | collective-permute-start | bytes 2408456 | tf_op jit(solution)/shard_map/ppermute | solution.py:58
  (151 other events, 1290.0 us)
Sparse Core Ops, SparseCore 0:
  194.8 49.3 all-gather.1

commit v3 on v2

--- a/solution.py
+++ b/solution.py
@@ -788,50 +788,883 @@
     )(value)
 
 
-def blocks_to_columns_kernel(in_ref, out_ref, send_sem, recv_sem):
-    c = lax.axis_index("ctx")
-    w = lax.axis_index("wa")
-    width = in_ref.shape[2]
+def gelu_slope(value):
+    inner = 0.7978845608028654 * (value + 0.044715 * value * value * value)
+    turned = jnp.tanh(inner)
+    slope = 0.7978845608028654 * (1.0 + 3.0 * 0.044715 * value * value)
+    return 0.5 * (1.0 + turned) + 0.5 * value * (1.0 - turned * turned) * slope
+
+
+def places_here():
+    return lax.axis_index("ctx"), lax.axis_index("wa")
+
+
+def meet_all():
+    c, w = places_here()
+    owner = c // 2
+    own = owner == w
     barrier = pltpu.get_barrier_semaphore()
     for j in range(1, 8):
         signal_to(barrier, c ^ j, w)
-    pl.semaphore_wait(barrier, 7)
+    for j in range(1, 4):
+        signal_to(barrier, c, w ^ j)
+    for j in range(1, 8):
+        signal_to(barrier, c ^ j, owner)
+    for r in range(4):
+        for h in range(2):
+
+            @pl.when(jnp.logical_not(jnp.logical_and(2 * w + h == c, r == 0)))
+            def _(r=r, h=h):
+                signal_to(barrier, 2 * w + h, w ^ r)
+
+    @pl.when(jnp.logical_not(own))
+    def _():
+        signal_to(barrier, c, owner)
+
+    pl.semaphore_wait(barrier, 26 - 2 * own.astype(jnp.int32))
+
+
+def meet_lines():
+    c, w = places_here()
+    barrier = pltpu.get_barrier_semaphore()
+    for j in range(1, 8):
+        signal_to(barrier, c ^ j, w)
+    for j in range(1, 4):
+        signal_to(barrier, c, w ^ j)
+    pl.semaphore_wait(barrier, 10)
+
+
+def remote(source, target, send, recv, ctx, wa):
+    return pltpu.make_async_remote_copy(
+        src_ref=source,
+        dst_ref=target,
+        send_sem=send,
+        recv_sem=recv,
+        device_id=(ctx, wa),
+        device_id_type=mesh_id,
+    )
+
+
+class GatherRows:
+
+    def __init__(self, buf, send, recv):
+        self.buf, self.send, self.recv = buf, send, recv
+        self.c, self.w = places_here()
+
+    def copy(self, k):
+        source, entry, j = ((0, 1, 1), (0, 2, 2), (2, 3, 1))[k]
+        return remote(
+            self.buf.at[source],
+            self.buf.at[entry],
+            self.send.at[k],
+            self.recv.at[k],
+            self.c,
+            self.w ^ j,
+        )
+
+    def start(self):
+        self.copy(1).start()
+        self.copy(0).start()
+
+    def near(self):
+        self.copy(0).wait()
+
+    def relay(self):
+        self.copy(1).wait()
+        self.copy(2).start()
+
+    def far(self):
+        self.copy(2).wait()
+
+
+class SumRows:
+
+    def __init__(self, out_buf, in_buf, send, recv):
+        self.out, self.inn, self.send, self.recv = out_buf, in_buf, send, recv
+        self.c, self.w = places_here()
+
+    def copy(self, k):
+        j = (1, 1, 2)[k]
+        return remote(
+            self.out.at[k], self.inn.at[k], self.send.at[k], self.recv.at[k], self.c, self.w ^ j
+        )
+
+    def give_near(self, value):
+        self.out[0] = value.astype(bf16)
+        self.copy(0).start()
+
+    def give_far(self, value):
+        self.out[1] = value.astype(bf16)
+        self.copy(1).start()
+
+    def pass_on(self, value):
+        self.copy(1).wait()
+        self.out[2] = (value + self.inn[1].astype(f32)).astype(bf16)
+        self.copy(2).start()
+
+    def total(self, value):
+        self.copy(0).wait()
+        value = value + self.inn[0].astype(f32)
+        self.copy(2).wait()
+        return value + self.inn[2].astype(f32)
+
+
+class CtxSum:
+
+    def __init__(self, send, recv, x=None, half=None, part=None, share=None, out=None, spread=0):
+        self.send, self.recv = send, recv
+        self.x, self.half, self.part, self.share, self.out = x, half, part, share, out
+        self.spread = spread
+        self.c, self.w = places_here()
+        self.z, self.y = self.c // 2, self.c % 2
+
+    def y_copy(self):
+        return remote(
+            self.x.at[:, 1 - self.y], self.half, self.send.at[0], self.recv.at[0], self.c ^ 1, self.w
+        )
+
+    def start_y(self):
+        self.y_copy().start()
+
+    def finish_y(self):
+        self.y_copy().wait()
+        for z in range(4):
+            mine = self.x[z, self.y].astype(f32)
+            self.half[z] = (self.half[z].astype(f32) + mine).astype(bf16)
+
+    def z_copy(self, j):
+        return remote(
+            self.half.at[self.z ^ j],
+            self.part.at[j - 1],
+            self.send.at[j],
+            self.recv.at[j],
+            self.c ^ (2 * j),
+            self.w,
+        )
+
+    def start_z(self):
+        for j in (2, 3, 1):
+            self.z_copy(j).start()
+
+    def finish_z(self):
+        total = self.half[self.z].astype(f32)
+        for j in (1, 2, 3):
+            self.z_copy(j).wait()
+            total = total + self.part[j - 1].astype(f32)
+        self.share[...] = total.astype(bf16)
+
+    def columns(self, place):
+        width = self.spread
+        return self.out.at[self.z, self.y, :, pl.ds(pl.multiple_of(place * width, 128), width)]
+
+    def wa_copy(self, j, place):
+        return remote(
+            self.share.at[self.w ^ j],
+            self.columns(place),
+            self.send.at[3 + j],
+            self.recv.at[3 + j],
+            self.c,
+            self.w ^ j,
+        )
+
+    def own_copy(self):
+        source = self.share.at[self.w] if self.spread else self.share
+        target = self.columns(self.w) if self.spread else self.out.at[self.z, self.y]
+        return pltpu.make_async_copy(source, target, self.send.at[11])
+
+    def start_wa(self):
+        if self.spread:
+            for j in (2, 3, 1):
+                self.wa_copy(j, self.w).start()
+        self.own_copy().start()
+
+    def finish_wa(self):
+        self.own_copy().wait()
+        if self.spread:
+            for j in (1, 2, 3):
+                self.wa_copy(j, self.w).wait_send()
+                self.wa_copy(j, self.w ^ j).wait_recv()
+
+    def back_z_copy(self, j, z):
+        mine = self.out.at[z, self.y]
+        return remote(mine, mine, self.send.at[6 + j], self.recv.at[6 + j], self.c ^ (2 * j), self.w)
+
+    def start_back_z(self):
+        for j in (2, 3, 1):
+            self.back_z_copy(j, self.z).start()
+
+    def finish_back_z(self):
+        for j in (1, 2, 3):
+            self.back_z_copy(j, self.z).wait_send()
+            self.back_z_copy(j, self.z ^ j).wait_recv()
+
+    def back_y_copy(self, y):
+        part = self.out.at[:, y]
+        return remote(part, part, self.send.at[10], self.recv.at[10], self.c ^ 1, self.w)
+
+    def start_back_y(self):
+        self.back_y_copy(self.y).start()
+
+    def finish_back_y(self):
+        self.back_y_copy(self.y).wait_send()
+        self.back_y_copy(1 - self.y).wait_recv()
+
+
+def put_shares(target, grads, first=0):
+    count = grads.shape[0] // 32
+    padded = target.shape[3]
+    for place in range(4):
+        for share in range(8):
+            start = (place * 8 + share) * count
+            part = grads[start : start + count]
+            part = jnp.concatenate([part, jnp.zeros((padded - count, part.shape[1]), f32)], axis=0)
+            target[share // 2, share % 2, place, :, first : first + part.shape[1]] = part.astype(bf16)
+
+
+def put_rows(target, grads):
+    count = grads.shape[0] // 8
+    for share in range(8):
+        target[share // 2, share % 2] = grads[share * count : (share + 1) * count].astype(bf16)
+
+
+def middle_back_kernel(
+    out_grad_ref,
+    down_ref,
+    pre_act_ref,
+    activated_ref,
+    normed_c_ref,
+    hidden_two_ref,
+    hidden_one_ref,
+    gains_ref,
+    up_any,
+    cross_out_any,
+    crossed_any,
+    cross_q_any,
+    cross_pair_any,
+    cross_query_any,
+    near_any,
+    normed_b_any,
+    output_any,
+    attended_any,
+    one_grad_ref,
+    gain_grad_ref,
+    heads_ref,
+    pair_grad_ref,
+    down_share,
+    up_share,
+    cross_half,
+    cross_out_x,
+    output_x,
+    up_ref,
+    cross_out_ref,
+    crossed_ref,
+    cross_q_ref,
+    cross_pair_ref,
+    cross_query_ref,
+    near_ref,
+    normed_b_ref,
+    output_ref,
+    attended_ref,
+    rows_ref,
+    rows_two_ref,
+    rows_one_ref,
+    pre_grad_ref,
+    query_grad_ref,
+    heads_out,
+    give_ref,
+    take_ref,
+    give_two_ref,
+    take_two_ref,
+    keep_ref,
+    down_x,
+    down_half,
+    down_part,
+    up_x,
+    up_half,
+    up_part,
+    cross_x,
+    load_sem,
+    g_send,
+    g_recv,
+    s_send,
+    s_recv,
+    h_send,
+    h_recv,
+    down_send,
+    down_recv,
+    up_send,
+    up_recv,
+    cross_send,
+    cross_recv,
+):
+    c, w = places_here()
+    tok = out_grad_ref.shape[0]
+    scale = HEAD_DIM ** (-0.5)
+    sources = (
+        up_any,
+        cross_out_any,
+        crossed_any,
+        cross_q_any,
+        cross_pair_any,
+        cross_query_any,
+        near_any,
+        normed_b_any,
+        output_any,
+        attended_any,
+    )
+    targets = (
+        up_ref,
+        cross_out_ref,
+        crossed_ref,
+        cross_q_ref,
+        cross_pair_ref,
+        cross_query_ref,
+        near_ref,
+        normed_b_ref,
+        output_ref,
+        attended_ref,
+    )
+    loads = [
+        pltpu.make_async_copy(source, target, load_sem.at[k])
+        for k, (source, target) in enumerate(zip(sources, targets))
+    ]
+    for load in loads:
+        load.start()
+    rows_ref[0] = out_grad_ref[...].astype(bf16)
+    meet_all()
+    first = GatherRows(rows_ref, g_send.at[0], g_recv.at[0])
+    second = GatherRows(rows_two_ref, g_send.at[1], g_recv.at[1])
+    third = GatherRows(rows_one_ref, g_send.at[2], g_recv.at[2])
+    sum_c = SumRows(give_ref, take_ref, s_send.at[0], s_recv.at[0])
+    sum_b = SumRows(give_two_ref, take_two_ref, s_send.at[1], s_recv.at[1])
+    down = CtxSum(down_send, down_recv, down_x, down_half, down_part, down_share)
+    up = CtxSum(up_send, up_recv, up_x, up_half, up_part, up_share)
+    cross = CtxSum(cross_send, cross_recv, cross_x, cross_half)
+
+    first.start()
+
+    def feed_back(r):
+        part = pl.ds(r * tok, tok)
+        act_grad = dot_nt(rows_ref[r], down_ref[...])
+        pre_grad_ref[part, :] = (act_grad * gelu_slope(pre_act_ref[part, :])).astype(bf16)
+        return dot_nt(pre_grad_ref[part, :], up_ref[...])
+
+    loads[0].wait()
+    keep_ref[0] = feed_back(0)
+    first.near()
+    sum_c.give_near(feed_back(1))
+    first.relay()
+    keep_ref[1] = feed_back(2)
+    first.far()
+    sum_c.give_far(feed_back(3))
+    sum_c.pass_on(keep_ref[1])
+    put_rows(down_x, dot_tn(activated_ref[...], rows_ref[...].reshape(4 * tok, -1)))
+    down.start_y()
+    put_shares(up_x, dot_tn(normed_c_ref[...], pre_grad_ref[...]))
+    for load in loads[1:]:
+        load.wait()
+    normed_grad = sum_c.total(keep_ref[0])
+    hidden = hidden_two_ref[...]
+    inverse = inverse_rms(hidden)
+    two_grad = out_grad_ref[...] + norm_pull(hidden, inverse, gains_ref[2:3, :], normed_grad)
+    gain_three = jnp.sum(normed_grad * hidden * inverse, axis=0, keepdims=True)
+    keep_ref[1] = two_grad
+    rows_two_ref[0] = two_grad.astype(bf16)
+
+    second.start()
+    width = cross_q_ref.shape[1]
+
+    def cross_back(r):
+        part = pl.ds(r * tok, tok)
+        crossed_grad = dot_nt(rows_two_ref[r], cross_out_ref[...]).astype(bf16)
+        for g in range(tok // GROUP):
+            at = r * tok + g * GROUP
+            near = (r * (tok // GROUP) + g) * NK
+            query = stack_all(cross_q_ref[at : at + GROUP, :])
+            grad = stack_all(crossed_grad[g * GROUP : (g + 1) * GROUP])
+            keys = cross_pair_ref[near : near + NK, 0:width]
+            shares = cross_shares(query, keys)
+            share_grad = dot_nt(grad, cross_pair_ref[near : near + NK, width:])
+            delta = jnp.sum(shares * share_grad, axis=1, keepdims=True)
+            score_grad = (shares * (share_grad - delta)).astype(bf16)
+            query_grad = join_all(dot_nn(score_grad, keys)) * scale
+            query_grad_ref[at : at + GROUP, :] = query_grad.astype(bf16)
+            pair_grad_ref[near : near + NK, 0:width] = (dot_tn(score_grad, query) * scale).astype(bf16)
+            pair_grad_ref[near : near + NK, width:] = dot_tn(shares.astype(bf16), grad).astype(bf16)
+        return dot_nt(query_grad_ref[part, :], cross_query_ref[...])
+
+    keep_ref[0] = cross_back(0)
+    second.near()
+    sum_b.give_near(cross_back(1))
+    second.relay()
+    keep_ref[2] = cross_back(2)
+    second.far()
+    sum_b.give_far(cross_back(3))
+    sum_b.pass_on(keep_ref[2])
+    down.finish_y()
+    down.start_z()
+    up.start_y()
+    normed_b = normed_b_ref[...]
+    put_rows(cross_out_x, dot_tn(crossed_ref[...], rows_two_ref[...].reshape(4 * tok, -1)))
+    put_shares(cross_x, dot_tn(normed_b, query_grad_ref[...]), 0)
+    normed_grad = sum_b.total(keep_ref[0])
+    hidden = hidden_one_ref[...]
+    inverse = inverse_rms(hidden)
+    one_grad = keep_ref[1] + norm_pull(hidden, inverse, gains_ref[1:2, :], normed_grad)
+    gain_two = jnp.sum(normed_grad * hidden * inverse, axis=0, keepdims=True)
+    gain_grad_ref[...] = jnp.concatenate(
+        [gain_two, gain_three, jnp.zeros((6, gain_two.shape[1]), f32)], axis=0
+    )
+    one_grad_ref[...] = one_grad
+    rows_one_ref[0] = one_grad.astype(bf16)
+
+    third.start()
+    put_shares(cross_x, dot_tn(near_ref[...], pair_grad_ref[...]), width)
+
+    def head_copy(r, h):
+        return remote(
+            heads_out.at[r, :, h * 128 : (h + 1) * 128],
+            heads_ref.at[c],
+            h_send.at[r * 2 + h],
+            h_recv.at[c],
+            2 * w + h,
+            w ^ r,
+        )
+
+    def head_back(r):
+        heads_out[r] = dot_nt(rows_one_ref[r], output_ref[...]).astype(bf16)
+        for h in range(2):
+            mine = jnp.logical_and(2 * w + h == c, r == 0)
+
+            @pl.when(jnp.logical_not(mine))
+            def _():
+                head_copy(r, h).start()
+
+            @pl.when(mine)
+            def _():
+                pltpu.make_async_copy(
+                    heads_out.at[r, :, h * 128 : (h + 1) * 128], heads_ref.at[c], h_recv.at[c]
+                ).start()
+
+    head_back(0)
+    third.near()
+    head_back(1)
+    third.relay()
+    head_back(2)
+    third.far()
+    head_back(3)
+    up.finish_y()
+    up.start_z()
+    cross.start_y()
+    put_rows(output_x, dot_tn(attended_ref[...], rows_one_ref[...].reshape(4 * tok, -1)))
+    for block in range(8):
+        remote(
+            heads_out.at[0, :, 0:128], heads_ref.at[block], h_send.at[0], h_recv.at[block], c ^ 1, w
+        ).wait_recv()
+    for r in range(4):
+        for h in range(2):
+
+            @pl.when(jnp.logical_not(jnp.logical_and(2 * w + h == c, r == 0)))
+            def _(r=r, h=h):
+                head_copy(r, h).wait_send()
+
+    down.finish_z()
+    up.finish_z()
+    cross.finish_y()
+
+
+def middle_back(
+    out_grad,
+    down_weight,
+    pre_act,
+    activated,
+    normed_c,
+    hidden_two,
+    hidden_one,
+    gains,
+    later,
+    collective_id,
+):
+    tok, width = out_grad.shape
+    hidden = down_weight.shape[0]
+    cols = later[3].shape[1]
+    near = later[6].shape[0]
+    any_space = pl.BlockSpec(memory_space=pl.ANY)
+    dma = pltpu.SemaphoreType.DMA
+    shape = jax.ShapeDtypeStruct
+    vmem = pltpu.VMEM
+    rows = -(-(width // 32) // 8) * 8
+    return pl.pallas_call(
+        middle_back_kernel,
+        out_shape=[
+            shape((tok, width), f32),
+            shape((8, width), f32),
+            shape((8, tok, 128), bf16),
+            shape((near, 2 * cols), bf16),
+            shape((hidden // 8, width), bf16),
+            shape((4, rows, hidden), bf16),
+            shape((4, 4, rows, 3 * cols), bf16),
+            shape((4, 2, cols // 8, width), bf16),
+            shape((4, 2, cols // 8, width), bf16),
+        ],
+        in_specs=[in_vmem] * 8 + [any_space] * 10,
+        out_specs=[in_vmem] * 9,
+        scratch_shapes=[vmem(value.shape, value.dtype) for value in later]
+        + [
+            vmem((4, tok, width), bf16),
+            vmem((4, tok, width), bf16),
+            vmem((4, tok, width), bf16),
+            vmem((4 * tok, hidden), bf16),
+            vmem((4 * tok, cols), bf16),
+            vmem((4, tok, cols), bf16),
+            vmem((3, tok, width), bf16),
+            vmem((3, tok, width), bf16),
+            vmem((3, tok, width), bf16),
+            vmem((3, tok, width), bf16),
+            vmem((3, tok, width), f32),
+            vmem((4, 2, hidden // 8, width), bf16),
+            vmem((4, hidden // 8, width), bf16),
+            vmem((3, hidden // 8, width), bf16),
+            vmem((4, 2, 4, rows, hidden), bf16),
+            vmem((4, 4, rows, hidden), bf16),
+            vmem((3, 4, rows, hidden), bf16),
+            vmem((4, 2, 4, rows, 3 * cols), bf16),
+            dma((10,)),
+            dma((3, 3)),
+            dma((3, 3)),
+            dma((2, 3)),
+            dma((2, 3)),
+            dma((8,)),
+            dma((8,)),
+            dma((12,)),
+            dma((12,)),
+            dma((12,)),
+            dma((12,)),
+            dma((12,)),
+            dma((12,)),
+        ],
+        compiler_params=pltpu.CompilerParams(
+            collective_id=collective_id, has_side_effects=True, vmem_limit_bytes=58 * 2**20
+        ),
+        name="middle_back",
+    )(out_grad, down_weight, pre_act, activated, normed_c, hidden_two, hidden_one, gains, *later)
+
+
+def finish_kernel(
+    query_grad_ref,
+    normed_a_ref,
+    waves_ref,
+    table_grad_ref,
+    small_ref,
+    pair_grad_ref,
+    pair_cols_ref,
+    down_share,
+    up_share,
+    cross_half,
+    cross_out_x,
+    output_x,
+    one_grad_ref,
+    tokens_ref,
+    gains_ref,
+    full_any,
+    tokens_grad_ref,
+    near_grad_ref,
+    total_ref,
+    down_out,
+    up_out,
+    cross_out,
+    cross_out_out,
+    output_out,
+    pair_out,
+    full_ref,
+    mine_ref,
+    sums_ref,
+    cross_part,
+    cross_share,
+    cross_out_half,
+    cross_out_part,
+    cross_out_share,
+    output_half,
+    output_part,
+    output_share,
+    pair_give,
+    pair_take,
+    pair_share,
+    near_give,
+    near_take,
+    near_keep,
+    near_sum,
+    far_sum,
+    load_sem,
+    b_send,
+    b_recv,
+    e_send,
+    e_recv,
+    n_send,
+    n_recv,
+    s_send,
+    s_recv,
+    chain_send,
+    chain_recv,
+):
+    c, w = places_here()
+    load = pltpu.make_async_copy(full_any, full_ref, load_sem)
+    load.start()
+    down = CtxSum(chain_send.at[0], chain_recv.at[0], share=down_share, out=down_out)
+    up = CtxSum(
+        chain_send.at[1], chain_recv.at[1], share=up_share, out=up_out, spread=up_share.shape[2]
+    )
+    cross = CtxSum(
+        chain_send.at[2],
+        chain_recv.at[2],
+        half=cross_half,
+        part=cross_part,
+        share=cross_share,
+        out=cross_out,
+        spread=cross_share.shape[2],
+    )
+    ctx_o = CtxSum(
+        chain_send.at[3],
+        chain_recv.at[3],
+        cross_out_x,
+        cross_out_half,
+        cross_out_part,
+        cross_out_share,
+        cross_out_out,
+    )
+    out_o = CtxSum(
+        chain_send.at[4],
+        chain_recv.at[4],
+        output_x,
+        output_half,
+        output_part,
+        output_share,
+        output_out,
+    )
+    pair = CtxSum(chain_send.at[5], chain_recv.at[5], share=pair_share, out=pair_out)
+    sum_pair = SumRows(pair_give, pair_take, e_send, e_recv)
+    sum_near = SumRows(near_give, near_take, n_send, n_recv)
+    width = query_grad_ref.shape[2]
 
     def columns(block):
-        return out_ref.at[:, pl.ds(pl.multiple_of(block * width, 128), width)]
-
-    def copy_to(j, block):
-        return pltpu.make_async_remote_copy(
-            src_ref=in_ref.at[c ^ j],
-            dst_ref=columns(block),
-            send_sem=send_sem.at[j],
-            recv_sem=recv_sem.at[j],
-            device_id=(c ^ j, w),
-            device_id_type=mesh_id,
+        return mine_ref.at[:, pl.ds(pl.multiple_of(block * width, 128), width)]
+
+    def block_copy(j, block):
+        return remote(
+            query_grad_ref.at[c ^ j], columns(block), b_send.at[j], b_recv.at[j], c ^ j, w
         )
 
+    meet_lines()
+    ctx_o.start_y()
+    out_o.start_y()
+    cross.start_z()
+    up.start_wa()
+    down.start_wa()
     for j in (4, 6, 5, 7, 2, 3, 1):
-        copy_to(j, c).start()
-    own = pltpu.make_async_copy(in_ref.at[c], columns(c), recv_sem.at[0])
+        block_copy(j, c).start()
+    own = pltpu.make_async_copy(query_grad_ref.at[c], columns(c), b_recv.at[0])
     own.start()
+
+    query_grad = query_grad_ref[...].reshape(-1, width)
+    high = table_grad_ref[...].astype(bf16)
+    low = (table_grad_ref[...] - high.astype(f32)).astype(bf16)
+    share = sums_ref.shape[1]
+    mixed = dot_tn(normed_a_ref[...], query_grad)
+    turned = dot_tn(waves_ref[...], high) + dot_tn(waves_ref[...], low)
+    for place in range(4):
+        at = place * share
+        sums_ref[place] = jnp.concatenate([mixed[at : at + share], turned[at : at + share]], axis=1)
+    sum_pair.give_far(sums_ref[w ^ 3])
+    sum_pair.give_near(sums_ref[w ^ 1])
+    down.finish_wa()
+    down.start_back_z()
+    up.finish_wa()
+    up.start_back_z()
+    ctx_o.finish_y()
+    ctx_o.start_z()
+    out_o.finish_y()
+    out_o.start_z()
+    sum_pair.pass_on(sums_ref[w ^ 2])
+
+    count = near_grad_ref.shape[0]
+
+    def near_part(r):
+        return dot_nt(pair_grad_ref[r * count : (r + 1) * count, :], pair_cols_ref[...])
+
+    sum_near.give_far(near_part(3))
+    sum_near.give_near(near_part(1))
+    cross.finish_z()
+    cross.start_wa()
+    pair_share[...] = sum_pair.total(sums_ref[w]).astype(bf16)
+    pair.start_wa()
+    pair.finish_wa()
+    pair.start_back_z()
+    sum_near.pass_on(near_part(2))
+    near_keep[...] = near_part(0)
+    ctx_o.finish_z()
+    ctx_o.start_wa()
+    out_o.finish_z()
+    out_o.start_wa()
+    cross.finish_wa()
+    cross.start_back_z()
+    ctx_o.finish_wa()
+    ctx_o.start_back_z()
+    out_o.finish_wa()
+    out_o.start_back_z()
+    down.finish_back_z()
+    down.start_back_y()
+
     for j in range(1, 8):
-        copy_to(j, c ^ j).wait_recv()
+        block_copy(j, c ^ j).wait_recv()
+    own.wait()
+    load.wait()
+    normed_grad = dot_nt(mine_ref[...], full_ref[...])
+    hidden = tokens_ref[...].astype(f32)
+    inverse = inverse_rms(hidden)
+    tokens_grad_ref[...] = one_grad_ref[...] + norm_pull(
+        hidden, inverse, gains_ref[0:1, :], normed_grad
+    )
+    gain_one = jnp.sum(normed_grad * hidden * inverse, axis=0, keepdims=True)
+    small_rows = small_ref.shape[0]
+    total_ref[...] = small_ref[...]
+    total_ref[small_rows - 8 : small_rows - 7, 0 : gain_one.shape[1]] = gain_one
+
+    def small_copy(source, k):
+        near = k < 3
+        j = k + 1 if near else k - 2
+        return remote(
+            source,
+            near_sum.at[k] if near else far_sum.at[k - 3],
+            s_send.at[k],
+            s_recv.at[k],
+            c if near else c ^ j,
+            w ^ j if near else w,
+        )
+
+    for k in range(3):
+        small_copy(total_ref, k).start()
+    up.finish_back_z()
+    up.start_back_y()
+    pair.finish_back_z()
+    pair.start_back_y()
+    near_grad_ref[...] = sum_near.total(near_keep[...])
+    for k in range(3):
+        small_copy(total_ref, k).wait()
+    total_ref[...] = tree_sum([total_ref[...]] + [near_sum[k] for k in range(3)])
+    for k in range(3, 10):
+        small_copy(total_ref, k).start()
+    cross.finish_back_z()
+    cross.start_back_y()
+    ctx_o.finish_back_z()
+    ctx_o.start_back_y()
+    out_o.finish_back_z()
+    out_o.start_back_y()
+    for k in range(3, 10):
+        small_copy(total_ref, k).wait()
+    total_ref[...] = tree_sum([total_ref[...]] + [far_sum[k] for k in range(7)])
     for j in range(1, 8):
-        copy_to(j, c).wait_send()
-    own.wait()
-
-
-def blocks_to_columns(value, collective_id):
-    blocks, rows, width = value.shape
+        block_copy(j, c).wait_send()
+    for chain in (down, up, pair, cross, ctx_o, out_o):
+        chain.finish_back_y()
+
+
+def finish(
+    query_grad,
+    normed_a,
+    waves,
+    table_grad,
+    small,
+    pair_grad,
+    pair_cols,
+    down_share,
+    up_share,
+    cross_half,
+    cross_out_x,
+    output_x,
+    one_grad,
+    tokens,
+    gains,
+    full,
+    collective_id,
+):
+    tok, width = tokens.shape
+    near = pair_grad.shape[0]
+    rows = up_share.shape[1]
+    cols = output_x.shape[2] * 8
+    share = width // 4
+    any_space = pl.BlockSpec(memory_space=pl.ANY)
+    dma = pltpu.SemaphoreType.DMA
+    shape = jax.ShapeDtypeStruct
+    vmem = pltpu.VMEM
     return pl.pallas_call(
-        blocks_to_columns_kernel,
-        out_shape=jax.ShapeDtypeStruct((rows, blocks * width), value.dtype),
-        in_specs=[in_vmem],
-        out_specs=in_vmem,
-        scratch_shapes=[pltpu.SemaphoreType.DMA((8,)), pltpu.SemaphoreType.DMA((8,))],
-        compiler_params=pltpu.CompilerParams(collective_id=collective_id, has_side_effects=True),
-        name="blocks_to_columns",
-    )(value)
+        finish_kernel,
+        out_shape=[
+            shape((tok, width), f32),
+            shape((near // 4, width), f32),
+            shape(small.shape, f32),
+            shape((4, 2) + down_share.shape, bf16),
+            shape((4, 2, rows, 4 * up_share.shape[2]), bf16),
+            shape((4, 2, rows, 12 * cols), bf16),
+            shape((4, 2, cols // 8, width), bf16),
+            shape((4, 2, cols // 8, width), bf16),
+            shape((4, 2, share, 512), bf16),
+        ],
+        in_specs=[in_vmem] * 15 + [any_space],
+        out_specs=[in_vmem] * 9,
+        scratch_shapes=[
+            vmem(full.shape, bf16),
+            vmem((tok, full.shape[1]), bf16),
+            vmem((4, share, 512), f32),
+            vmem((3, 4, rows, 3 * cols), bf16),
+            vmem((4, rows, 3 * cols), bf16),
+            vmem((4, cols // 8, width), bf16),
+            vmem((3, cols // 8, width), bf16),
+            vmem((cols // 8, width), bf16),
+            vmem((4, cols // 8, width), bf16),
+            vmem((3, cols // 8, width), bf16),
+            vmem((cols // 8, width), bf16),
+            vmem((3, share, 512), bf16),
+            vmem((3, share, 512), bf16),
+            vmem((share, 512), bf16),
+            vmem((3, near // 4, width), bf16),
+            vmem((3, near // 4, width), bf16),
+            vmem((near // 4, width), f32),
+            vmem((3,) + small.shape, f32),
+            vmem((7,) + small.shape, f32),
+            dma(()),
+            dma((8,)),
+            dma((8,)),
+            dma((3,)),
+            dma((3,)),
+            dma((3,)),
+            dma((3,)),
+            dma((10,)),
+            dma((10,)),
+            dma((6, 12)),
+            dma((6, 12)),
+        ],
+        compiler_params=pltpu.CompilerParams(
+            collective_id=collective_id, has_side_effects=True, vmem_limit_bytes=60 * 2**20
+        ),
+        name="finish",
+    )(
+        query_grad,
+        normed_a,
+        waves,
+        table_grad,
+        small,
+        pair_grad,
+        pair_cols,
+        down_share,
+        up_share,
+        cross_half,
+        cross_out_x,
+        output_x,
+        one_grad,
+        tokens,
+        gains,
+        full,
+    )
 
 
 def skew(wide, count):
@@ -1292,6 +2125,7 @@
     bias_all = gains[:, 3:5].transpose(1, 0, 2).reshape(2, attn)
     gains = gains[:, :3, :share].transpose(1, 0, 2).reshape(3, width)
     gain_one, gain_two, gain_three = gains[0:1], gains[1:2], gains[2:3]
+    gains_eight = jnp.pad(gains, ((0, 5), (0, 0)))
 
     cross_query_cols, cross_key_cols, cross_value_cols = [
         take_columns(weight) for weight in (cross_query_weight, cross_key_weight, cross_value_weight)
@@ -1344,83 +2178,95 @@
     error_sum = jnp.sum(valid * error * error)
     out_grad = (places * seq_len) / count * valid * error
 
-    out_low = from_all(out_grad.astype(bf16))
-    act_grad = dot_nt(out_low, down_weight)
-    _, gelu_pull = jax.vjp(gelu_tanh, pre_act)
-    pre_grad = gelu_pull(act_grad)[0].astype(bf16)
-    down_grad = dot_tn(activated, out_low).astype(bf16)
-    up_grad = dot_tn(normed_c, pre_grad).astype(bf16)
-    normed_c_grad = to_owner(dot_nt(pre_grad, up_cols))
-    two_grad = out_grad + norm_pull(hidden_two, scale_three, gain_three, normed_c_grad)
-    gain_three_grad = jnp.sum(normed_c_grad * hidden_two * scale_three, axis=0)
-    down_out = sum_row_grads(down_grad)
-    up_out = sum_column_grads(up_grad[None])[0]
-
-    two_low = from_all(two_grad.astype(bf16))
-    crossed_grad = dot_nt(two_low, cross_output_weight).astype(bf16)
-    cross_q_grad, cross_pair_grad = cross_backward(cross_q, cross_pair, crossed_grad)
-    normed_b_grad = to_owner(dot_nt(cross_q_grad, cross_query_cols))
-    one_grad = two_grad + norm_pull(hidden_one, scale_two, gain_two, normed_b_grad)
-    gain_two_grad = jnp.sum(normed_b_grad * hidden_one * scale_two, axis=0)
-    cross_output_grad = dot_tn(crossed, two_low).astype(bf16)
-    cross_query_grad = dot_tn(normed_b, cross_q_grad).astype(bf16)
-    cross_key_grad = dot_tn(near_rows, cross_pair_grad[:, :cols]).astype(bf16)
-    cross_value_grad = dot_tn(near_rows, cross_pair_grad[:, cols:]).astype(bf16)
-    cross_output_out = sum_row_grads(cross_output_grad)
-    cross_out = sum_column_grads(jnp.stack([cross_key_grad, cross_value_grad]))
-    cross_query_out = sum_column_grads(cross_query_grad[None])[0]
-    near_grad = dot_nt(cross_pair_grad, cross_pair_cols)
-    near_count = near_rows.shape[0] // places
-    near_grad = scatter_parts(
-        [near_grad[r * near_count : (r + 1) * near_count] for r in range(places)]
-    )
-    neighbours_grad = near_grad.reshape(neighbours.shape)
-
-    one_low = from_all(one_grad.astype(bf16))
-    attended_grad = dot_nt(one_low, output_weight).astype(bf16)
-    output_grad = dot_tn(attended, one_low).astype(bf16)
-    output_out = sum_row_grads(output_grad)
-    grad = swap_heads(attended_grad.reshape(places, tok_dev, cols), False, 3)
+    one_grad, gain_part, heads_grad, cross_pair_grad, down_share, up_share, cross_x, cross_o_x, output_x = (
+        middle_back(
+            out_grad,
+            down_weight,
+            pre_act,
+            activated,
+            normed_c,
+            hidden_two,
+            hidden_one,
+            gains_eight,
+            (
+                up_cols,
+                cross_output_weight,
+                crossed,
+                cross_q,
+                cross_pair,
+                cross_query_cols,
+                near_rows,
+                normed_b,
+                output_weight,
+                attended,
+            ),
+            3,
+        )
+    )
     qkv_grad, table_grad, bias_part = attend_backward(
-        inverse, qkv, table, my_biases, grad.reshape(seq_len, 128), block
-    )
-    table_high = table_grad.astype(bf16)
-    table_low = (table_grad - table_high.astype(f32)).astype(bf16)
-    relative_grad = dot_tn(waves, table_high) + dot_tn(waves, table_low)
-    pair_grad = jnp.concatenate([dot_tn(normed_a, qkv_grad), relative_grad], axis=1).astype(bf16)
-    pair_grad = pair_grad.reshape(places, share, 512)
-    for bit in reversed(bits_of("wa")):
-        keep, send = split(pair_grad, my_bit("wa", bit), 0)
-        pair_grad = (keep.astype(f32) + swap(send, "wa", bit).astype(f32)).astype(bf16)
-
-    mine = blocks_to_columns(qkv_grad.reshape(ctx_count, tok_dev, 384), 4)
-    normed_a_grad = dot_nt(mine, qkv_full)
-    scale_one = inverse_rms(hidden_in)
-    tokens_grad = one_grad + norm_pull(hidden_in, scale_one, gain_one, normed_a_grad)
-    gain_one_grad = jnp.sum(normed_a_grad * hidden_in * scale_one, axis=0)
+        inverse, qkv, table, my_biases, heads_grad.reshape(seq_len, 128), block
+    )
 
     pair_slots = jnp.arange(ctx_count)[:, None, None]
     bias_slots = jnp.where(pair_slots == here, bias_part[None, 0:2], 0.0)
-    gain_grads = jnp.concatenate([gain_one_grad, gain_two_grad, gain_three_grad])
     small = jnp.concatenate(
         [
-            gain_grads.reshape(-1, 128),
-            bias_slots.reshape(-1, 128),
-            jnp.broadcast_to(error_sum, (3, 128)),
+            jnp.pad(gain_part[2:3], ((0, 0), (0, attn - width))),
+            jnp.pad(gain_part[0:2], ((0, 0), (0, attn - width))),
+            bias_slots.reshape(2, attn),
+            jnp.broadcast_to(error_sum, (3, attn)),
         ],
         axis=0,
     )
-    pair_all, small, _ = gather_all(pair_grad[0], small, (), 5)
-    gain_count = gain_grads.shape[0] // 128
-    gain_out = small[:gain_count].reshape(3, width)
-    gain_out = lax.dynamic_slice_in_dim(gain_out, place * share, share, 1)
-    bias_out = small[gain_count : gain_count + 2 * ctx_count].reshape(ctx_count, 2, 128)
-    bias_out = lax.dynamic_slice_in_dim(bias_out, place * 2, 2, 0)
+    (
+        tokens_grad,
+        near_grad,
+        small,
+        down_out,
+        up_out,
+        cross_out,
+        cross_output_out,
+        output_out,
+        pair_all,
+    ) = finish(
+        qkv_grad.reshape(ctx_count, tok_dev, 384),
+        normed_a,
+        waves,
+        table_grad,
+        small,
+        cross_pair_grad,
+        cross_pair_cols,
+        down_share,
+        up_share,
+        cross_x,
+        cross_o_x,
+        output_x,
+        one_grad,
+        tokens[0],
+        gains_eight,
+        qkv_full,
+        4,
+    )
+    neighbours_grad = near_grad.reshape(neighbours.shape)
+    gain_out = lax.dynamic_slice_in_dim(small[0:3], place * share, share, 1)
+    bias_out = lax.dynamic_slice_in_dim(
+        small[3:5].reshape(ctx_count, 2, 128), place * 2, 2, 0
+    )
     bias_out = bias_out.transpose(1, 0, 2).reshape(2, cols)
-    loss = small[gain_count + 2 * ctx_count, 0] / (2.0 * count[0, 0] * width)
+    loss = small[5, 0] / (2.0 * count[0, 0] * width)
+    pair_all = pair_all.reshape(ctx_count, share, 512)
     whole = [
         pair_all[:, :, 128 * m : 128 * (m + 1)].transpose(1, 0, 2).reshape(share, attn).astype(f32)
         for m in range(4)
+    ]
+    down_out = down_out.reshape(down_weight.shape).astype(f32)
+    cross_output_out = cross_output_out.reshape(cols, width).astype(f32)
+    output_out = output_out.reshape(cols, width).astype(f32)
+    used = share // ctx_count
+    up_out = up_out.reshape(ctx_count, -1, up_out.shape[-1])[:, :used].reshape(share, -1).astype(f32)
+    cross_out = cross_out.reshape(ctx_count, -1, places, 3 * cols)[:, :used]
+    cross_query_out, *cross_out = [
+        cross_out[..., m * cols : (m + 1) * cols].reshape(share, attn).astype(f32) for m in range(3)
     ]
 
     return (

time: 603 us -> 553 us (0.917)
  Pallas kernels: 157 us -> 354 us
  waiting for transfers between devices: 190 us -> 47.6 us
  starting transfers between devices: 64.9 us -> 16.1 us
  matrix products: 49.3 us -> 17.2 us
  other arithmetic: 58.5 us -> 46.1 us
  local copies, waits for them, and re-layouts: 54 us -> 46.1 us
    pallas_call x2, Pallas kernels: 32.6 us -> 283 us  [the longest x1 194 us: finish(): pl.pallas_call(finish_kernel, out_shape=[shape((tok, width), f32), shape(...]
    ppermute x88 -> x26, waiting for transfers between devices: 190 us -> 47.6 us  [swap(): return lax.ppermute(value, axis, pairs)]
    ppermute x88 -> x26, starting transfers between devices: 64.9 us -> 16 us  [swap(): return lax.ppermute(value, axis, pairs)]
    dot_general x17 -> x0, matrix products: 33.1 us -> none  [the longest x7 17.2 us: dot_nt(): lax.dot_general(a, b, (((1,), (1,)), ((), ())), preferred_element_type=f32)]
    pallas_call x2 -> x1, Pallas kernels: 64.5 us -> 36 us  [gather_all(): pl.pallas_call(functools.partial(gather_kernel, count), out_shape=[jax.Sh...]
    pallas_call x2 -> x1, Pallas kernels: 33.8 us -> 8.31 us  [swap_heads(): pl.pallas_call(functools.partial(swap_heads_kernel, outward), out_shape=j...]
    concatenate x1 -> x6, other arithmetic: 0.04 us -> 12.4 us  [the longest x1 8.11 us: local_by_heads(): jnp.concatenate(gather_parts(neighbours.reshape(-1, width)), axis=0)]
    select_n x37 -> x7, other arithmetic: 13.6 us -> 5.79 us  [ordered(): jnp.where(bit == 0, jnp.concatenate([own, other], axis=dim), jnp.concaten...]
  transfers between devices with their start and end apart: 89 -> 27, of which waited for: 47 -> 8; matrix products, arithmetic and copies ran while one was open for 22% -> 14% of each run, Pallas kernels for 22% -> 29%
where the time goes in v3:
time: 553 us; the launch traced here: 545 us
  Pallas kernels  354 us (64%)
  waiting for transfers between devices  47.6 us (9%)
  local copies, waits for them, and re-layouts  46.1 us (8%)
  other arithmetic  46.1 us (8%)
  between operations  18.1 us (3%)
  matrix products  17.2 us (3%)
  starting transfers between devices  16.1 us (3%)
    pallas_call x1, Pallas kernels, finish(): pl.pallas_call(finish_kernel, out_shape=[shape((tok, width), f32), shape(...  194 us
    pallas_call x1, Pallas kernels, middle_back(): pl.pallas_call(middle_back_kernel, out_shape=[shape((tok, width), f32), s...  89 us
    ppermute x26, waiting for transfers between devices, swap(): return lax.ppermute(value, axis, pairs)  47.6 us
    pallas_call x1, Pallas kernels, gather_all(): pl.pallas_call(functools.partial(gather_kernel, count), out_shape=[jax.Sh...  36 us
    dot_general x8, matrix products, dot_nn(): lax.dot_general(a, b, (((1,), (0,)), ((), ())), preferred_element_type=f32)  17.2 us
    ppermute x26, starting transfers between devices, swap(): return lax.ppermute(value, axis, pairs)  16 us
    pallas_call x1, Pallas kernels, attend_backward(): pl.pallas_call(functools.partial(attend_backward_kernel, rows, block), ou...  13.3 us
    unnamed x93, local copies, waits for them, and re-layouts  11.3 us
  transfers between devices with their start and end apart: 27, of which 8 were waited for; matrix products, arithmetic and copies ran while one was open for 14% of the time, Pallas kernels for 29%

profile of v3, /device:TPU:0, one launch (start us, length us, event | category | flops | bytes accessed | tf_op | source)
XLA Modules:
  0.0 545.0 jit_solution(5111769233390058557)
XLA Ops:
  7.2 3.0 collective-permute-start.9
  18.3 36.0 %gather_all.1 = (bf16[8,128,896]{2,1,0:T(8,128)(2,1)S(1)}, f32[8,128]{1,0:T(8,128)S(1)}, bf16[4,224,512]{2,1,0:T(8,128)(2,1)S(1)}, f32[4,8,256]{2,1,0:T(8,128)S(1)}) custom-call(bf16[128,896]{1,0:T(8,128)(2,1)S(1)} %bitcast.147, f32[8,128]{1,0:T(8,128)S(1)} %broadcast_in_dim.97.small_ref, bf16[224,512]{1,0:T(8,128)(2,1)S(1)} %pad_maximum_fusion.6.refs_0_, ...), custom_call_target="tpu_custom_call" | custom-call | tf_op jit(solution)/shard_map/gather_all/pallas_call | solution.py:631
  56.7 8.1 %fusion.2 = (bf16[1024,448]{1,0:T(8,128)(2,1)S(1)}, bf16[1024,448]{1,0:T(8,128)(2,1)S(1)}) fusion(f32[448]{0:T(512)S(1)} %multiply_exponential_fusion, f32[1024]{0:T(1024)S(1)} %subtract_convert_fusion), kind=kLoop, calls=%fused_computation.9 | loop fusion | flops 1376256 | bytes 1840896 | tf_op jit(solution)/shard_map/convert.25
  66.7 6.1 %attend_forward.1 = bf16[1024,128]{1,0:T(8,128)(2,1)S(1)} custom-call(s32[16]{0:T(128)S(1)} %select_reduce_fusion.order_ref, bf16[1024,384]{1,0:T(8,128)(2,1)S(1)} %convolution_convert_fusion.1.qkv_ref, bf16[1152,128]{1,0:T(8,128)(2,1)S(1)} %concatenate.162.rel_ref, f32[8,128]{1,0:T(8,128)S(1)} %concatenate.163.bias_ref), custom_call_target="tpu_custom_call" | custom-call | flops 2147483648 | bytes 1331200 | tf_op jit(solution)/shard_map/attend_forward/pallas_call | solution.py:313
  73.5 8.3 %swap_heads.1 = bf16[4,128,256]{2,1,0:T(8,128)(2,1)} custom-call(bf16[8,128,128]{2,1,0:T(8,128)(2,1)} %bitcast.149), custom_call_target="tpu_custom_call" | custom-call | tf_op jit(solution)/shard_map/swap_heads/pallas_call | solution.py:780
  81.9 2.7 fusion.44
  85.8 1.8 dynamic-slice_bitcast_fusion.15
  87.5 4.8 collective-permute-start.6
  94.0 1.4 pad_maximum_fusion.2
  95.4 2.6 copy.62
  99.8 2.7 dynamic-slice_bitcast_fusion.3
  103.7 2.1 collective-permute-start.13
  105.8 10.1 %collective-permute-done.11 = bf16[1,224,512]{2,1,0:T(8,128)(2,1)S(1)} collective-permute-done((bf16[1,224,512]{2,1,0:T(8,128)(2,1)S(1)}, bf16[1,224,512]{2,1,0:T(8,128)(2,1)S(1)}, u32[]{:S(2)}, u32[]{:S(2)}) %collective-permute-start.11) | collective-permute-done | bytes 229408 | tf_op jit(solution)/shard_map/ppermute | solution.py:58
  117.2 8.6 %collective-permute-done.13 = bf16[1,224,512]{2,1,0:T(8,128)(2,1)S(1)} collective-permute-done((bf16[1,224,512]{2,1,0:T(8,128)(2,1)}, bf16[1,224,512]{2,1,0:T(8,128)(2,1)S(1)}, u32[]{:S(2)}, u32[]{:S(2)}) %collective-permute-start.13) | collective-permute-done | bytes 229408 | tf_op jit(solution)/shard_map/ppermute | solution.py:58
  126.5 7.8 %collective-permute-done.2 = bf16[128,896]{1,0:T(8,128)(2,1)S(1)} collective-permute-done((bf16[128,896]{1,0:T(8,128)(2,1)S(1)}, bf16[128,896]{1,0:T(8,128)(2,1)S(1)}, u32[]{:S(2)}, u32[]{:S(2)}) %collective-permute-start.2) | collective-permute-done | bytes 229408 | tf_op jit(solution)/shard_map/ppermute | solution.py:58
  136.7 12.4 %collective-permute-done.4 = bf16[128,896]{1,0:T(8,128)(2,1)S(1)} collective-permute-done((bf16[128,896]{1,0:T(8,128)(2,1)S(1)}, bf16[128,896]{1,0:T(8,128)(2,1)S(1)}, u32[]{:S(2)}, u32[]{:S(2)}) %collective-permute-start.4) | collective-permute-done | bytes 229408 | tf_op jit(solution)/shard_map/ppermute | solution.py:58
  152.7 5.2 convolution_convert_fusion.kv_ref.cross_pair_any
  157.9 7.6 %cross_forward.1.crossed_any = bf16[512,256]{1,0:T(8,128)(2,1)} custom-call(bf16[512,256]{1,0:T(8,128)(2,1)} %convolution_convert_fusion.3.q_ref.cross_q_any, bf16[2048,512]{1,0:T(8,128)(2,1)} %convolution_convert_fusion.kv_ref.cross_pair_any), custom_call_target="tpu_custom_call" | custom-call | flops 536870912 | bytes 2640000 | tf_op jit(solution)/shard_map/cross_forward/pallas_call | solution.py:407
  165.4 2.6 fusion.45
  171.6 2.2 maximum_select_fusion
  173.7 1.3 dynamic-slice_bitcast_fusion.1
  175.1 3.3 collective-permute-done.17
  183.4 3.3 collective-permute-done.19
  186.7 2.2 maximum_select_fusion.1
  189.0 2.6 fusion.11
  196.6 8.1 %pad_maximum_fusion.near_any = bf16[2048,896]{1,0:T(8,128)(2,1)} fusion(bf16[512,896]{1,0:T(8,128)(2,1)S(1)} %copy-done.25, bf16[512,896]{1,0:T(8,128)(2,1)} %collective-permute-done.9, bf16[512,896]{1,0:T(8,128)(2,1)} %collective-permute-done.8, bf16[512,896]{1,0:T(8,128)(2,1)S(1)} %bitcast.177), kind=kLoop, calls=%fused_computation | loop fusion | flops 14680064 | bytes 7340032 | tf_op jit(solution)/shard_map/concatenate | solution.py:2134
  207.5 89.0 %middle_back.1 = (f32[128,896]{1,0:T(8,128)}, f32[8,896]{1,0:T(8,128)}, bf16[8,128,128]{2,1,0:T(8,128)(2,1)}, bf16[2048,512]{1,0:T(8,128)(2,1)}, bf16[112,896]{1...) custom-call(f32[128,896]{1,0:T(8,128)} %fusion.23.out_grad_ref, ...), custom_call_target="tpu_custom_call" | custom-call | tf_op jit(solution)/shard_map/middle_back/pallas_call | solution.py:1297
  299.0 13.3 %attend_backward.1 = (bf16[1024,384]{1,0:T(8,128)(2,1)S(1)}, f32[1024,128]{1,0:T(8,128)S(1)}, f32[8,128]{1,0:T(8,128)S(1)}) custom-call(s32[16]{0:T(128)S(1)} %select_reduce_fusion.order_ref, bf16[1024,384]{1,0:T(8,128)(2,1)S(1)} %convolution_convert_fusion.1.qkv_ref, bf16[1152,128]{1,0:T(8,128)(2,1)S(1)} %concatenate.162.rel_ref, ...), custom_call_target="tpu_custom_call" | custom-call | flops 5368709120 | bytes 3072000 | tf_op jit(solution)/shard_map/attend_backward/pallas_call | solution.py:329
  315.4 193.6 %finish.1 = (f32[128,896]{1,0:T(8,128)}, f32[512,896]{1,0:T(8,128)}, f32[8,1024]{1,0:T(8,128)}, bf16[4,2,112,896]{3,2,1,0:T(8,128)(2,1)}, bf16[4,2,32,3584]{3,2,...) custom-call(bf16[8,128,384]{2,1,0:T(8,128)(2,1)} %bitcast.148, ...), custom_call_target="tpu_custom_call" | custom-call | tf_op jit(solution)/shard_map/finish/pallas_call | solution.py:1599
  511.7 3.7 slice_convert_fusion
  515.5 3.5 reshape.544
  528.8 2.0 bitcast_convert_fusion
  (235 shorter events, 64.8 us)
Async XLA Ops:
  7.2 308.3 %all-gather.2.cloned.1.call-start = ((), (), s32[]{:S(2)}) async-start(), calls=%async_computation | async-start | bytes 6881280 | tf_op jit(solution)/shard_map/all_gather | solution.py:2140
  7.2 128.4 %collective-permute-start.9 = (bf16[512,896]{1,0:T(8,128)(2,1)}, bf16[512,896]{1,0:T(8,128)(2,1)}, u32[]{:S(2)}, u32[]{:S(2)}) collective-permute-start(bf16[512,896]{1,0:T(8,128)(2,1)} %bitcast.174), channel_id=1, source_target_pairs={{0,2},{1,3},{2,0},{3,1},{4,6},{5,7},{6,4},{7,5},{8,10},{9,11},{10,... | collective-permute-start | bytes 2752520 | tf_op jit(solution)/shard_map/ppermute | solution.py:58
  10.2 141.5 %collective-permute-start.8 = (bf16[512,896]{1,0:T(8,128)(2,1)}, bf16[512,896]{1,0:T(8,128)(2,1)}, u32[]{:S(2)}, u32[]{:S(2)}) collective-permute-start(bf16[512,896]{1,0:T(8,128)(2,1)} %bitcast.175), channel_id=1, source_target_pairs={{0,1},{1,0},{2,3},{3,2},{4,5},{5,4},{6,7},{7,6},{8,9},{9,8},{10,11... | collective-permute-start | bytes 2752520 | tf_op jit(solution)/shard_map/ppermute | solution.py:58
  66.7 15.1 %copy-start.17 = (bf16[256,896]{1,0:T(8,128)(2,1)S(1)}, bf16[256,896]{1,0:T(8,128)(2,1)}, u32[]{:S(2)}) copy-start(bf16[256,896]{1,0:T(8,128)(2,1)} %output_any.1) | copy-start | bytes 1376260
  85.3 17.3 %collective-permute-start.1 = (bf16[128,896]{1,0:T(8,128)(2,1)}, bf16[128,896]{1,0:T(8,128)(2,1)S(1)}, u32[]{:S(2)}, u32[]{:S(2)}) collective-permute-start(bf16[128,896]{1,0:T(8,128)(2,1)} %get-tuple-element.95), channel_id=1, source_target_pairs={{0,1},{1,0},{2,3},{3,2},{4,5},{5,4},{6,7},{7,6},{8,9},{9,8},{10,11... | collective-permute-start | bytes 688136 | tf_op jit(solution)/shard_map/ppermute | solution.py:58
  85.4 40.5 %collective-permute-start = (bf16[128,896]{1,0:T(8,128)(2,1)S(1)}, bf16[128,896]{1,0:T(8,128)(2,1)}, u32[]{:S(2)}, u32[]{:S(2)}) collective-permute-start(bf16[128,896]{1,0:T(8,128)(2,1)S(1)} %get-tuple-element.94), channel_id=1, source_target_pairs={{0,1},{1,0},{2,3},{3,2},{4,5},{5,4},{6,7},{7,6},{8,9},{9,8},{10,11... | collective-permute-start | bytes 688136 | tf_op jit(solution)/shard_map/ppermute | solution.py:58
  87.5 16.2 %collective-permute-start.6 = (bf16[1,224,512]{2,1,0:T(8,128)(2,1)}, bf16[1,224,512]{2,1,0:T(8,128)(2,1)}, u32[]{:S(2)}, u32[]{:S(2)}) collective-permute-start(bf16[1,224,512]{2,1,0:T(8,128)(2,1)} %get-tuple-element.107), channel_id=1, source_target_pairs={{0,2},{1,3},{2,0},{3,1},{4,6},{5,7},{6,4},{7,5},{8,10},{9,11},{10,... | collective-permute-start | bytes 688136 | tf_op jit(solution)/shard_map/ppermute | solution.py:58
  102.6 13.4 %collective-permute-start.11 = (bf16[1,224,512]{2,1,0:T(8,128)(2,1)S(1)}, bf16[1,224,512]{2,1,0:T(8,128)(2,1)S(1)}, u32[]{:S(2)}, u32[]{:S(2)}) collective-permute-start(bf16[1,224,512]{2,1,0:T(8,128)(2,1)S(1)} %copy-done.41), channel_id=1, source_target_pairs={{0,2},{1,3},{2,0},{3,1},{4,6},{5,7},{6,4},{7,5},{8,10},{9,11},{10,... | collective-permute-start | bytes 688136 | tf_op jit(solution)/shard_map/ppermute | solution.py:58
  103.7 22.0 %collective-permute-start.13 = (bf16[1,224,512]{2,1,0:T(8,128)(2,1)}, bf16[1,224,512]{2,1,0:T(8,128)(2,1)S(1)}, u32[]{:S(2)}, u32[]{:S(2)}) collective-permute-start(bf16[1,224,512]{2,1,0:T(8,128)(2,1)} %get-tuple-element.103), channel_id=1, source_target_pairs={{0,2},{1,3},{2,0},{3,1},{4,6},{5,7},{6,4},{7,5},{8,10},{9,11},{10,... | collective-permute-start | bytes 688136 | tf_op jit(solution)/shard_map/ppermute | solution.py:58
  116.0 18.3 %collective-permute-start.2 = (bf16[128,896]{1,0:T(8,128)(2,1)S(1)}, bf16[128,896]{1,0:T(8,128)(2,1)S(1)}, u32[]{:S(2)}, u32[]{:S(2)}) collective-permute-start(bf16[128,896]{1,0:T(8,128)(2,1)S(1)} %fusion.20), channel_id=1, source_target_pairs={{0,2},{1,3},{2,0},{3,1},{4,6},{5,7},{6,4},{7,5},{8,10},{9,11},{10,... | collective-permute-start | bytes 688136 | tf_op jit(solution)/shard_map/ppermute | solution.py:58
  117.2 17.1 %copy-start.1 = (bf16[1,128,896]{2,1,0:T(8,128)(2,1)S(1)}, bf16[1,128,896]{2,1,0:T(8,128)(2,1)}, u32[]{:S(2)}) copy-start(bf16[1,128,896]{2,1,0:T(8,128)(2,1)} %param.21) | copy-start | bytes 688132
  125.8 10.2 %collective-permute-start.12 = (bf16[2,224,256]{2,1,0:T(8,128)(2,1)S(1)}, bf16[2,224,256]{2,1,0:T(8,128)(2,1)S(1)}, u32[]{:S(2)}, u32[]{:S(2)}) collective-permute-start(bf16[2,224,256]{2,1,0:T(8,128)(2,1)S(1)} %get-tuple-element.97), channel_id=1, source_target_pairs={{0,1},{1,0},{2,3},{3,2},{4,5},{5,4},{6,7},{7,6},{8,9},{9,8},{10,11... | collective-permute-start | bytes 688136 | tf_op jit(solution)/shard_map/ppermute | solution.py:58
  125.9 10.7 %collective-permute-start.14 = (bf16[2,224,256]{2,1,0:T(8,128)(2,1)S(1)}, bf16[2,224,256]{2,1,0:T(8,128)(2,1)S(1)}, u32[]{:S(2)}, u32[]{:S(2)}) collective-permute-start(bf16[2,224,256]{2,1,0:T(8,128)(2,1)S(1)} %get-tuple-element.101), channel_id=1, source_target_pairs={{0,1},{1,0},{2,3},{3,2},{4,5},{5,4},{6,7},{7,6},{8,9},{9,8},{10,11... | collective-permute-start | bytes 688136 | tf_op jit(solution)/shard_map/ppermute | solution.py:58
  135.7 42.8 %copy-start.9 = (f32[128,896]{1,0:T(8,128)}, f32[128,896]{1,0:T(8,128)S(1)}, u32[]{:S(2)}) copy-start(f32[128,896]{1,0:T(8,128)S(1)} %get-tuple-element.78.hidden_one_ref) | copy-start | bytes 1376260
  135.7 16.1 %collective-permute-start.10 = (bf16[512,896]{1,0:T(8,128)(2,1)}, bf16[512,896]{1,0:T(8,128)(2,1)S(1)}, u32[]{:S(2)}, u32[]{:S(2)}) collective-permute-start(bf16[512,896]{1,0:T(8,128)(2,1)} %collective-permute-done.9), channel_id=1, source_target_pairs={{0,1},{1,0},{2,3},{3,2},{4,5},{5,4},{6,7},{7,6},{8,9},{9,8},{10,11... | collective-permute-start | bytes 2752520 | tf_op jit(solution)/shard_map/ppermute | solution.py:58
  135.9 13.3 %collective-permute-start.4 = (bf16[128,896]{1,0:T(8,128)(2,1)S(1)}, bf16[128,896]{1,0:T(8,128)(2,1)S(1)}, u32[]{:S(2)}, u32[]{:S(2)}) collective-permute-start(bf16[128,896]{1,0:T(8,128)(2,1)S(1)} %multiply_convert_fusion.1), channel_id=1, source_target_pairs={{0,2},{1,3},{2,0},{3,1},{4,6},{5,7},{6,4},{7,5},{8,10},{9,11},{10,... | collective-permute-start | bytes 688136 | tf_op jit(solution)/shard_map/ppermute | solution.py:58
  136.0 13.2 %collective-permute-start.7 = (bf16[2,224,256]{2,1,0:T(8,128)(2,1)S(1)}, bf16[2,224,256]{2,1,0:T(8,128)(2,1)S(1)}, u32[]{:S(2)}, u32[]{:S(2)}) collective-permute-start(bf16[2,224,256]{2,1,0:T(8,128)(2,1)S(1)} %get-tuple-element.105), channel_id=1, source_target_pairs={{0,1},{1,0},{2,3},{3,2},{4,5},{5,4},{6,7},{7,6},{8,9},{9,8},{10,11... | collective-permute-start | bytes 688136 | tf_op jit(solution)/shard_map/ppermute | solution.py:58
  136.6 12.8 %collective-permute-start.3 = (bf16[128,896]{1,0:T(8,128)(2,1)S(1)}, bf16[128,896]{1,0:T(8,128)(2,1)S(1)}, u32[]{:S(2)}, u32[]{:S(2)}) collective-permute-start(bf16[128,896]{1,0:T(8,128)(2,1)S(1)} %multiply_convert_fusion.1), channel_id=1, source_target_pairs={{0,1},{1,0},{2,3},{3,2},{4,5},{5,4},{6,7},{7,6},{8,9},{9,8},{10,11... | collective-permute-start | bytes 688136 | tf_op jit(solution)/shard_map/ppermute | solution.py:58
  149.1 1.5 collective-permute-start.5
  149.2 22.4 %collective-permute-start.21 = (bf16[1,224,1792]{2,1,0:T(8,128)(2,1)}, bf16[1,224,1792]{2,1,0:T(8,128)(2,1)}, u32[]{:S(2)}, u32[]{:S(2)}) collective-permute-start(bf16[1,224,1792]{2,1,0:T(8,128)(2,1)} %get-tuple-element.86), channel_id=1, source_target_pairs={{0,2},{1,3},{2,0},{3,1},{4,6},{5,7},{6,4},{7,5},{8,10},{9,11},{10,... | collective-permute-start | bytes 2408456 | tf_op jit(solution)/shard_map/ppermute | solution.py:58
  168.1 1.6 collective-permute-start.16
  168.4 6.7 %collective-permute-start.15 = (bf16[128,896]{1,0:T(8,128)(2,1)S(1)}, bf16[128,896]{1,0:T(8,128)(2,1)S(1)}, u32[]{:S(2)}, u32[]{:S(2)}) collective-permute-start(bf16[128,896]{1,0:T(8,128)(2,1)S(1)} %get-tuple-element.92), channel_id=1, source_target_pairs={{0,1},{1,0},{2,3},{3,2},{4,5},{5,4},{6,7},{7,6},{8,9},{9,8},{10,11... | collective-permute-start | bytes 688136 | tf_op jit(solution)/shard_map/ppermute | solution.py:58
  170.7 7.7 %collective-permute-start.17 = (bf16[128,896]{1,0:T(8,128)(2,1)S(1)}, bf16[128,896]{1,0:T(8,128)(2,1)S(1)}, u32[]{:S(2)}, u32[]{:S(2)}) collective-permute-start(bf16[128,896]{1,0:T(8,128)(2,1)S(1)} %fusion.17), channel_id=1, source_target_pairs={{0,2},{1,3},{2,0},{3,1},{4,6},{5,7},{6,4},{7,5},{8,10},{9,11},{10,... | collective-permute-start | bytes 688136 | tf_op jit(solution)/shard_map/ppermute | solution.py:58
  175.1 11.6 %collective-permute-start.22 = (bf16[2,224,896]{2,1,0:T(8,128)(2,1)}, bf16[2,224,896]{2,1,0:T(8,128)(2,1)}, u32[]{:S(2)}, u32[]{:S(2)}) collective-permute-start(bf16[2,224,896]{2,1,0:T(8,128)(2,1)} %get-tuple-element.84), channel_id=1, source_target_pairs={{0,1},{1,0},{2,3},{3,2},{4,5},{5,4},{6,7},{7,6},{8,9},{9,8},{10,11... | collective-permute-start | bytes 2408456 | tf_op jit(solution)/shard_map/ppermute | solution.py:58
  179.7 26.1 %copy-start.7 = (f32[128,896]{1,0:T(8,128)}, f32[128,896]{1,0:T(8,128)S(1)}, u32[]{:S(2)}) copy-start(f32[128,896]{1,0:T(8,128)S(1)} %get-tuple-element.76.hidden_two_ref) | copy-start | bytes 1376260
  179.8 6.9 %collective-permute-start.19 = (bf16[128,896]{1,0:T(8,128)(2,1)S(1)}, bf16[128,896]{1,0:T(8,128)(2,1)S(1)}, u32[]{:S(2)}, u32[]{:S(2)}) collective-permute-start(bf16[128,896]{1,0:T(8,128)(2,1)S(1)} %multiply_convert_fusion), channel_id=1, source_target_pairs={{0,2},{1,3},{2,0},{3,1},{4,6},{5,7},{6,4},{7,5},{8,10},{9,11},{10,... | collective-permute-start | bytes 688136 | tf_op jit(solution)/shard_map/ppermute | solution.py:58
  183.3 5.6 %collective-permute-start.18 = (bf16[128,896]{1,0:T(8,128)(2,1)S(1)}, bf16[128,896]{1,0:T(8,128)(2,1)S(1)}, u32[]{:S(2)}, u32[]{:S(2)}) collective-permute-start(bf16[128,896]{1,0:T(8,128)(2,1)S(1)} %multiply_convert_fusion), channel_id=1, source_target_pairs={{0,1},{1,0},{2,3},{3,2},{4,5},{5,4},{6,7},{7,6},{8,9},{9,8},{10,11... | collective-permute-start | bytes 688136 | tf_op jit(solution)/shard_map/ppermute | solution.py:58
  186.7 2.3 collective-permute-start.20
  192.9 2.6 collective-permute-start.24
  195.4 10.3 %collective-permute-start.23 = (bf16[128,896]{1,0:T(8,128)(2,1)S(1)}, bf16[128,896]{1,0:T(8,128)(2,1)S(1)}, u32[]{:S(2)}, u32[]{:S(2)}) collective-permute-start(bf16[128,896]{1,0:T(8,128)(2,1)S(1)} %get-tuple-element.90), channel_id=1, source_target_pairs={{0,1},{1,0},{2,3},{3,2},{4,5},{5,4},{6,7},{7,6},{8,9},{9,8},{10,11... | collective-permute-start | bytes 688136 | tf_op jit(solution)/shard_map/ppermute | solution.py:58
  195.6 10.2 %collective-permute-start.25 = (bf16[128,896]{1,0:T(8,128)(2,1)S(1)}, bf16[128,896]{1,0:T(8,128)(2,1)S(1)}, u32[]{:S(2)}, u32[]{:S(2)}) collective-permute-start(bf16[128,896]{1,0:T(8,128)(2,1)S(1)} %fusion.14), channel_id=1, source_target_pairs={{0,2},{1,3},{2,0},{3,1},{4,6},{5,7},{6,4},{7,5},{8,10},{9,11},{10,... | collective-permute-start | bytes 688136 | tf_op jit(solution)/shard_map/ppermute | solution.py:58
  206.6 89.9 %copy-start.14 = (f32[128,896]{1,0:T(8,128)}, f32[128,896]{1,0:T(8,128)S(1)}, u32[]{:S(2)}) copy-start(f32[128,896]{1,0:T(8,128)S(1)} %get-tuple-element.74) | copy-start | bytes 1376260
  (39 other events, 109.7 us)
Sparse Core Ops, SparseCore 0:
  98.2 58.6 all-gather.1

commit v4 on v3

--- a/solution.py
+++ b/solution.py
@@ -1,4 +1,5 @@
 import functools
+import types
 
 import jax
 import jax.numpy as jnp
@@ -212,12 +213,10 @@
     return raised * (1.0 / total)
 
 
-def attend_forward_kernel(seq_len, block, order_ref, qkv_ref, rel_ref, bias_ref, out_ref, qkv, out):
-    copy_blocks(order_ref, qkv_ref, qkv, block, True)
+def attend_tiles(qkv, rel_ref, content_bias, position_bias, out):
+    seq_len = qkv.shape[0]
     keys = qkv.at[:, 128:256]
     values = qkv.at[:, 256:384]
-    content_bias = bias_ref[0:1, :]
-    position_bias = bias_ref[1:2, :]
     for tile in range(seq_len // TILE):
         start = tile * TILE
         query = qkv[start : start + TILE, 0:128].astype(f32)
@@ -226,7 +225,6 @@
         shares = attention_shares(content, position, keys, rel_ref, start, seq_len)
         got = dot_nn(shares.astype(bf16), values[0 : start + TILE, :])
         out[start : start + TILE, :] = join_heads(got).astype(bf16)
-    copy_blocks(order_ref, out, out_ref, block, False)
 
 
 def attend_backward_kernel(
@@ -252,8 +250,8 @@
     copy_blocks(order_ref, grad_ref, grad, block, True)
     keys = qkv.at[:, 128:256]
     values = qkv.at[:, 256:384]
-    content_bias = bias_ref[0:1, :]
-    position_bias = bias_ref[1:2, :]
+    content_bias = bias_ref[3:4, :]
+    position_bias = bias_ref[4:5, :]
     dkey[...] = jnp.zeros_like(dkey)
     dvalue[...] = jnp.zeros_like(dvalue)
     drel[...] = jnp.zeros_like(drel)
@@ -308,22 +306,6 @@
 in_smem = pl.BlockSpec(memory_space=pltpu.SMEM)
 
 
-def attend_forward(order, qkv, rel, bias, block):
-    rows = qkv.shape[0]
-    return pl.pallas_call(
-        functools.partial(attend_forward_kernel, rows, block),
-        out_shape=jax.ShapeDtypeStruct((rows, 128), bf16),
-        in_specs=[in_smem, in_vmem, in_vmem, in_vmem],
-        out_specs=in_vmem,
-        scratch_shapes=[pltpu.VMEM((rows, 384), bf16), pltpu.VMEM((rows, 128), bf16)],
-        compiler_params=pltpu.CompilerParams(vmem_limit_bytes=40 * 2**20),
-        cost_estimate=pl.CostEstimate(
-            flops=4 * 256 * rows * rows * 2, bytes_accessed=rows * 1300, transcendentals=rows * rows
-        ),
-        name="attend_forward",
-    )(order, qkv, rel, bias)
-
-
 def attend_backward(order, qkv, rel, bias, grad, block):
     rows = qkv.shape[0]
     return pl.pallas_call(
@@ -459,335 +441,6 @@
     return values[0]
 
 
-def gather_kernel(
-    parts,
-    block_ref,
-    small_ref,
-    *refs,
-):
-    part_refs = refs[:parts]
-    out_ref, total_ref = refs[parts : parts + 2]
-    part_outs = refs[parts + 2 : 2 * parts + 2]
-    near, far, y_send, y_recv, r_send, r_recv, l_send, l_recv, s_send, s_recv, p_send, p_recv, o_sem = refs[
-        2 * parts + 2 :
-    ]
-    c = lax.axis_index("ctx")
-    w = lax.axis_index("wa")
-    z = c // 2
-    right = z < 3
-    left = z > 0
-    barrier = pltpu.get_barrier_semaphore()
-    for j in range(1, 8):
-        signal_to(barrier, c ^ j, w)
-    for j in range(1, 4):
-        signal_to(barrier, c, w ^ j)
-    pl.semaphore_wait(barrier, 10)
-
-    def small_copy(source, j):
-        wide = j < 4
-        return pltpu.make_async_remote_copy(
-            src_ref=source,
-            dst_ref=near.at[j] if wide else far.at[j - 3],
-            send_sem=s_send.at[j],
-            recv_sem=s_recv.at[j],
-            device_id=(c, w ^ j) if wide else (c ^ (j - 3), w),
-            device_id_type=mesh_id,
-        )
-
-    for j in range(1, 4):
-        small_copy(small_ref, j).start()
-
-    def part_copy(m, j):
-        return pltpu.make_async_remote_copy(
-            src_ref=part_refs[m],
-            dst_ref=part_outs[m].at[w],
-            send_sem=p_send.at[m, j],
-            recv_sem=p_recv.at[m, j],
-            device_id=(c, w ^ j),
-            device_id_type=mesh_id,
-        )
-
-    for m in reversed(range(parts)):
-        for j in (1, 2, 3):
-            part_copy(m, j).start()
-
-    def y_copy(source, block, slot):
-        return pltpu.make_async_remote_copy(
-            src_ref=source,
-            dst_ref=out_ref.at[block],
-            send_sem=y_send.at[slot],
-            recv_sem=y_recv.at[slot],
-            device_id=(c ^ 1, w),
-            device_id_type=mesh_id,
-        )
-
-    def z_copy(source, block, slot, step, send, recv):
-        return pltpu.make_async_remote_copy(
-            src_ref=source,
-            dst_ref=out_ref.at[block],
-            send_sem=send.at[slot],
-            recv_sem=recv.at[slot],
-            device_id=(c + step, w),
-            device_id_type=mesh_id,
-        )
-
-    @pl.when(right)
-    def _():
-        z_copy(block_ref, c, 0, 2, r_send, r_recv).start()
-
-    @pl.when(left)
-    def _():
-        z_copy(block_ref, c, 0, -2, l_send, l_recv).start()
-
-    y_copy(block_ref, c, 0).start()
-    own = [pltpu.make_async_copy(block_ref, out_ref.at[c], o_sem.at[0])]
-    for m in range(parts):
-        own.append(pltpu.make_async_copy(part_refs[m], part_outs[m].at[w], o_sem.at[1 + m]))
-    for copy in own:
-        copy.start()
-    for j in range(1, 4):
-        small_copy(small_ref, j).wait()
-    total_ref[...] = tree_sum([small_ref[...]] + [near[j] for j in range(1, 4)])
-    for j in range(4, 11):
-        small_copy(total_ref, j).start()
-    for t in range(3):
-
-        @pl.when(z > t)
-        def _(t=t):
-            block = c - 2 * (t + 1)
-            z_copy(out_ref.at[block], block, t, 2, r_send, r_recv).wait_recv()
-            if t < 2:
-
-                @pl.when(right)
-                def _():
-                    z_copy(out_ref.at[block], block, t + 1, 2, r_send, r_recv).start()
-
-            y_copy(out_ref.at[block], block, t + 1).start()
-
-        @pl.when(z < 3 - t)
-        def _(t=t):
-            block = c + 2 * (t + 1)
-            z_copy(out_ref.at[block], block, t, -2, l_send, l_recv).wait_recv()
-            if t < 2:
-
-                @pl.when(left)
-                def _():
-                    z_copy(out_ref.at[block], block, t + 1, -2, l_send, l_recv).start()
-
-            y_copy(out_ref.at[block], block, t + 4).start()
-
-    for j in range(4, 11):
-        small_copy(total_ref, j).wait()
-    total_ref[...] = tree_sum([total_ref[...]] + [far[j] for j in range(1, 8)])
-    y_copy(block_ref, c ^ 1, 0).wait()
-    for t in range(3):
-
-        @pl.when(z > t)
-        def _(t=t):
-            block = (c ^ 1) - 2 * (t + 1)
-            y_copy(out_ref.at[block], block, t + 1).wait()
-
-        @pl.when(z < 3 - t)
-        def _(t=t):
-            block = (c ^ 1) + 2 * (t + 1)
-            y_copy(out_ref.at[block], block, t + 4).wait()
-
-    @pl.when(right)
-    def _():
-        z_copy(block_ref, c, 0, 2, r_send, r_recv).wait_send()
-
-    @pl.when(left)
-    def _():
-        z_copy(block_ref, c, 0, -2, l_send, l_recv).wait_send()
-
-    for t in range(2):
-
-        @pl.when(jnp.logical_and(z > t, right))
-        def _(t=t):
-            z_copy(block_ref, c, t + 1, 2, r_send, r_recv).wait_send()
-
-        @pl.when(jnp.logical_and(z < 3 - t, left))
-        def _(t=t):
-            z_copy(block_ref, c, t + 1, -2, l_send, l_recv).wait_send()
-
-    for m in range(parts):
-        for j in range(1, 4):
-            part_copy(m, j).wait_send()
-            pltpu.make_async_remote_copy(
-                src_ref=part_refs[m],
-                dst_ref=part_outs[m].at[w ^ j],
-                send_sem=p_send.at[m, j],
-                recv_sem=p_recv.at[m, j],
-                device_id=(c, w ^ j),
-                device_id_type=mesh_id,
-            ).wait_recv()
-    for copy in own:
-        copy.wait()
-
-
-def gather_all(block, small, parts, collective_id):
-    dma = pltpu.SemaphoreType.DMA
-    count = len(parts)
-    got = pl.pallas_call(
-        functools.partial(gather_kernel, count),
-        out_shape=[
-            jax.ShapeDtypeStruct((8,) + block.shape, block.dtype),
-            jax.ShapeDtypeStruct(small.shape, small.dtype),
-        ]
-        + [jax.ShapeDtypeStruct((4,) + part.shape, part.dtype) for part in parts],
-        in_specs=[in_vmem] * (2 + count),
-        out_specs=[in_vmem] * (2 + count),
-        scratch_shapes=[
-            pltpu.VMEM((4,) + small.shape, small.dtype),
-            pltpu.VMEM((8,) + small.shape, small.dtype),
-            dma((7,)),
-            dma((7,)),
-            dma((3,)),
-            dma((3,)),
-            dma((3,)),
-            dma((3,)),
-            dma((11,)),
-            dma((11,)),
-            dma((max(count, 1), 4)),
-            dma((max(count, 1), 4)),
-            dma((1 + count,)),
-        ],
-        compiler_params=pltpu.CompilerParams(
-            collective_id=collective_id, has_side_effects=True, vmem_limit_bytes=40 * 2**20
-        ),
-        name="gather_all",
-    )(block, small, *parts)
-    return got[0], got[1], got[2:]
-
-
-def swap_heads_kernel(outward, in_ref, out_ref, send_sem, recv_sem):
-    c = lax.axis_index("ctx")
-    w = lax.axis_index("wa")
-    owner = c // 2
-    half = c % 2
-    own = owner == w
-    other = jnp.logical_not(own)
-    barrier = pltpu.get_barrier_semaphore()
-
-    def lanes(start):
-        return pl.ds(pl.multiple_of(start * 128, 128), 128)
-
-    for j in range(1, 8):
-        signal_to(barrier, c ^ j, owner)
-    for r in range(4):
-        for h in range(2):
-            mine = jnp.logical_and(2 * w + h == c, r == 0)
-
-            @pl.when(jnp.logical_not(mine))
-            def _(r=r, h=h):
-                signal_to(barrier, 2 * w + h, w ^ r)
-
-    @pl.when(other)
-    def _():
-        signal_to(barrier, c, owner)
-
-    pl.semaphore_wait(barrier, 16 - 2 * own.astype(jnp.int32))
-    slot = w ^ owner
-    if outward:
-
-        def copy_to(j):
-            return pltpu.make_async_remote_copy(
-                src_ref=in_ref.at[c ^ j],
-                dst_ref=out_ref.at[slot, :, lanes(half)],
-                send_sem=send_sem.at[j],
-                recv_sem=recv_sem.at[slot * 2 + half],
-                device_id=(c ^ j, owner),
-                device_id_type=mesh_id,
-            )
-
-        for j in range(7, 0, -1):
-            copy_to(j).start()
-
-        @pl.when(other)
-        def _():
-            copy_to(0).start()
-
-        @pl.when(own)
-        def _():
-            pltpu.make_async_copy(
-                in_ref.at[c], out_ref.at[slot, :, lanes(half)], recv_sem.at[slot * 2 + half]
-            ).start()
-
-        for r in range(4):
-            for h in range(2):
-                pltpu.make_async_remote_copy(
-                    src_ref=in_ref.at[0],
-                    dst_ref=out_ref.at[r, :, h * 128 : (h + 1) * 128],
-                    send_sem=send_sem.at[0],
-                    recv_sem=recv_sem.at[r * 2 + h],
-                    device_id=(c ^ 1, w),
-                    device_id_type=mesh_id,
-                ).wait_recv()
-        for j in range(1, 8):
-            copy_to(j).wait_send()
-
-        @pl.when(other)
-        def _():
-            copy_to(0).wait_send()
-
-    else:
-
-        def copy_to(r, h):
-            return pltpu.make_async_remote_copy(
-                src_ref=in_ref.at[r, :, h * 128 : (h + 1) * 128],
-                dst_ref=out_ref.at[c],
-                send_sem=send_sem.at[r * 2 + h],
-                recv_sem=recv_sem.at[c],
-                device_id=(2 * w + h, w ^ r),
-                device_id_type=mesh_id,
-            )
-
-        for r in (3, 2, 1, 0):
-            for h in range(2):
-                mine = jnp.logical_and(2 * w + h == c, r == 0)
-
-                @pl.when(jnp.logical_not(mine))
-                def _(r=r, h=h):
-                    copy_to(r, h).start()
-
-                @pl.when(mine)
-                def _(r=r, h=h):
-                    pltpu.make_async_copy(
-                        in_ref.at[r, :, h * 128 : (h + 1) * 128], out_ref.at[c], recv_sem.at[c]
-                    ).start()
-
-        for block in range(8):
-            pltpu.make_async_remote_copy(
-                src_ref=in_ref.at[0, :, 0:128],
-                dst_ref=out_ref.at[block],
-                send_sem=send_sem.at[0],
-                recv_sem=recv_sem.at[block],
-                device_id=(c ^ 1, w),
-                device_id_type=mesh_id,
-            ).wait_recv()
-        for r in range(4):
-            for h in range(2):
-                mine = jnp.logical_and(2 * w + h == c, r == 0)
-
-                @pl.when(jnp.logical_not(mine))
-                def _(r=r, h=h):
-                    copy_to(r, h).wait_send()
-
-
-def swap_heads(value, outward, collective_id):
-    rows = value.shape[1]
-    shape = (4, rows, 256) if outward else (8, rows, 128)
-    return pl.pallas_call(
-        functools.partial(swap_heads_kernel, outward),
-        out_shape=jax.ShapeDtypeStruct(shape, value.dtype),
-        in_specs=[in_vmem],
-        out_specs=in_vmem,
-        scratch_shapes=[pltpu.SemaphoreType.DMA((8,)), pltpu.SemaphoreType.DMA((8,))],
-        compiler_params=pltpu.CompilerParams(collective_id=collective_id, has_side_effects=True),
-        name="swap_heads",
-    )(value)
-
-
 def gelu_slope(value):
     inner = 0.7978845608028654 * (value + 0.044715 * value * value * value)
     turned = jnp.tanh(inner)
@@ -1027,224 +680,573 @@
         target[share // 2, share % 2] = grads[share * count : (share + 1) * count].astype(bf16)
 
 
-def middle_back_kernel(
-    out_grad_ref,
-    down_ref,
-    pre_act_ref,
-    activated_ref,
-    normed_c_ref,
-    hidden_two_ref,
-    hidden_one_ref,
-    gains_ref,
-    up_any,
-    cross_out_any,
-    crossed_any,
-    cross_q_any,
-    cross_pair_any,
-    cross_query_any,
-    near_any,
-    normed_b_any,
-    output_any,
-    attended_any,
-    one_grad_ref,
-    gain_grad_ref,
-    heads_ref,
-    pair_grad_ref,
-    down_share,
-    up_share,
-    cross_half,
-    cross_out_x,
-    output_x,
-    up_ref,
-    cross_out_ref,
-    crossed_ref,
-    cross_q_ref,
-    cross_pair_ref,
-    cross_query_ref,
-    near_ref,
-    normed_b_ref,
-    output_ref,
-    attended_ref,
-    rows_ref,
-    rows_two_ref,
-    rows_one_ref,
-    pre_grad_ref,
-    query_grad_ref,
-    heads_out,
-    give_ref,
-    take_ref,
-    give_two_ref,
-    take_two_ref,
-    keep_ref,
-    down_x,
-    down_half,
-    down_part,
-    up_x,
-    up_half,
-    up_part,
-    cross_x,
-    load_sem,
-    g_send,
-    g_recv,
-    s_send,
-    s_recv,
-    h_send,
-    h_recv,
-    down_send,
-    down_recv,
-    up_send,
-    up_recv,
-    cross_send,
-    cross_recv,
-):
+class Cut:
+
+    def __init__(self, ref, start):
+        self.ref, self.start = ref, start
+
+    @property
+    def at(self):
+        return self
+
+    def __getitem__(self, k):
+        return self.ref.at[self.start + k]
+
+
+class Pool:
+    def __init__(self, ref):
+        self.ref, self.used = ref, 0
+
+    def take(self, count):
+        cut = Cut(self.ref, self.used)
+        self.used += count
+        return cut
+
+
+class LineGather:
+
+    def __init__(self, out, send, recv):
+        self.out, self.send, self.recv = out, send, recv
+        self.c, self.w = places_here()
+        self.z = self.c // 2
+        self.right, self.left = self.z < 3, self.z > 0
+
+    def y_copy(self, block, slot):
+        ref = self.out.at[block]
+        return remote(ref, ref, self.send.at[slot], self.recv.at[slot], self.c ^ 1, self.w)
+
+    def z_copy(self, block, slot, step):
+        k = slot + (7 if step > 0 else 10)
+        ref = self.out.at[block]
+        return remote(ref, ref, self.send.at[k], self.recv.at[k], self.c + step, self.w)
+
+    def start(self):
+        @pl.when(self.right)
+        def _():
+            self.z_copy(self.c, 0, 2).start()
+
+        @pl.when(self.left)
+        def _():
+            self.z_copy(self.c, 0, -2).start()
+
+        self.y_copy(self.c, 0).start()
+
+    def step(self, t):
+        @pl.when(self.z > t)
+        def _():
+            block = self.c - 2 * (t + 1)
+            self.z_copy(block, t, 2).wait_recv()
+            if t < 2:
+
+                @pl.when(self.right)
+                def _():
+                    self.z_copy(block, t + 1, 2).start()
+
+            self.y_copy(block, t + 1).start()
+
+        @pl.when(self.z < 3 - t)
+        def _():
+            block = self.c + 2 * (t + 1)
+            self.z_copy(block, t, -2).wait_recv()
+            if t < 2:
+
+                @pl.when(self.left)
+                def _():
+                    self.z_copy(block, t + 1, -2).start()
+
+            self.y_copy(block, t + 4).start()
+
+    def finish(self):
+        self.y_copy(self.c, 0).wait_send()
+        self.y_copy(self.c ^ 1, 0).wait_recv()
+        for t in range(3):
+            for step, at, near in ((-2, t + 1, self.z > t), (2, t + 4, self.z < 3 - t)):
+
+                @pl.when(near)
+                def _(step=step, at=at):
+                    self.y_copy(self.c + step * (t + 1), at).wait_send()
+                    self.y_copy((self.c ^ 1) + step * (t + 1), at).wait_recv()
+
+        @pl.when(self.right)
+        def _():
+            self.z_copy(self.c, 0, 2).wait_send()
+
+        @pl.when(self.left)
+        def _():
+            self.z_copy(self.c, 0, -2).wait_send()
+
+        for t in range(2):
+
+            @pl.when(jnp.logical_and(self.z > t, self.right))
+            def _():
+                self.z_copy(self.c, t + 1, 2).wait_send()
+
+            @pl.when(jnp.logical_and(self.z < 3 - t, self.left))
+            def _():
+                self.z_copy(self.c, t + 1, -2).wait_send()
+
+
+class Columns:
+
+    def __init__(self, source, target, width, first, send, recv, at=None):
+        self.source, self.target, self.width, self.first = source, target, width, first
+        self.send, self.recv, self.column = send, recv, at
+        self.c, self.w = places_here()
+
+    def taken(self, place):
+        start = place * self.width if self.column is None else self.column
+        return self.source.at[:, pl.ds(pl.multiple_of(start, 128), self.width)]
+
+    def put(self, place):
+        rows = self.source.shape[0]
+        return self.target.at[
+            pl.ds(pl.multiple_of(place * rows, 32), rows), self.first : self.first + self.width
+        ]
+
+    def copy(self, j, place):
+        return remote(
+            self.taken(self.w ^ j),
+            self.put(place),
+            self.send.at[j],
+            self.recv.at[j],
+            self.c,
+            self.w ^ j,
+        )
+
+    def own(self):
+        return pltpu.make_async_copy(self.taken(self.w), self.put(self.w), self.send.at[0])
+
+    def start(self):
+        for j in (2, 3, 1):
+            self.copy(j, self.w).start()
+        self.own().start()
+
+    def finish(self):
+        self.own().wait()
+        for j in (1, 2, 3):
+            self.copy(j, self.w).wait_send()
+            self.copy(j, self.w ^ j).wait_recv()
+
+
+class SmallSum:
+
+    def __init__(self, ref, got, axis, send, recv):
+        self.ref, self.got, self.axis, self.send, self.recv = ref, got, axis, send, recv
+        self.c, self.w = places_here()
+
+    def copy(self, k):
+        j = k + 1
+        ctx, wa = (self.c ^ j, self.w) if self.axis == "ctx" else (self.c, self.w ^ j)
+        return remote(self.ref, self.got.at[k], self.send.at[k], self.recv.at[k], ctx, wa)
+
+    def start(self):
+        for k in range(self.got.shape[0]):
+            self.copy(k).start()
+
+    def finish(self):
+        count = self.got.shape[0]
+        for k in range(count):
+            self.copy(k).wait()
+        self.ref[...] = tree_sum([self.ref[...]] + [self.got[k] for k in range(count)])
+
+
+class SwapHeads:
+
+    def __init__(self, by_heads, by_rows, outward, send, recv):
+        self.heads, self.rows, self.outward = by_heads, by_rows, outward
+        self.send, self.recv = send, recv
+        self.c, self.w = places_here()
+        self.owner, self.half = self.c // 2, self.c % 2
+        self.own = self.owner == self.w
+        self.other = jnp.logical_not(self.own)
+
+    def lanes(self):
+        return pl.ds(pl.multiple_of(self.half * 128, 128), 128)
+
+    def out_copy(self, j):
+        slot = self.w ^ self.owner
+        return remote(
+            self.heads.at[self.c ^ j],
+            self.rows.at[slot, :, self.lanes()],
+            self.send.at[j],
+            self.recv.at[slot * 2 + self.half],
+            self.c ^ j,
+            self.owner,
+        )
+
+    def start_out(self):
+        for j in range(7, 0, -1):
+            self.out_copy(j).start()
+
+        @pl.when(self.other)
+        def _():
+            self.out_copy(0).start()
+
+        @pl.when(self.own)
+        def _():
+            slot = self.w ^ self.owner
+            pltpu.make_async_copy(
+                self.heads.at[self.c],
+                self.rows.at[slot, :, self.lanes()],
+                self.recv.at[slot * 2 + self.half],
+            ).start()
+
+    def wait_rows(self, r):
+        for h in range(2):
+            remote(
+                self.heads.at[0],
+                self.rows.at[r, :, h * 128 : (h + 1) * 128],
+                self.send.at[0],
+                self.recv.at[r * 2 + h],
+                self.c ^ 1,
+                self.w,
+            ).wait_recv()
+
+    def finish_out(self):
+        for j in range(1, 8):
+            self.out_copy(j).wait_send()
+
+        @pl.when(self.other)
+        def _():
+            self.out_copy(0).wait_send()
+
+    def in_copy(self, r, h):
+        return remote(
+            self.rows.at[r, :, h * 128 : (h + 1) * 128],
+            self.heads.at[self.c],
+            self.send.at[r * 2 + h],
+            self.recv.at[self.c],
+            2 * self.w + h,
+            self.w ^ r,
+        )
+
+    def mine(self, r, h):
+        return jnp.logical_and(2 * self.w + h == self.c, r == 0)
+
+    def start_in(self, r):
+        for h in range(2):
+
+            @pl.when(jnp.logical_not(self.mine(r, h)))
+            def _():
+                self.in_copy(r, h).start()
+
+            @pl.when(self.mine(r, h))
+            def _():
+                pltpu.make_async_copy(
+                    self.rows.at[r, :, h * 128 : (h + 1) * 128],
+                    self.heads.at[self.c],
+                    self.recv.at[self.c],
+                ).start()
+
+    def finish_in(self):
+        for block in range(8):
+            remote(
+                self.rows.at[0, :, 0:128],
+                self.heads.at[block],
+                self.send.at[0],
+                self.recv.at[block],
+                self.c ^ 1,
+                self.w,
+            ).wait_recv()
+        for r in range(4):
+            for h in range(2):
+
+                @pl.when(jnp.logical_not(self.mine(r, h)))
+                def _(r=r, h=h):
+                    self.in_copy(r, h).wait_send()
+
+
+def layer_kernel(names, total_tokens, *refs):
+    v = types.SimpleNamespace(**dict(zip(names, refs, strict=True)))
     c, w = places_here()
-    tok = out_grad_ref.shape[0]
+    send, recv, local = Pool(v.send), Pool(v.recv), Pool(v.local)
+    tok, width = v.tokens.shape
+    seq_len = 8 * tok
+    rows = 4 * tok
+    cols = v.output_w.shape[0]
+    hidden = v.down_w.shape[0]
     scale = HEAD_DIM ** (-0.5)
-    sources = (
-        up_any,
-        cross_out_any,
-        crossed_any,
-        cross_q_any,
-        cross_pair_any,
-        cross_query_any,
-        near_any,
-        normed_b_any,
-        output_any,
-        attended_any,
-    )
-    targets = (
-        up_ref,
-        cross_out_ref,
-        crossed_ref,
-        cross_q_ref,
-        cross_pair_ref,
-        cross_query_ref,
-        near_ref,
-        normed_b_ref,
-        output_ref,
-        attended_ref,
-    )
-    loads = [
-        pltpu.make_async_copy(source, target, load_sem.at[k])
-        for k, (source, target) in enumerate(zip(sources, targets))
+
+    def load(source, target):
+        copy = pltpu.make_async_copy(source, target, local.take(1).at[0])
+        copy.start()
+        return copy
+
+    near_load = load(v.neighbours, v.near.at[0])
+    early = [load(v.waves_any, v.waves)]
+    late = [
+        load(v.output_any, v.output_w),
+        load(v.cross_out_any, v.cross_out_w),
+        load(v.down_any, v.down_w),
     ]
-    for load in loads:
-        load.start()
-    rows_ref[0] = out_grad_ref[...].astype(bf16)
+    v.small_all[...] = v.small[...]
+    v.tokens_all[c] = v.tokens[...]
     meet_all()
-    first = GatherRows(rows_ref, g_send.at[0], g_recv.at[0])
-    second = GatherRows(rows_two_ref, g_send.at[1], g_recv.at[1])
-    third = GatherRows(rows_one_ref, g_send.at[2], g_recv.at[2])
-    sum_c = SumRows(give_ref, take_ref, s_send.at[0], s_recv.at[0])
-    sum_b = SumRows(give_two_ref, take_two_ref, s_send.at[1], s_recv.at[1])
-    down = CtxSum(down_send, down_recv, down_x, down_half, down_part, down_share)
-    up = CtxSum(up_send, up_recv, up_x, up_half, up_part, up_share)
-    cross = CtxSum(cross_send, cross_recv, cross_x, cross_half)
+
+    near_sum = SmallSum(v.small_all, v.small_near, "wa", send.take(3), recv.take(3))
+    count_sum = SmallSum(v.count, v.count_far, "ctx", send.take(7), recv.take(7))
+    gather = LineGather(v.tokens_all, send.take(13), recv.take(13))
+    pair = [
+        Columns(weight, v.pair, 128, 128 * m, send.take(4), recv.take(4), c * 128)
+        for m, weight in enumerate((v.query_any, v.key_any, v.value_any, v.relative_any))
+    ]
+    cross = [
+        Columns(weight, target, cols, first, send.take(4), recv.take(4))
+        for weight, target, first in (
+            (v.cross_key_any, v.pair_cols, 0),
+            (v.cross_value_any, v.pair_cols, cols),
+            (v.cross_query_any, v.query_cols, 0),
+        )
+    ]
+    up_columns = Columns(v.up_any, v.up_cols, hidden, 0, send.take(4), recv.take(4))
+    near_send, near_recv = send.take(3), recv.take(3)
+    near_gather = GatherRows(v.near, near_send, near_recv)
+    gather.start()
+    near_sum.start()
+    for part in pair:
+        part.start()
+    gather.step(0)
+    near_sum.finish()
+    v.count[...] = jnp.broadcast_to(v.small_all[5:6, 0:128], v.count.shape)
+    count_sum.start()
+    gather.step(1)
+    for part in pair:
+        part.finish()
+    near_load.wait()
+    near_gather.start()
+    for part in cross:
+        part.start()
+    for copy in early:
+        copy.wait()
+    v.table[0:seq_len, :] = dot_nn(v.waves[...], v.pair[:, 384:512]).astype(bf16)
+    v.table[seq_len:, :] = jnp.zeros((TILE, 128), bf16)
+    v.biases[...] = v.small_all[:, pl.ds(pl.multiple_of(c * 128, 128), 128)]
+    v.gains[...] = v.small_all[:, 0:width]
+    gather.step(2)
+    gather.finish()
+    gain_one, gain_two, gain_three = (v.gains[k : k + 1, :] for k in range(3))
+
+    def project(part, carry):
+        start = pl.multiple_of(part * tok, tok)
+        value = v.tokens_all[part].astype(f32)
+        normed = (value * inverse_rms(value) * gain_one).astype(bf16)
+        v.normed_a[pl.ds(start, tok), :] = normed
+        v.qkv[pl.ds(start, tok), :] = dot_nn(normed, v.pair[:, 0:384]).astype(bf16)
+        return carry
+
+    lax.fori_loop(0, 8, project, 0)
+    column = lax.broadcasted_iota(jnp.int32, (TILE, seq_len), 1)
+
+    def move_rows(source, chosen, target):
+        def some(part, carry):
+            start = pl.multiple_of(part * TILE, TILE)
+            pick = jnp.where(chosen[pl.ds(start, TILE), :] == column, 1.0, 0.0).astype(bf16)
+            target[pl.ds(start, TILE), :] = dot_nn(pick, source[...]).astype(bf16)
+            return carry
+
+        lax.fori_loop(0, seq_len // TILE, some, 0)
+
+    move_rows(v.qkv, v.inverse, v.qkv_order)
+    near_gather.near()
+    near_gather.relay()
+    attend_tiles(v.qkv_order, v.table, v.biases[3:4, :], v.biases[4:5, :], v.heads_order)
+    move_rows(v.heads_order, v.order, v.heads_stored)
+    for part in range(8):
+        v.heads[part] = v.heads_stored[part * tok : (part + 1) * tok, :]
+    out_swap = SwapHeads(v.heads, v.attended, True, send.take(8), recv.take(8))
+    out_swap.start_out()
+    for copy in late:
+        copy.wait()
+
+    gathers = [GatherRows(ref, send.take(3), recv.take(3)) for ref in (v.rows_b, v.rows_c)]
+    sums = [SumRows(v.give.at[k], v.take.at[k], send.take(3), recv.take(3)) for k in range(3)]
+
+    def output_part(r):
+        return dot_nn(v.attended[r], v.output_w[...])
+
+    out_swap.wait_rows(3)
+    sums[0].give_far(output_part(3))
+    out_swap.wait_rows(1)
+    sums[0].give_near(output_part(1))
+    out_swap.wait_rows(2)
+    sums[0].pass_on(output_part(2))
+    out_swap.wait_rows(0)
+    v.hidden_one[...] = v.tokens[...].astype(f32) + sums[0].total(output_part(0))
+    value = v.hidden_one[...]
+    v.rows_b[0] = (value * inverse_rms(value) * gain_two).astype(bf16)
+
+    gathers[0].start()
+    out_swap.finish_out()
+    near_gather.far()
+    for part in cross:
+        part.finish()
+    up_columns.start()
+    near_count = v.near.shape[1]
+
+    def near_project(r, carry):
+        start = pl.multiple_of(r * near_count, near_count)
+        v.cross_pair[pl.ds(start, near_count), :] = dot_nn(v.near[r], v.pair_cols[...]).astype(bf16)
+        return carry
+
+    lax.fori_loop(0, 4, near_project, 0)
+
+    def cross_part(r):
+        v.cross_q[r * tok : (r + 1) * tok, :] = dot_nn(v.rows_b[r], v.query_cols[...]).astype(bf16)
+
+        def group(g, carry):
+            at = pl.multiple_of(r * tok + g * GROUP, GROUP)
+            near = pl.multiple_of((r * (tok // GROUP) + g) * NK, NK)
+            query = stack_all(v.cross_q[pl.ds(at, GROUP), :])
+            shares = cross_shares(query, v.cross_pair[pl.ds(near, NK), 0:cols])
+            out = dot_nn(shares.astype(bf16), v.cross_pair[pl.ds(near, NK), cols:])
+            v.crossed[pl.ds(at, GROUP), :] = join_all(out).astype(bf16)
+            return carry
+
+        lax.fori_loop(0, tok // GROUP, group, 0)
+        return dot_nn(v.crossed[r * tok : (r + 1) * tok, :], v.cross_out_w[...])
+
+    def in_turn(gathered, summed, part, between=None):
+        v.keep[0] = part(0)
+        gathered.near()
+        summed.give_near(part(1))
+        gathered.relay()
+        v.keep[2] = part(2)
+        gathered.far()
+        summed.give_far(part(3))
+        summed.pass_on(v.keep[2])
+        if between is not None:
+            between()
+        return summed.total(v.keep[0])
+
+    v.hidden_two[...] = v.hidden_one[...] + in_turn(gathers[0], sums[1], cross_part)
+    value = v.hidden_two[...]
+    v.rows_c[0] = (value * inverse_rms(value) * gain_three).astype(bf16)
+
+    gathers[1].start()
+    up_columns.finish()
+
+    def feed_part(r):
+        part = pl.ds(r * tok, tok)
+        v.pre_act[part, :] = dot_nn(v.rows_c[r], v.up_cols[...])
+        v.activated[part, :] = gelu_tanh(v.pre_act[part, :]).astype(bf16)
+        return dot_nn(v.activated[part, :], v.down_w[...])
+
+    layer_out = v.hidden_two[...] + in_turn(gathers[1], sums[2], feed_part)
+    v.layer_out[...] = layer_out
+
+    count_sum.finish()
+    error = layer_out - v.teacher[...].astype(f32)
+    valid = v.valid[...]
+    weighted = valid * error
+    v.error[...] = jnp.broadcast_to(jnp.sum(weighted * error, keepdims=True), v.error.shape)
+    v.out_grad[...] = (total_tokens / v.count[0:1, 0:1]) * weighted
+
+    middle_back(v, send, recv)
+
+
+def middle_back(v, send, recv):
+    c, w = places_here()
+    tok, width = v.tokens.shape
+    rows = 4 * tok
+    cols = v.output_w.shape[0]
+    scale = HEAD_DIM ** (-0.5)
+    first, second, third = (
+        GatherRows(ref, send.take(3), recv.take(3)) for ref in (v.rows_o, v.rows_two, v.rows_one)
+    )
+    sum_c, sum_b = (
+        SumRows(v.give.at[k], v.take.at[k], send.take(3), recv.take(3)) for k in (3, 4)
+    )
+    down = CtxSum(send.take(12), recv.take(12), v.down_x, v.down_half, v.down_part, v.down_share)
+    up = CtxSum(send.take(12), recv.take(12), v.up_x, v.up_half, v.up_part, v.up_share)
+    cross = CtxSum(send.take(12), recv.take(12), v.cross_x, v.cross_half)
+    heads = SwapHeads(v.heads_grad, v.heads_out, False, send.take(8), recv.take(8))
+    v.rows_o[0] = v.out_grad[...].astype(bf16)
 
     first.start()
 
     def feed_back(r):
         part = pl.ds(r * tok, tok)
-        act_grad = dot_nt(rows_ref[r], down_ref[...])
-        pre_grad_ref[part, :] = (act_grad * gelu_slope(pre_act_ref[part, :])).astype(bf16)
-        return dot_nt(pre_grad_ref[part, :], up_ref[...])
-
-    loads[0].wait()
-    keep_ref[0] = feed_back(0)
+        act_grad = dot_nt(v.rows_o[r], v.down_w[...])
+        v.pre_grad[part, :] = (act_grad * gelu_slope(v.pre_act[part, :])).astype(bf16)
+        return dot_nt(v.pre_grad[part, :], v.up_cols[...])
+
+    v.keep[0] = feed_back(0)
     first.near()
     sum_c.give_near(feed_back(1))
     first.relay()
-    keep_ref[1] = feed_back(2)
+    v.keep[1] = feed_back(2)
     first.far()
     sum_c.give_far(feed_back(3))
-    sum_c.pass_on(keep_ref[1])
-    put_rows(down_x, dot_tn(activated_ref[...], rows_ref[...].reshape(4 * tok, -1)))
+    sum_c.pass_on(v.keep[1])
+    put_rows(v.down_x, dot_tn(v.activated[...], v.rows_o[...].reshape(rows, width)))
     down.start_y()
-    put_shares(up_x, dot_tn(normed_c_ref[...], pre_grad_ref[...]))
-    for load in loads[1:]:
-        load.wait()
-    normed_grad = sum_c.total(keep_ref[0])
-    hidden = hidden_two_ref[...]
-    inverse = inverse_rms(hidden)
-    two_grad = out_grad_ref[...] + norm_pull(hidden, inverse, gains_ref[2:3, :], normed_grad)
-    gain_three = jnp.sum(normed_grad * hidden * inverse, axis=0, keepdims=True)
-    keep_ref[1] = two_grad
-    rows_two_ref[0] = two_grad.astype(bf16)
+    put_shares(v.up_x, dot_tn(v.rows_c[...].reshape(rows, width), v.pre_grad[...]))
+    normed_grad = sum_c.total(v.keep[0])
+    value = v.hidden_two[...]
+    inverse = inverse_rms(value)
+    two_grad = v.out_grad[...] + norm_pull(value, inverse, v.gains[2:3, :], normed_grad)
+    gain_three = jnp.sum(normed_grad * value * inverse, axis=0, keepdims=True)
+    v.keep[1] = two_grad
+    v.rows_two[0] = two_grad.astype(bf16)
 
     second.start()
-    width = cross_q_ref.shape[1]
 
     def cross_back(r):
-        part = pl.ds(r * tok, tok)
-        crossed_grad = dot_nt(rows_two_ref[r], cross_out_ref[...]).astype(bf16)
-        for g in range(tok // GROUP):
-            at = r * tok + g * GROUP
-            near = (r * (tok // GROUP) + g) * NK
-            query = stack_all(cross_q_ref[at : at + GROUP, :])
-            grad = stack_all(crossed_grad[g * GROUP : (g + 1) * GROUP])
-            keys = cross_pair_ref[near : near + NK, 0:width]
+        part = slice(r * tok, (r + 1) * tok)
+        v.crossed_grad[...] = dot_nt(v.rows_two[r], v.cross_out_w[...]).astype(bf16)
+
+        def group(g, carry):
+            within = pl.multiple_of(g * GROUP, GROUP)
+            at = pl.multiple_of(r * tok + g * GROUP, GROUP)
+            near = pl.ds(pl.multiple_of((r * (tok // GROUP) + g) * NK, NK), NK)
+            query = stack_all(v.cross_q[pl.ds(at, GROUP), :])
+            grad = stack_all(v.crossed_grad[pl.ds(within, GROUP), :])
+            keys = v.cross_pair[near, 0:cols]
             shares = cross_shares(query, keys)
-            share_grad = dot_nt(grad, cross_pair_ref[near : near + NK, width:])
+            share_grad = dot_nt(grad, v.cross_pair[near, cols:])
             delta = jnp.sum(shares * share_grad, axis=1, keepdims=True)
             score_grad = (shares * (share_grad - delta)).astype(bf16)
             query_grad = join_all(dot_nn(score_grad, keys)) * scale
-            query_grad_ref[at : at + GROUP, :] = query_grad.astype(bf16)
-            pair_grad_ref[near : near + NK, 0:width] = (dot_tn(score_grad, query) * scale).astype(bf16)
-            pair_grad_ref[near : near + NK, width:] = dot_tn(shares.astype(bf16), grad).astype(bf16)
-        return dot_nt(query_grad_ref[part, :], cross_query_ref[...])
-
-    keep_ref[0] = cross_back(0)
+            v.query_grad[pl.ds(at, GROUP), :] = query_grad.astype(bf16)
+            v.pair_grad[near, 0:cols] = (dot_tn(score_grad, query) * scale).astype(bf16)
+            v.pair_grad[near, cols:] = dot_tn(shares.astype(bf16), grad).astype(bf16)
+            return carry
+
+        lax.fori_loop(0, tok // GROUP, group, 0)
+        return dot_nt(v.query_grad[part, :], v.query_cols[...])
+
+    v.keep[0] = cross_back(0)
     second.near()
     sum_b.give_near(cross_back(1))
     second.relay()
-    keep_ref[2] = cross_back(2)
+    v.keep[2] = cross_back(2)
     second.far()
     sum_b.give_far(cross_back(3))
-    sum_b.pass_on(keep_ref[2])
+    sum_b.pass_on(v.keep[2])
     down.finish_y()
     down.start_z()
     up.start_y()
-    normed_b = normed_b_ref[...]
-    put_rows(cross_out_x, dot_tn(crossed_ref[...], rows_two_ref[...].reshape(4 * tok, -1)))
-    put_shares(cross_x, dot_tn(normed_b, query_grad_ref[...]), 0)
-    normed_grad = sum_b.total(keep_ref[0])
-    hidden = hidden_one_ref[...]
-    inverse = inverse_rms(hidden)
-    one_grad = keep_ref[1] + norm_pull(hidden, inverse, gains_ref[1:2, :], normed_grad)
-    gain_two = jnp.sum(normed_grad * hidden * inverse, axis=0, keepdims=True)
-    gain_grad_ref[...] = jnp.concatenate(
+    normed_b = v.rows_b[...].reshape(rows, width)
+    put_rows(v.cross_out_x, dot_tn(v.crossed[...], v.rows_two[...].reshape(rows, width)))
+    put_shares(v.cross_x, dot_tn(normed_b, v.query_grad[...]), 0)
+    normed_grad = sum_b.total(v.keep[0])
+    value = v.hidden_one[...]
+    inverse = inverse_rms(value)
+    one_grad = v.keep[1] + norm_pull(value, inverse, v.gains[1:2, :], normed_grad)
+    gain_two = jnp.sum(normed_grad * value * inverse, axis=0, keepdims=True)
+    v.gain_grad[...] = jnp.concatenate(
         [gain_two, gain_three, jnp.zeros((6, gain_two.shape[1]), f32)], axis=0
     )
-    one_grad_ref[...] = one_grad
-    rows_one_ref[0] = one_grad.astype(bf16)
+    v.one_grad[...] = one_grad
+    v.rows_one[0] = one_grad.astype(bf16)
 
     third.start()
-    put_shares(cross_x, dot_tn(near_ref[...], pair_grad_ref[...]), width)
-
-    def head_copy(r, h):
-        return remote(
-            heads_out.at[r, :, h * 128 : (h + 1) * 128],
-            heads_ref.at[c],
-            h_send.at[r * 2 + h],
-            h_recv.at[c],
-            2 * w + h,
-            w ^ r,
-        )
+    near = v.near[...].reshape(-1, width)
+    put_shares(v.cross_x, dot_tn(near, v.pair_grad[...]), cols)
 
     def head_back(r):
-        heads_out[r] = dot_nt(rows_one_ref[r], output_ref[...]).astype(bf16)
-        for h in range(2):
-            mine = jnp.logical_and(2 * w + h == c, r == 0)
-
-            @pl.when(jnp.logical_not(mine))
-            def _():
-                head_copy(r, h).start()
-
-            @pl.when(mine)
-            def _():
-                pltpu.make_async_copy(
-                    heads_out.at[r, :, h * 128 : (h + 1) * 128], heads_ref.at[c], h_recv.at[c]
-                ).start()
+        v.heads_out[r] = dot_nt(v.rows_one[r], v.output_w[...]).astype(bf16)
+        heads.start_in(r)
 
     head_back(0)
     third.near()
@@ -1256,98 +1258,111 @@
     up.finish_y()
     up.start_z()
     cross.start_y()
-    put_rows(output_x, dot_tn(attended_ref[...], rows_one_ref[...].reshape(4 * tok, -1)))
-    for block in range(8):
-        remote(
-            heads_out.at[0, :, 0:128], heads_ref.at[block], h_send.at[0], h_recv.at[block], c ^ 1, w
-        ).wait_recv()
-    for r in range(4):
-        for h in range(2):
-
-            @pl.when(jnp.logical_not(jnp.logical_and(2 * w + h == c, r == 0)))
-            def _(r=r, h=h):
-                head_copy(r, h).wait_send()
-
+    attended = jnp.concatenate([v.attended[r] for r in range(4)], axis=0)
+    put_rows(v.output_x, dot_tn(attended, v.rows_one[...].reshape(rows, width)))
+    heads.finish_in()
     down.finish_z()
     up.finish_z()
     cross.finish_y()
 
 
-def middle_back(
-    out_grad,
-    down_weight,
-    pre_act,
-    activated,
-    normed_c,
-    hidden_two,
-    hidden_one,
-    gains,
-    later,
-    collective_id,
-):
-    tok, width = out_grad.shape
-    hidden = down_weight.shape[0]
-    cols = later[3].shape[1]
-    near = later[6].shape[0]
+def layer(total_tokens, given, collective_id):
+    tok, width = given["tokens"].shape
+    hidden = given["down_any"].shape[0]
+    cols = given["output_any"].shape[0]
+    near = given["neighbours"].shape[0]
+    seq_len = 8 * tok
+    rows = 4 * tok
+    padded = -(-(width // 32) // 8) * 8
     any_space = pl.BlockSpec(memory_space=pl.ANY)
-    dma = pltpu.SemaphoreType.DMA
     shape = jax.ShapeDtypeStruct
     vmem = pltpu.VMEM
-    rows = -(-(width // 32) // 8) * 8
-    return pl.pallas_call(
-        middle_back_kernel,
-        out_shape=[
-            shape((tok, width), f32),
-            shape((8, width), f32),
-            shape((8, tok, 128), bf16),
-            shape((near, 2 * cols), bf16),
-            shape((hidden // 8, width), bf16),
-            shape((4, rows, hidden), bf16),
-            shape((4, 4, rows, 3 * cols), bf16),
-            shape((4, 2, cols // 8, width), bf16),
-            shape((4, 2, cols // 8, width), bf16),
-        ],
-        in_specs=[in_vmem] * 8 + [any_space] * 10,
-        out_specs=[in_vmem] * 9,
-        scratch_shapes=[vmem(value.shape, value.dtype) for value in later]
-        + [
-            vmem((4, tok, width), bf16),
-            vmem((4, tok, width), bf16),
-            vmem((4, tok, width), bf16),
-            vmem((4 * tok, hidden), bf16),
-            vmem((4 * tok, cols), bf16),
-            vmem((4, tok, cols), bf16),
-            vmem((3, tok, width), bf16),
-            vmem((3, tok, width), bf16),
-            vmem((3, tok, width), bf16),
-            vmem((3, tok, width), bf16),
-            vmem((3, tok, width), f32),
-            vmem((4, 2, hidden // 8, width), bf16),
-            vmem((4, hidden // 8, width), bf16),
-            vmem((3, hidden // 8, width), bf16),
-            vmem((4, 2, 4, rows, hidden), bf16),
-            vmem((4, 4, rows, hidden), bf16),
-            vmem((3, 4, rows, hidden), bf16),
-            vmem((4, 2, 4, rows, 3 * cols), bf16),
-            dma((10,)),
-            dma((3, 3)),
-            dma((3, 3)),
-            dma((2, 3)),
-            dma((2, 3)),
-            dma((8,)),
-            dma((8,)),
-            dma((12,)),
-            dma((12,)),
-            dma((12,)),
-            dma((12,)),
-            dma((12,)),
-            dma((12,)),
-        ],
+    dma = pltpu.SemaphoreType.DMA
+    results = dict(
+        layer_out=shape((tok, width), f32),
+        error=shape((8, 128), f32),
+        count=shape((8, 128), f32),
+        qkv=shape((seq_len, 384), bf16),
+        table=shape((seq_len + TILE, 128), bf16),
+        biases=shape((8, 128), f32),
+        gains=shape((8, width), f32),
+        normed_a=shape((seq_len, width), bf16),
+        pair_cols=shape((width, 2 * cols), bf16),
+        one_grad=shape((tok, width), f32),
+        gain_grad=shape((8, width), f32),
+        heads_grad=shape((8, tok, 128), bf16),
+        pair_grad=shape((4 * near, 2 * cols), bf16),
+        down_share=shape((hidden // 8, width), bf16),
+        up_share=shape((4, padded, hidden), bf16),
+        cross_half=shape((4, 4, padded, 3 * cols), bf16),
+        cross_out_x=shape((4, 2, cols // 8, width), bf16),
+        output_x=shape((4, 2, cols // 8, width), bf16),
+    )
+    scratch = dict(
+        small_all=vmem(given["small"].shape, f32),
+        small_near=vmem((3,) + given["small"].shape, f32),
+        count_far=vmem((7, 8, 128), f32),
+        tokens_all=vmem((8, tok, width), bf16),
+        pair=vmem((width, 512), bf16),
+        waves=vmem((seq_len, width), bf16),
+        qkv_order=vmem((seq_len, 384), bf16),
+        heads_order=vmem((seq_len, 128), bf16),
+        heads_stored=vmem((seq_len, 128), bf16),
+        heads=vmem((8, tok, 128), bf16),
+        attended=vmem((4, tok, cols), bf16),
+        near=vmem((4, near, width), bf16),
+        query_cols=vmem((width, cols), bf16),
+        up_cols=vmem((width, hidden), bf16),
+        output_w=vmem((cols, width), bf16),
+        cross_out_w=vmem((cols, width), bf16),
+        down_w=vmem((hidden, width), bf16),
+        cross_pair=vmem((4 * near, 2 * cols), bf16),
+        cross_q=vmem((rows, cols), bf16),
+        crossed=vmem((rows, cols), bf16),
+        crossed_grad=vmem((tok, cols), bf16),
+        hidden_one=vmem((tok, width), f32),
+        hidden_two=vmem((tok, width), f32),
+        out_grad=vmem((tok, width), f32),
+        pre_act=vmem((rows, hidden), f32),
+        activated=vmem((rows, hidden), bf16),
+        rows_b=vmem((4, tok, width), bf16),
+        rows_c=vmem((4, tok, width), bf16),
+        rows_o=vmem((4, tok, width), bf16),
+        rows_two=vmem((4, tok, width), bf16),
+        rows_one=vmem((4, tok, width), bf16),
+        give=vmem((5, 3, tok, width), bf16),
+        take=vmem((5, 3, tok, width), bf16),
+        keep=vmem((3, tok, width), f32),
+        pre_grad=vmem((rows, hidden), bf16),
+        query_grad=vmem((rows, cols), bf16),
+        heads_out=vmem((4, tok, cols), bf16),
+        down_x=vmem((4, 2, hidden // 8, width), bf16),
+        down_half=vmem((4, hidden // 8, width), bf16),
+        down_part=vmem((3, hidden // 8, width), bf16),
+        up_x=vmem((4, 2, 4, padded, hidden), bf16),
+        up_half=vmem((4, 4, padded, hidden), bf16),
+        up_part=vmem((3, 4, padded, hidden), bf16),
+        cross_x=vmem((4, 2, 4, padded, 3 * cols), bf16),
+        send=dma((200,)),
+        recv=dma((200,)),
+        local=dma((8,)),
+    )
+    names = [*given, *results, *scratch]
+    specs = [
+        any_space if name.endswith("_any") or name == "neighbours" else in_vmem for name in given
+    ]
+    got = pl.pallas_call(
+        functools.partial(layer_kernel, names, total_tokens),
+        out_shape=list(results.values()),
+        in_specs=specs,
+        out_specs=[in_vmem] * len(results),
+        scratch_shapes=list(scratch.values()),
         compiler_params=pltpu.CompilerParams(
-            collective_id=collective_id, has_side_effects=True, vmem_limit_bytes=58 * 2**20
+            collective_id=collective_id, has_side_effects=True, vmem_limit_bytes=62 * 2**20
         ),
-        name="middle_back",
-    )(out_grad, down_weight, pre_act, activated, normed_c, hidden_two, hidden_one, gains, *later)
+        name="layer",
+    )(*given.values())
+    return types.SimpleNamespace(**dict(zip(results, got, strict=True)))
 
 
 def finish_kernel(
@@ -2096,125 +2111,77 @@
     block = tok_dev // 2
     attn = HEADS * HEAD_DIM
     cols = attn // places
-    rows = places * tok_dev
     share = width // places
 
     slots = jnp.arange(2 * ctx_count)
     inverse = jnp.sum(jnp.where(block_order[None, :] == slots[:, None], slots[None, :], 0), axis=1)
     inverse = inverse.astype(jnp.int32)
-    valid = valid_mask.astype(f32).reshape(tok_dev, 1)
-
-    pair_rows = jnp.concatenate(
-        [
-            lax.dynamic_slice_in_dim(weight, here * 128, 128, 1)
-            for weight in (query_weight, key_weight, value_weight, relative_weight)
-        ],
-        axis=1,
-    )
+    valid = valid_mask.astype(f32)
+
+    def rows_of(blocks):
+        return (blocks[:, None] * block + jnp.arange(block, dtype=jnp.int32)).reshape(seq_len, 1)
+
+
+    small = jnp.concatenate([jnp.zeros((5, attn), f32), jnp.broadcast_to(jnp.sum(valid), (3, attn))])
     gain_rows = jnp.stack([attention_gain, cross_gain, feedforward_gain]).astype(f32)
     bias_rows = jnp.stack([content_bias, position_bias]).astype(f32)
-    gain_rows = jnp.concatenate(
-        [jnp.pad(gain_rows, ((0, 0), (0, cols - share))), bias_rows, jnp.zeros((3, cols), f32)], axis=0
-    )
-    count_row = jnp.broadcast_to(jnp.sum(valid), (8, 128))
-    tokens_all, count_all, (pair_cols, gains) = gather_all(
-        tokens[0], count_row, (pair_rows, gain_rows), 1
-    )
-    count = count_all[0:1, 0:1]
-    pair_cols = pair_cols.reshape(width, 512)
-    bias_all = gains[:, 3:5].transpose(1, 0, 2).reshape(2, attn)
-    gains = gains[:, :3, :share].transpose(1, 0, 2).reshape(3, width)
-    gain_one, gain_two, gain_three = gains[0:1], gains[1:2], gains[2:3]
-    gains_eight = jnp.pad(gains, ((0, 5), (0, 0)))
-
-    cross_query_cols, cross_key_cols, cross_value_cols = [
-        take_columns(weight) for weight in (cross_query_weight, cross_key_weight, cross_value_weight)
-    ]
-    cross_pair_cols = jnp.concatenate([cross_key_cols, cross_value_cols], axis=1)
-    near_rows = jnp.concatenate(gather_parts(neighbours.reshape(-1, width)), axis=0)
-    up_cols = take_columns(up_weight)
+    small = lax.dynamic_update_slice(small, gain_rows, (0, place * share))
+    small = lax.dynamic_update_slice(small, bias_rows, (3, place * cols))
+
+    half = width // 2
+    freq = jnp.exp(-jnp.log(10000.0) * jnp.arange(half, dtype=f32) * 2.0 / width)
+    coarse = (64.0 * jnp.arange(seq_len // 64, dtype=f32)[::-1])[:, None] * freq
+    fine = jnp.arange(64, dtype=f32)[::-1][:, None] * freq
+    sin_a, cos_a = jnp.sin(coarse)[:, None], jnp.cos(coarse)[:, None]
+    sin_b, cos_b = jnp.sin(fine)[None], jnp.cos(fine)[None]
+    waves = jnp.concatenate(
+        [sin_a * cos_b + cos_a * sin_b, cos_a * cos_b - sin_a * sin_b], axis=-1
+    )
+    waves = waves.reshape(seq_len, width).astype(bf16)
+
+    done = layer(
+        float(places * seq_len),
+        dict(
+            inverse=rows_of(inverse),
+            order=rows_of(block_order),
+            tokens=tokens[0],
+            teacher=teacher[0],
+            valid=valid.reshape(tok_dev, 1),
+            small=small,
+            neighbours=neighbours.reshape(-1, width),
+            waves_any=waves,
+            query_any=query_weight,
+            key_any=key_weight,
+            value_any=value_weight,
+            relative_any=relative_weight,
+            cross_query_any=cross_query_weight,
+            cross_key_any=cross_key_weight,
+            cross_value_any=cross_value_weight,
+            up_any=up_weight,
+            output_any=output_weight,
+            cross_out_any=cross_output_weight,
+            down_any=down_weight,
+        ),
+        1,
+    )
     qkv_rows = jnp.stack(
         [weight.reshape(share, ctx_count, 128) for weight in (query_weight, key_weight, value_weight)],
         axis=2,
     ).reshape(share, 3 * attn)
     qkv_full = lax.all_gather(qkv_rows, "wa", axis=0, tiled=True)
-
-    distance = (seq_len - 1 - jnp.arange(seq_len)).astype(f32)
-    waves = sinusoid(distance, width).astype(bf16)
-
-    hidden_all = tokens_all.reshape(seq_len, width).astype(f32)
-    normed_a = (hidden_all * inverse_rms(hidden_all) * gain_one).astype(bf16)
-    qkv = dot_nn(normed_a, pair_cols[:, :384]).astype(bf16)
-    table = dot_nn(waves, pair_cols[:, 384:]).astype(bf16)
-    table = jnp.concatenate([table, jnp.zeros((TILE, 128), bf16)], axis=0)
-    my_biases = lax.dynamic_slice_in_dim(bias_all, here * 128, 128, 1)
-    my_biases = jnp.concatenate([my_biases, jnp.zeros((6, 128), f32)], axis=0)
-    out = attend_forward(inverse, qkv, table, my_biases, block)
-    attended = swap_heads(out.reshape(ctx_count, tok_dev, 128), True, 2).reshape(rows, cols)
-
-    def to_owner(product):
-        return scatter_parts([product[r * tok_dev : (r + 1) * tok_dev] for r in range(places)])
-
-    def from_all(value):
-        return jnp.concatenate(gather_parts(value), axis=0)
-
-    hidden_in = tokens[0].astype(f32)
-    hidden_one = hidden_in + to_owner(dot_nn(attended, output_weight))
-
-    scale_two = inverse_rms(hidden_one)
-    normed_b = from_all((hidden_one * scale_two * gain_two).astype(bf16))
-    cross_q = dot_nn(normed_b, cross_query_cols).astype(bf16)
-    cross_pair = dot_nn(near_rows, cross_pair_cols).astype(bf16)
-    crossed = cross_forward(cross_q, cross_pair)
-    hidden_two = hidden_one + to_owner(dot_nn(crossed, cross_output_weight))
-
-    scale_three = inverse_rms(hidden_two)
-    normed_c = from_all((hidden_two * scale_three * gain_three).astype(bf16))
-    pre_act = dot_nn(normed_c, up_cols)
-    activated = gelu_tanh(pre_act).astype(bf16)
-    layer_out = hidden_two + to_owner(dot_nn(activated, down_weight))
-
-    error = layer_out - teacher[0].astype(f32)
-    error_sum = jnp.sum(valid * error * error)
-    out_grad = (places * seq_len) / count * valid * error
-
-    one_grad, gain_part, heads_grad, cross_pair_grad, down_share, up_share, cross_x, cross_o_x, output_x = (
-        middle_back(
-            out_grad,
-            down_weight,
-            pre_act,
-            activated,
-            normed_c,
-            hidden_two,
-            hidden_one,
-            gains_eight,
-            (
-                up_cols,
-                cross_output_weight,
-                crossed,
-                cross_q,
-                cross_pair,
-                cross_query_cols,
-                near_rows,
-                normed_b,
-                output_weight,
-                attended,
-            ),
-            3,
-        )
-    )
     qkv_grad, table_grad, bias_part = attend_backward(
-        inverse, qkv, table, my_biases, heads_grad.reshape(seq_len, 128), block
+        inverse, done.qkv, done.table, done.biases, done.heads_grad.reshape(seq_len, 128), block
     )
 
     pair_slots = jnp.arange(ctx_count)[:, None, None]
     bias_slots = jnp.where(pair_slots == here, bias_part[None, 0:2], 0.0)
+    gain_part = done.gain_grad
     small = jnp.concatenate(
         [
             jnp.pad(gain_part[2:3], ((0, 0), (0, attn - width))),
             jnp.pad(gain_part[0:2], ((0, 0), (0, attn - width))),
             bias_slots.reshape(2, attn),
-            jnp.broadcast_to(error_sum, (3, attn)),
+            jnp.broadcast_to(done.error[0:1, 0:1], (3, attn)),
         ],
         axis=0,
     )
@@ -2230,30 +2197,28 @@
         pair_all,
     ) = finish(
         qkv_grad.reshape(ctx_count, tok_dev, 384),
-        normed_a,
+        done.normed_a,
         waves,
         table_grad,
         small,
-        cross_pair_grad,
-        cross_pair_cols,
-        down_share,
-        up_share,
-        cross_x,
-        cross_o_x,
-        output_x,
-        one_grad,
+        done.pair_grad,
+        done.pair_cols,
+        done.down_share,
+        done.up_share,
+        done.cross_half,
+        done.cross_out_x,
+        done.output_x,
+        done.one_grad,
         tokens[0],
-        gains_eight,
+        done.gains,
         qkv_full,
         4,
     )
     neighbours_grad = near_grad.reshape(neighbours.shape)
     gain_out = lax.dynamic_slice_in_dim(small[0:3], place * share, share, 1)
-    bias_out = lax.dynamic_slice_in_dim(
-        small[3:5].reshape(ctx_count, 2, 128), place * 2, 2, 0
-    )
+    bias_out = lax.dynamic_slice_in_dim(small[3:5].reshape(ctx_count, 2, 128), place * 2, 2, 0)
     bias_out = bias_out.transpose(1, 0, 2).reshape(2, cols)
-    loss = small[5, 0] / (2.0 * count[0, 0] * width)
+    loss = small[5, 0] / (2.0 * done.count[0, 0] * width)
     pair_all = pair_all.reshape(ctx_count, share, 512)
     whole = [
         pair_all[:, :, 128 * m : 128 * (m + 1)].transpose(1, 0, 2).reshape(share, attn).astype(f32)
@@ -2270,7 +2235,7 @@
     ]
 
     return (
-        layer_out[None],
+        done.layer_out[None],
         loss,
         tokens_grad[None],
         neighbours_grad,

time: 553 us -> 521 us (0.942)
  the two profiles are of different devices: /device:TPU:0 before, /device:TPU:18 now
where the time goes in v4:
time: 521 us; the launch traced here: 512 us
  Pallas kernels  443 us (85%)
  local copies, waits for them, and re-layouts  39.3 us (8%)
  between operations  17.2 us (3%)
  other arithmetic  12 us (2%)
    pallas_call x1, Pallas kernels, layer(): pl.pallas_call(functools.partial(layer_kernel, names, total_tokens), out_...  232 us
    pallas_call x1, Pallas kernels, finish(): pl.pallas_call(finish_kernel, out_shape=[shape((tok, width), f32), shape(...  198 us
    pallas_call x1, Pallas kernels, attend_backward(): pl.pallas_call(functools.partial(attend_backward_kernel, rows, block), ou...  13.1 us
    unnamed x52, local copies, waits for them, and re-layouts  11.6 us
  transfers between devices with their start and end apart: 1, of which 0 were waited for; matrix products, arithmetic and copies ran while one was open for 3% of the time, Pallas kernels for 48%

profile of v4, /device:TPU:18, one launch (start us, length us, event | category | flops | bytes accessed | tf_op | source)
XLA Modules:
  0.0 511.5 jit_solution(10554159791084696236)
XLA Ops:
  7.2 1.3 copy.71
  8.5 1.2 copy.72
  10.3 1.5 copy.66
  13.2 1.3 add.82.refs_0_
  14.5 1.3 add.83.refs_1_
  19.7 1.8 pad_maximum_fusion.refs_7_.waves_ref
  21.5 231.6 %layer.1 = (f32[128,896]{1,0:T(8,128)}, f32[8,128]{1,0:T(8,128)}, f32[8,128]{1,0:T(8,128)}, bf16[1024,384]{1,0:T(8,128)(2,1)}, bf16[1152,128]{1,0:T(8,128)(2,1)}...) custom-call(s32[1024,1]{1,0:T(8,128)} %add.82.refs_0_, ...), custom_call_target="tpu_custom_call" | custom-call | tf_op jit(solution)/shard_map/layer/pallas_call | solution.py:1354
  254.6 1.2 slice.74
  255.8 1.2 slice.72
  257.0 1.1 copy-done.2
  258.2 1.0 copy-done.3
  259.1 0.9 copy-done.4
  260.7 13.1 %attend_backward.1 = (bf16[1024,384]{1,0:T(8,128)(2,1)S(1)}, f32[1024,128]{1,0:T(8,128)S(1)}, f32[8,128]{1,0:T(8,128)S(1)}) custom-call(s32[16]{0:T(128)S(1)} %select_reduce_fusion.order_ref, bf16[1024,384]{1,0:T(8,128)(2,1)S(1)} %copy-done.2, bf16[1152,128]{1,0:T(8,128)(2,1)S(1)} %copy-done.3, f32[8,128]{1,0:T(8,128)S(1)} %copy-done.5, ...), custom_call_target="tpu_custom_call" | custom-call | flops 5368709120 | bytes 3072000 | tf_op jit(solution)/shard_map/attend_backward/pallas_call | solution.py:311
  273.8 0.9 copy-done
  274.7 0.8 copy-done.1
  277.7 198.1 %finish.1 = (f32[128,896]{1,0:T(8,128)}, f32[512,896]{1,0:T(8,128)}, f32[8,1024]{1,0:T(8,128)}, bf16[4,2,112,896]{3,2,1,0:T(8,128)(2,1)}, bf16[4,2,32,3584]{3,2,...) custom-call(bf16[8,128,384]{2,1,0:T(8,128)(2,1)} %bitcast.67, ...), custom_call_target="tpu_custom_call" | custom-call | tf_op jit(solution)/shard_map/finish/pallas_call | solution.py:1614
  475.8 1.2 slice.73
  477.0 0.8 slice.79
  477.8 0.8 slice.86
  479.1 3.3 reshape.303
  483.2 1.1 copy.80
  484.3 1.1 copy.79
  485.4 1.1 copy.78
  486.5 2.0 bitcast_convert_fusion
  488.5 2.2 slice_convert_fusion
  490.7 3.5 reshape.314
  495.4 1.4 bitcast_convert_fusion.1
  496.8 1.5 copy_bitcast_fusion
  498.3 1.5 copy_bitcast_fusion.2
  500.4 0.8 copy.90
  501.2 0.8 copy.91
  501.9 1.2 copy.92
  (90 shorter events, 11.9 us)
Async XLA Ops:
  7.2 2.6 copy-start.7
  7.2 270.5 %all-gather.2.cloned.1.call-start = ((), (), s32[]{:S(2)}) async-start(), calls=%async_computation | async-start | bytes 6881280 | tf_op jit(solution)/shard_map/all_gather | solution.py:2171
  10.3 1.9 copy-start.16
  10.3 1.8 copy-start.17
  10.3 1.9 copy-start.18
  10.3 1.9 copy-start.19
  10.3 1.9 copy-start.20
  10.3 1.9 copy-start.22
  10.3 2.6 copy-start.21
  18.2 3.3 copy-start.15
  257.0 1.1 copy-start.2
  258.1 1.0 copy-start.3
  259.1 0.9 copy-start.4
  260.1 0.7 copy-start.5
  273.8 0.9 copy-start
  274.7 0.8 copy-start.1
  484.3 2.2 copy-start.10
  486.5 2.0 copy-start.9
  490.7 3.5 copy-start.8
  494.2 1.1 copy-start.13
  494.2 1.2 copy-start.14
  498.3 2.1 copy-start.11
  498.3 2.9 copy-start.12
  499.7 2.2 copy-start.6
Sparse Core Ops, SparseCore 0:
  12.0 64.8 all-gather.1
